TPU v7x, 256 devices: a whole 4x4x8 slice. The times are simulated.
256 devices in a mesh: gx: 16 (over y_lo, z), gy: 8 (over y_hi, x), gz: 2 (over core).
Axes of the slice: x: 4, y: 4 (y_hi: 2, y_lo: 2; y = y_hi * 2 + y_lo), z: 8, core: 2. Of those that a mesh axis runs over, the one named last changes fastest.
Arguments:
- tokens: bfloat16 [128, 128, 128, 128], P('gx', 'gy', 'gz'), may hold values from -6 to 6
- w_qkv: bfloat16 [128, 384], replicated, may hold values from -0.5 to 0.5
- w_out: bfloat16 [128, 128], replicated, may hold values from -0.5 to 0.5
- w_gate_up: bfloat16 [128, 1024], replicated, may hold values from -0.5 to 0.5
- w_down: bfloat16 [512, 128], replicated, may hold values from -0.25 to 0.25
Outputs:
- updated: bfloat16 [128, 128, 128, 128], P('gx', 'gy', 'gz')
All inputs are finite; a program needn't handle non-finite values.
Results may differ from a plain program's by a relative error of at most 0.014.
Values may be sent and summed in bfloat16 or wider, within the bound.
No kernel may reach another device: no remote copies, remote signals or barrier semaphores. Data moves between devices by JAX's collectives and lax.ppermute only.
A program may use at most 64 MiB of HBM per device.

v0:
```python
import math

import jax
import jax.numpy as jnp
from jax import lax
from jax.sharding import PartitionSpec as P

HEADS = 8
FF = 512


EPS = 1e-05


def norm_rows(values):
    mean = jnp.mean(values, axis=-1, keepdims=True)
    centred = values - mean
    spread = jnp.mean(centred * centred, axis=-1, keepdims=True)
    return centred * lax.rsqrt(spread + EPS)


def unit_scale(values):
    return values * lax.rsqrt(jnp.mean(values * values) + 1e-06)


def make_kernel(pooled, length):
    width = pooled.shape[1] // 2
    head_dim = width // HEADS
    query = unit_scale(pooled[:, :width]).reshape(length, HEADS, head_dim)
    key_part = unit_scale(pooled[:, width:]).reshape(length, HEADS, head_dim)
    kernel = jnp.einsum("ahd,bhd->hab", query, key_part, precision=lax.Precision.HIGHEST)
    return (kernel / math.sqrt(head_dim * length)).astype(jnp.bfloat16)


def apply_first(kernel, block):
    split = block.reshape(block.shape[0], -1, HEADS, block.shape[-1] // HEADS)
    mixed = jnp.einsum("hab,bmhd->amhd", kernel, split, preferred_element_type=jnp.float32)
    return mixed.reshape((kernel.shape[1],) + block.shape[1:])


def apply_middle(kernel, block):
    split = block.reshape(block.shape[0], block.shape[1], -1, HEADS, block.shape[-1] // HEADS)
    mixed = jnp.einsum("hab,xbmhd->xamhd", kernel, split, preferred_element_type=jnp.float32)
    return mixed.reshape((block.shape[0], kernel.shape[1]) + block.shape[2:])


def apply_third(kernel, block):
    split = block.reshape(
        block.shape[0], block.shape[1], block.shape[2], HEADS, block.shape[-1] // HEADS
    )
    mixed = jnp.einsum("hab,xybhd->xyahd", kernel, split, preferred_element_type=jnp.float32)
    return mixed.reshape(block.shape[0], block.shape[1], kernel.shape[1], block.shape[-1])


def finish(mixed, slab, w_out, w_gate_up, w_down):
    width = slab.shape[-1]
    resid = slab.astype(jnp.float32).reshape(-1, width) + jnp.dot(
        mixed.reshape(-1, width), w_out, preferred_element_type=jnp.float32
    )
    inner = norm_rows(resid).astype(jnp.bfloat16)
    both = jnp.dot(inner, w_gate_up, preferred_element_type=jnp.float32)
    hidden = (jax.nn.gelu(both[:, :FF]) * both[:, FF:]).astype(jnp.bfloat16)
    result = resid + jnp.dot(hidden, w_down, preferred_element_type=jnp.float32)
    return result.astype(jnp.bfloat16).reshape(slab.shape)


def body(tokens, w_qkv, w_out, w_gate_up, w_down):
    rows_x, rows_y, rows_z, width = tokens.shape
    count_x = lax.axis_size("gx")
    count_y = lax.axis_size("gy")
    line_x = rows_x * count_x
    line_y = rows_y * count_y
    line_z = rows_z * lax.axis_size("gz")

    def project(slab):
        normed = norm_rows(slab.astype(jnp.float32)).astype(jnp.bfloat16)
        qkv = jnp.dot(normed.reshape(-1, width), w_qkv, preferred_element_type=jnp.float32)
        qkv = qkv.reshape(rows_y, rows_z, 3 * width)
        both = qkv[..., : 2 * width]
        return (
            qkv[..., 2 * width :].astype(jnp.bfloat16),
            jnp.sum(both, axis=(0, 1)),
            jnp.sum(both, axis=1),
            jnp.sum(both, axis=0),
        )

    value, part_x, part_y, part_z = lax.map(project, tokens)
    part_y = jnp.sum(part_y, axis=0)
    part_z = jnp.sum(part_z, axis=0)
    total_x = lax.psum(part_x, ("gy", "gz"))
    total_y = lax.psum(part_y, ("gx", "gz"))
    total_z = lax.psum(part_z, ("gx", "gy"))
    pooled_x = lax.all_gather(total_x, "gx", axis=0, tiled=True)
    pooled_y = lax.all_gather(total_y, "gy", axis=0, tiled=True)
    pooled_z = lax.all_gather(total_z.astype(jnp.bfloat16), "gz", axis=0, tiled=True).astype(
        total_z.dtype
    )
    kernel_x = make_kernel(pooled_x, line_x)
    kernel_y = make_kernel(pooled_y, line_y)
    kernel_z = make_kernel(pooled_z, line_z)
    applied = apply_first(
        kernel_x, lax.all_to_all(value, "gx", split_axis=1, concat_axis=0, tiled=True)
    ).astype(jnp.bfloat16)
    after_x = lax.all_to_all(applied, "gx", split_axis=0, concat_axis=1, tiled=True)
    applied = apply_middle(
        kernel_y, lax.all_to_all(after_x, "gy", split_axis=0, concat_axis=1, tiled=True)
    ).astype(jnp.bfloat16)
    after_y = lax.all_to_all(applied, "gy", split_axis=1, concat_axis=0, tiled=True)
    applied = apply_third(
        kernel_z, lax.all_to_all(after_y, "gz", split_axis=0, concat_axis=2, tiled=True)
    ).astype(jnp.bfloat16)
    mixed = lax.all_to_all(applied, "gz", split_axis=2, concat_axis=0, tiled=True)

    def closing(pair):
        block, slab = pair
        return finish(block, slab, w_out, w_gate_up, w_down)

    return lax.map(closing, (mixed, tokens))


def solution(mesh):
    in_specs = (P("gx", "gy", "gz", None), P(), P(), P(), P())
    out_specs = P("gx", "gy", "gz", None)
    return jax.shard_map(body, mesh=mesh, in_specs=in_specs, out_specs=out_specs, check_vma=False)
```

profile of v0, /device:TPU:1, one launch (start us, length us, event | category | flops | bytes accessed | tf_op | source)
XLA Modules:
  0.0 1132.5 jit_solution(17426018462102678975)
XLA Ops:
  0.0 40.3 %while.26 = (s32[]{:T(128)}, bf16[8,16,64,128]{3,2,0,1:T(8,128)(2,1)}, f32[8,256]{1,0:T(8,128)S(1)}, f32[8,16,256]{2,1,0:T(8,128)S(1)}, f32[8,64,256]{2,1,0:T(8,...) while((s32[]{:T(128)}, ...), condition=%wide.region_6.7_spmd, body=%wide.region_0.6_spmd.sunk | while | flops 102740736 | bytes 4317297 | solution.py:87
  2.5 1.5 fusion.76
  7.6 1.5 fusion.76
  12.6 1.5 fusion.76
  17.7 1.5 fusion.76
  22.7 1.5 fusion.76
  27.8 1.5 fusion.76
  32.8 1.5 fusion.76
  37.9 1.5 fusion.76
  40.4 10.1 all-to-all-start
  50.5 34.7 %psum.21 = f32[8,256]{1,0:T(8,128)S(1)} all-reduce(f32[8,256]{1,0:T(8,128)S(1)} %get-tuple-element.83), channel_id=1, replica_groups=mesh['gx'=16,'gy'=8,'gz'=2] {'gy','gz'}, use_global_device_ids=true, to_apply=%region_7.8 | all-reduce | flops 2048 | bytes 16384 | tf_op jit(solution)/shard_map/psum | solution.py:90
  85.2 32.1 %all_gather.9 = f32[128,256]{1,0:T(8,128)S(1)} all-gather(f32[8,256]{1,0:T(8,128)S(1)} %psum.21), channel_id=1, replica_groups=mesh['gx'=16,'gy'=8,'gz'=2] {'gx'}, dimensions={0}, use_global_device_ids=true | all-gather | bytes 139264 | tf_op jit(solution)/shard_map/all_gather | solution.py:93
  121.5 3.2 copy.31
  124.6 7.3 copy.34
  133.3 2.8 copy.36
  136.1 45.7 %all_to_all.87 = bf16[128,1,64,128]{3,2,1,0:T(8,128)(2,1)S(1)} all-to-all(bf16[128,1,64,128]{3,2,1,0:T(8,128)(2,1)} %copy.36), channel_id=1, replica_groups=mesh['gx'=16,'gy'=8,'gz'=2] {'gx'}, dimensions={0} | all-to-all | bytes 4194304 | tf_op jit(solution)/shard_map/all_to_all | solution.py:104
  181.8 1.5 copy.37
  183.3 5.8 all-to-all-start.2
  189.0 111.3 %psum.22 = f32[16,256]{1,0:T(8,128)S(1)} all-reduce(f32[16,256]{1,0:T(8,128)S(1)} %reduce_sum.137), channel_id=1, replica_groups=mesh['gx'=16,'gy'=8,'gz'=2] {'gx','gz'}, use_global_device_ids=true, to_apply=%region_11.12 | all-reduce | flops 4096 | bytes 32768 | tf_op jit(solution)/shard_map/psum | solution.py:91
  300.3 28.6 %all_gather.10 = f32[128,256]{1,0:T(8,128)S(1)} all-gather(f32[16,256]{1,0:T(8,128)S(1)} %psum.22), channel_id=1, replica_groups=mesh['gx'=16,'gy'=8,'gz'=2] {'gy'}, dimensions={0}, use_global_device_ids=true | all-gather | bytes 147456 | tf_op jit(solution)/shard_map/all_gather | solution.py:94
  333.0 3.2 copy.38
  336.2 7.3 copy.41
  344.8 2.9 copy.43
  347.7 6.3 all-to-all-start.3
  354.1 590.0 %psum.23 = bf16[64,256]{1,0:T(8,128)(2,1)S(1)} all-reduce(f32[64,256]{1,0:T(8,128)S(1)} %reduce_sum.140), channel_id=1, replica_groups=mesh['gx'=16,'gy'=8,'gz'=2] {'gx','gy'}, use_global_device_ids=true, to_apply=%region_15.16 | all-reduce | flops 16384 | bytes 98304 | tf_op jit(solution)/shard_map/psum | solution.py:92
  944.1 117.7 %all_gather.11 = bf16[128,256]{1,0:T(8,128)(2,1)S(1)} all-gather(bf16[64,256]{1,0:T(8,128)(2,1)S(1)} %psum.23), channel_id=1, replica_groups=mesh['gx'=16,'gy'=8,'gz'=2] {'gz'}, dimensions={0}, use_global_device_ids=true | all-gather | bytes 98304 | tf_op jit(solution)/shard_map/all_gather | solution.py:95
  1066.2 6.6 all_to_all.88
  1072.8 7.3 copy.44
  1080.1 6.8 reshape.130
  1088.2 3.0 copy.48
  1091.3 6.6 all_to_all.89
  1099.3 33.2 %while.27 = (s32[]{:T(128)}, bf16[8,16,64,128]{3,2,1,0:T(8,128)(2,1)}, bf16[8,16,64,128]{3,2,1,0:T(8,128)(2,1)}, bf16[8,16,64,128]{3,2,1,0:T(8,128)(2,1)S(1)}, b...) while((s32[]{:T(128)}, ...), condition=%wide.region_21.22_spmd, body=%wide.region_18.21_spmd.sunk | while | flops 442893312 | bytes 13308505 | solution.py:118
  (182 shorter events, 74.7 us)
Async XLA Ops:
  40.4 81.1 %all-to-all-start = ((bf16[8,16,64,128]{3,2,0,1:T(8,128)(2,1)}), bf16[8,16,64,128]{3,2,0,1:T(8,128)(2,1)S(1)}, u32[]{:S(2)}, u32[]{:S(2)}) async-start(bf16[8,16,64,128]{3,2,0,1:T(8,128)(2,1)} %get-tuple-element.82), calls=%async_computation | async-start | bytes 4194304 | tf_op jit(solution)/shard_map/all_to_all | solution.py:102
  183.3 149.7 %all-to-all-start.2 = ((bf16[8,16,64,128]{3,2,1,0:T(8,128)(2,1)}), bf16[8,16,64,128]{3,2,1,0:T(8,128)(2,1)S(1)}, u32[]{:S(2)}, u32[]{:S(2)}) async-start(bf16[8,16,64,128]{3,2,1,0:T(8,128)(2,1)} %copy.37), calls=%async_computation.2 | async-start | bytes 4194304 | tf_op jit(solution)/shard_map/all_to_all | solution.py:106
  347.7 717.1 %all-to-all-start.3 = ((bf16[1,128,64,128]{3,2,0,1:T(8,128)(2,1)}), bf16[1,128,64,128]{3,2,0,1:T(8,128)(2,1)S(1)}, u32[]{:S(2)}, u32[]{:S(2)}) async-start(bf16[1,128,64,128]{3,2,0,1:T(8,128)(2,1)} %copy.43), calls=%async_computation.3 | async-start | bytes 4194304 | tf_op jit(solution)/shard_map/all_to_all | solution.py:108
  1064.9 1.4 copy-start
  1097.9 1.4 copy-start.1
  1097.9 1.4 copy-start.2
  1097.9 1.4 copy-start.3
where the time goes:
time: 1140 us; the launch traced here: 1130 us
  blocking collectives  973 us (85%)
  local copies, waits for them, and re-layouts  70.5 us (6%)
  matrix products  33.2 us (3%)
  other arithmetic  28.1 us (2%)
  starting transfers between devices  22.2 us (2%)
    psum x1, blocking collectives, body(): total_z = lax.psum(part_z, ('gx', 'gy'))  590 us
    all_gather x1, blocking collectives, body(): lax.all_gather(total_z.astype(jnp.bfloat16), 'gz', axis=0, tiled=True)  118 us
    psum x1, blocking collectives, body(): total_y = lax.psum(part_y, ('gx', 'gz'))  111 us
    all_to_all x1, blocking collectives, body(): lax.all_to_all(applied, 'gx', split_axis=0, concat_axis=1, tiled=True)  45.7 us
    psum x1, blocking collectives, body(): total_x = lax.psum(part_x, ('gy', 'gz'))  34.7 us
    all_gather x1, blocking collectives, body(): pooled_x = lax.all_gather(total_x, 'gx', axis=0, tiled=True)  32.1 us
    all_gather x1, blocking collectives, body(): pooled_y = lax.all_gather(total_y, 'gy', axis=0, tiled=True)  28.6 us
  transfers between devices with their start and end apart: 3, of which 0 were waited for; matrix products, arithmetic and copies ran while one was open for 1% of the time, Pallas kernels for 0%

commit v1 on v0

v1 whole, which is shorter than its diff:
```python
import functools
import math

import jax
import jax.numpy as jnp
from jax import lax
from jax.experimental import pallas as pl
from jax.experimental.pallas import tpu as pltpu
from jax.sharding import PartitionSpec as P

HEADS = 8
HD = 16
C = 128
FF = 512
EPS = 1e-05

BF = jnp.bfloat16
F32 = jnp.float32
NT = (((1,), (1,)), ((), ()))


def dot(a, b, dims=(((1,), (0,)), ((), ()))):
    return lax.dot_general(a, b, dims, preferred_element_type=F32)


def norm_rows(values):
    mean = jnp.mean(values, axis=-1, keepdims=True)
    centred = values - mean
    spread = jnp.mean(centred * centred, axis=-1, keepdims=True)
    return centred * lax.rsqrt(spread + EPS)


def halves(values):
    high = values.astype(BF)
    low = (values - high.astype(F32)).astype(BF)
    return jnp.concatenate([high, low], axis=1)


def twice(values):
    return jnp.concatenate([values, values], axis=0)


def iota2(shape, dim):
    return lax.broadcasted_iota(jnp.int32, shape, dim)


def ones_where(cond):
    return jnp.where(cond, 1.0, 0.0).astype(BF)


def first_kernel(tok_ref, wv_ref, vt_ref, pool_ref, sx_ref, sy_acc, sz_acc):
    step = pl.program_id(0)
    _, ny, nz, _ = tok_ref.shape
    x = tok_ref[0].reshape(ny * nz, C).astype(F32)
    normed = norm_rows(x).astype(BF)
    vt = dot(wv_ref[...].T, normed, NT).astype(BF)
    vt_ref[...] = vt.reshape(HEADS, 1, HD, ny * nz)
    n32 = normed.astype(F32).reshape(ny, nz, C)
    sy = jnp.sum(n32, axis=1)
    sz = jnp.sum(n32, axis=0)

    @pl.when(step == 0)
    def _():
        sy_acc[...] = jnp.zeros_like(sy_acc)
        sz_acc[...] = jnp.zeros_like(sz_acc)

    sy_acc[...] += sy
    sz_acc[...] += sz
    sx_ref[pl.ds(step, 1), :] = jnp.sum(sy, axis=0, keepdims=True)

    @pl.when(step == pl.num_programs(0) - 1)
    def _():
        parts = pool_ref.shape[0]
        ry = ny // parts
        rz = nz // parts
        pool_ref[...] = jnp.zeros_like(pool_ref)
        pool_ref[:, 0:ry, :] = sy_acc[...].reshape(parts, ry, C)
        pool_ref[:, ry : ry + rz, :] = sz_acc[...].reshape(parts, rz, C)


def first(tokens, wv, parts):
    nx, ny, nz, _ = tokens.shape
    rows = -(-(ny // parts + nz // parts) // 8) * 8
    return pl.pallas_call(
        first_kernel,
        grid=(nx,),
        in_specs=[
            pl.BlockSpec((1, ny, nz, C), lambda i: (i, 0, 0, 0)),
            pl.BlockSpec((C, C), lambda i: (0, 0)),
        ],
        out_specs=[
            pl.BlockSpec((HEADS, 1, HD, ny * nz), lambda i: (0, i, 0, 0)),
            pl.BlockSpec((parts, rows, C), lambda i: (0, 0, 0)),
            pl.BlockSpec((nx, C), lambda i: (0, 0)),
        ],
        out_shape=[
            jax.ShapeDtypeStruct((HEADS, nx, HD, ny * nz), BF),
            jax.ShapeDtypeStruct((parts, rows, C), F32),
            jax.ShapeDtypeStruct((nx, C), F32),
        ],
        scratch_shapes=[pltpu.VMEM((ny, C), F32), pltpu.VMEM((nz, C), F32)],
        name="first",
    )(tokens, wv)


def lane_expand(rows, head, fine):
    col = iota2((C, HD * HD), 1)
    pick = (col % HD) if fine else (col // HD)
    return dot(halves(rows), twice(ones_where(iota2((C, HD * HD), 0) == head * HD + pick)))


def outer_yz(ky, kz, head):
    wide_y = lane_expand(ky, head, False)
    wide_z = lane_expand(kz, head, True)
    ny = ky.shape[0]
    nz = kz.shape[0]
    both = wide_y.reshape(ny, 1, HD * HD) * wide_z.reshape(1, nz, HD * HD)
    return both.reshape(ny * nz, HD * HD).astype(BF)


def repeat_rows(rows):
    n = rows.shape[0]
    return jnp.broadcast_to(rows.reshape(n, 1, C), (n, HD, C)).reshape(n * HD, C)


def second_kernel(
    idx_ref, r_ref, w_ref, vt_ref, send_ref, keep_ref, qo_ref, qk_scr, k_scr, *, sizes
):
    step = pl.program_id(0)
    nx, ny, nz = sizes
    px, rows, _ = r_ref.shape
    gx, gy, gz = idx_ref[0], idx_ref[1], idx_ref[2]
    py = (rows - nx) // 2
    pz = 2
    ry = ny // px
    rz = nz // px
    py = (rows - nx - pz * rz) // ry

    @pl.when(step == 0)
    def _():
        pooled = r_ref[...].reshape(px * rows, C)
        qk = dot(halves(pooled), twice(w_ref[...])).reshape(px, rows, 2 * C)
        qk_scr[...] = qk
        cuts = (0, nx, nx + py * ry, rows)
        scaled = []
        for axis in range(3):
            part = qk[:, cuts[axis] : cuts[axis + 1], :]
            length = px * (cuts[axis + 1] - cuts[axis])
            total = jnp.sum(jnp.sum(part * part, axis=0), axis=0, keepdims=True)
            mean_q = jnp.sum(total[:, :C], axis=1, keepdims=True) / (length * C)
            mean_k = jnp.sum(total[:, C:], axis=1, keepdims=True) / (length * C)
            root = 1.0 / math.sqrt(HD * length)
            scaled.append((lax.rsqrt(mean_q + 1e-06) * root, lax.rsqrt(mean_k + 1e-06)))
        own_x = qk_scr[gx, 0:nx, :]
        own_y = jnp.zeros((px, ry, 2 * C), F32)
        for g in range(py):
            at = nx + g * ry
            own_y = jnp.where(gy == g, qk[:, at : at + ry, :], own_y)
        own_y = own_y.reshape(ny, 2 * C)
        own_z = jnp.zeros((px, rz, 2 * C), F32)
        for g in range(pz):
            at = nx + py * ry + g * rz
            own_z = jnp.where(gz == g, qk[:, at : at + rz, :], own_z)
        own_z = own_z.reshape(nz, 2 * C)
        at = 0
        for own, (scale_q, scale_k) in zip((own_x, own_y, own_z), scaled):
            n = own.shape[0]
            qo_ref[at : at + n, :] = own[:, :C] * scale_q
            k_scr[at : at + n, :] = own[:, C:] * scale_k
            at += n

    half = HEADS // 2
    head = jnp.where(step < half, (1 - gz) * half + step, gz * half + step - half)
    kx = k_scr[0:nx, :]
    ky = k_scr[nx : nx + ny, :]
    kz = k_scr[nx + ny : nx + ny + nz, :]
    mixer = outer_yz(ky, kz, head)
    narrow = dot(vt_ref[0].reshape(nx * HD, ny * nz), mixer).astype(BF)
    shape = (HD * HD, C)
    pick = ones_where(iota2(shape, 1) == head * HD + iota2(shape, 0) // HD)
    spread = dot(jnp.concatenate([pick, pick], axis=1), halves(repeat_rows(kx)), NT)
    n = nx * HD
    same = iota2((HD * HD, n), 0) % HD == iota2((HD * HD, n), 1) % HD
    left = jnp.where(same, spread, 0.0).astype(BF)
    result = dot(left, narrow).astype(BF)

    @pl.when(step < half)
    def _():
        send_ref[...] = result

    @pl.when(step >= half)
    def _():
        keep_ref[...] = result


def second(idx, pooled, w_qk, vt, sizes):
    nx, ny, nz = sizes
    half = HEADS // 2
    block = HD * HD

    def head_of(i, idx_ref):
        gz = idx_ref[2]
        return jnp.where(i < half, (1 - gz) * half + i, gz * half + i - half)

    return pl.pallas_call(
        functools.partial(second_kernel, sizes=sizes),
        grid_spec=pltpu.PrefetchScalarGridSpec(
            num_scalar_prefetch=1,
            grid=(HEADS,),
            in_specs=[
                pl.BlockSpec(pooled.shape, lambda i, s: (0, 0, 0)),
                pl.BlockSpec((C, 2 * C), lambda i, s: (0, 0)),
                pl.BlockSpec((1, nx, HD, ny * nz), lambda i, s: (head_of(i, s), 0, 0, 0)),
            ],
            out_specs=[
                pl.BlockSpec((block, block), lambda i, s: (jnp.minimum(i, half - 1), 0)),
                pl.BlockSpec((block, block), lambda i, s: (jnp.maximum(i - half, 0), 0)),
                pl.BlockSpec((nx + ny + nz, C), lambda i, s: (0, 0)),
            ],
            scratch_shapes=[
                pltpu.VMEM(pooled.shape[:2] + (2 * C,), F32),
                pltpu.VMEM((nx + ny + nz, C), F32),
            ],
        ),
        out_shape=[
            jax.ShapeDtypeStruct((half * block, block), BF),
            jax.ShapeDtypeStruct((half * block, block), BF),
            jax.ShapeDtypeStruct((nx + ny + nz, C), F32),
        ],
        name="second",
    )(idx, pooled, w_qk, vt)


def third_kernel(
    idx_ref, q_ref, mine_ref, other_ref, tok_ref, wo_ref, wg_ref, wd_ref, out_ref, mix_scr, *, chunk
):
    step = pl.program_id(0)
    _, ny, nz, _ = tok_ref.shape
    nx = pl.num_programs(0)
    nx = q_ref.shape[0] - ny - nz
    half = HEADS // 2
    gz = idx_ref[2]

    @pl.when(step == 0)
    def _():
        qx = q_ref[0:nx, :]
        qy = q_ref[nx : nx + ny, :]
        qz = q_ref[nx + ny : nx + ny + nz, :]
        qx_rows = halves(repeat_rows(qx))
        n = nx * HD
        same = iota2((n, HD * HD), 0) % HD == iota2((n, HD * HD), 1) % HD
        for j in range(HEADS):
            source = mine_ref if j < half else other_ref
            head = jnp.where(gz == 0, j, (j + half) % HEADS)
            local = j % half
            mixer = outer_yz(qy, qz, head)
            shape = (C, HD * HD)
            pick = ones_where(iota2(shape, 0) == head * HD + iota2(shape, 1) // HD)
            left = jnp.where(same, dot(qx_rows, twice(pick)), 0.0).astype(BF)
            core = source[local * HD * HD : (local + 1) * HD * HD, :]
            narrow = dot(left, core).astype(BF)
            mixed = dot(narrow, mixer, NT).astype(BF)
            mix_scr[:, head, :, :] = mixed.reshape(nx, HD, ny * nz)

    mixed_t = mix_scr[step].reshape(C, ny * nz)
    mixed = mixed_t.T
    tok = tok_ref[0].reshape(ny * nz, C)
    out = []
    for at in range(0, ny * nz, chunk):
        resid = tok[at : at + chunk].astype(F32) + dot(mixed[at : at + chunk], wo_ref[...])
        inner = norm_rows(resid).astype(BF)
        both = dot(inner, wg_ref[...])
        hidden = (jax.nn.gelu(both[:, :FF]) * both[:, FF:]).astype(BF)
        result = (resid + dot(hidden, wd_ref[...])).astype(BF)
        out_ref[0, at // nz : (at + chunk) // nz] = result.reshape(chunk // nz, nz, C)


def third(idx, q, mine, other, tokens, w_out, w_gate_up, w_down):
    nx, ny, nz, _ = tokens.shape
    full = lambda a: pl.BlockSpec(a.shape, lambda i, s: (0,) * a.ndim)
    slab = pl.BlockSpec((1, ny, nz, C), lambda i, s: (i, 0, 0, 0))
    return pl.pallas_call(
        functools.partial(third_kernel, chunk=min(256, ny * nz)),
        grid_spec=pltpu.PrefetchScalarGridSpec(
            num_scalar_prefetch=1,
            grid=(nx,),
            in_specs=[
                full(q),
                full(mine),
                full(other),
                slab,
                full(w_out),
                full(w_gate_up),
                full(w_down),
            ],
            out_specs=slab,
            scratch_shapes=[pltpu.VMEM((nx, HEADS, HD, ny * nz), BF)],
        ),
        out_shape=jax.ShapeDtypeStruct(tokens.shape, BF),
        name="third",
    )(idx, q, mine, other, tokens, w_out, w_gate_up, w_down)


def a2a(values, axes):
    return lax.all_to_all(values, axes, 0, 0, tiled=True)


def body(tokens, w_qkv, w_out, w_gate_up, w_down):
    nx, ny, nz, _ = tokens.shape
    cx, cy, cz = (lax.axis_size(a) for a in ("gx", "gy", "gz"))
    idx = jnp.stack([lax.axis_index(a) for a in ("gx", "gy", "gz")]).astype(jnp.int32)
    ry = ny // cx
    rz = nz // cx
    vt, pool, sum_x = first(tokens, w_qkv[:, 2 * C :], cx)
    got = jnp.sum(a2a(pool, "gx"), axis=0)
    packed = jnp.concatenate([sum_x, got], axis=0)
    wide = jnp.broadcast_to(packed, (cy * cz,) + packed.shape)
    wide = a2a(wide, ("gy", "gz")).reshape(cy, cz, *packed.shape)
    total_x = jnp.sum(wide[:, :, :nx], axis=(0, 1))
    total_y = jnp.sum(wide[:, :, nx : nx + ry], axis=1).reshape(cy * ry, C)
    total_z = jnp.sum(wide[:, :, nx + ry : nx + ry + rz], axis=0).reshape(cz * rz, C)
    packed = jnp.concatenate([total_x, total_y, total_z], axis=0)
    pooled = a2a(jnp.broadcast_to(packed, (cx,) + packed.shape), "gx")

    send, keep, q = second(idx, pooled, w_qkv[:, : 2 * C], vt, (nx, ny, nz))
    swap = [(0, 1), (1, 0)]
    part = keep.astype(F32) + lax.ppermute(send, "gz", swap).astype(F32)
    size = cx * cy
    part = part.astype(BF).reshape(size, -1, HD * HD)
    piece = jnp.sum(a2a(part, ("gx", "gy")).astype(F32), axis=0).astype(BF)
    mine = a2a(jnp.broadcast_to(piece, (size,) + piece.shape), ("gx", "gy"))
    mine = mine.reshape(keep.shape)
    other = lax.ppermute(mine, "gz", swap)
    return third(idx, q, mine, other, tokens, w_out, w_gate_up, w_down)


def solution(mesh):
    in_specs = (P("gx", "gy", "gz", None), P(), P(), P(), P())
    out_specs = P("gx", "gy", "gz", None)
    return jax.shard_map(body, mesh=mesh, in_specs=in_specs, out_specs=out_specs, check_vma=False)
```

time: 1140 us -> 155 us (0.14)
  blocking collectives: 973 us -> 82.3 us
  local copies, waits for them, and re-layouts: 70.5 us -> 4.28 us
  Pallas kernels: 0 us -> 45.9 us
  matrix products: 33.2 us -> 0 us
  other arithmetic: 28.1 us -> 2.67 us
  starting transfers between devices: 22.2 us -> 9.5 us
    psum x3 -> x0, blocking collectives: 736 us -> none  [the longest x1 590 us: body(): total_z = lax.psum(part_z, ('gx', 'gy'))]
    all_gather x3 -> x0, blocking collectives: 178 us -> none  [the longest x1 118 us: body(): lax.all_gather(total_z.astype(jnp.bfloat16), 'gz', axis=0, tiled=True)]
    pallas_call x0 -> x3, Pallas kernels: none -> 45.9 us  [the longest x1 28.9 us: third(): pl.pallas_call(functools.partial(third_kernel, chunk=min(256, ny * nz)),...]
    dot_general x38 -> x0, matrix products: 33.2 us -> none  [the longest x8 11.8 us: project(): jnp.dot(normed.reshape(-1, width), w_qkv, preferred_element_type=jnp.floa...]
    reduce_sum x39 -> x5, other arithmetic: 27.9 us -> 0.21 us  [the longest x1 0.14 us: body(): piece = jnp.sum(a2a(part, ('gx', 'gy')).astype(F32), axis=0).astype(BF)]
    all_to_all x3 -> x4, blocking collectives: 58.9 us -> 82.3 us  [a2a(): return lax.all_to_all(values, axes, 0, 0, tiled=True)]
    all_to_all x3 -> x1, starting transfers between devices: 22.2 us -> 3.52 us  [a2a(): return lax.all_to_all(values, axes, 0, 0, tiled=True)]
    all_to_all x5 -> x0, local copies, waits for them, and re-layouts: 16.5 us -> none  [the longest x1 7.3 us: body(): lax.all_to_all(after_y, 'gz', split_axis=0, concat_axis=2, tiled=True)]
  transfers between devices with their start and end apart: 3 -> 3, of which waited for: 0 -> 3; matrix products, arithmetic and copies ran while one was open for 1% -> 1% of each run, Pallas kernels for 0% -> 0%
where the time goes in v1:
time: 155 us; the launch traced here: 154 us
  blocking collectives  82.3 us (53%)
  Pallas kernels  45.9 us (30%)
  starting transfers between devices  9.5 us (6%)
  waiting for transfers between devices  9.48 us (6%)
  local copies, waits for them, and re-layouts  4.28 us (3%)
  other arithmetic  2.67 us (2%)
    all_to_all x4, blocking collectives, a2a(): return lax.all_to_all(values, axes, 0, 0, tiled=True)  82.3 us
    pallas_call x1, Pallas kernels, third(): pl.pallas_call(functools.partial(third_kernel, chunk=min(256, ny * nz)),...  28.9 us
    pallas_call x1, Pallas kernels, second(): pl.pallas_call(functools.partial(second_kernel, sizes=sizes), grid_spec=p...  9.21 us
    pallas_call x1, Pallas kernels, first(): pl.pallas_call(first_kernel, grid=(nx,), in_specs=[pl.BlockSpec((1, ny, n...  7.71 us
    all_to_all x1, waiting for transfers between devices, a2a(): return lax.all_to_all(values, axes, 0, 0, tiled=True)  6.2 us
    ppermute x1, starting transfers between devices, body(): other = lax.ppermute(mine, 'gz', swap)  3.8 us
    all_to_all x1, starting transfers between devices, a2a(): return lax.all_to_all(values, axes, 0, 0, tiled=True)  3.52 us
  transfers between devices with their start and end apart: 3, of which 3 were waited for; matrix products, arithmetic and copies ran while one was open for 1% of the time, Pallas kernels for 0%

profile of v1, /device:TPU:1, one launch (start us, length us, event | category | flops | bytes accessed | tf_op | source)
XLA Modules:
  0.0 154.1 jit_solution(7852201812382191912)
XLA Ops:
  0.0 0.0 copy-start.3
  0.0 1.4 slice.15.wv_ref
  1.4 7.7 %first.1 = (bf16[8,8,16,1024]{3,2,1,0:T(8,128)(2,1)}, f32[16,8,128]{2,1,0:T(8,128)}, f32[8,128]{1,0:T(8,128)}) custom-call(bf16[8,16,64,128]{3,2,1,0:T(8,128)(2,1)} %tok_ref.3, bf16[128,128]{1,0:T(8,128)(2,1)} %slice.15.wv_ref), custom_call_target="tpu_custom_call" | custom-call | tf_op jit(solution)/shard_map/first/pallas_call | solution.py:84
  9.1 17.5 %all_to_all.25 = f32[16,8,128]{2,1,0:T(8,128)S(1)} all-to-all(f32[16,8,128]{2,1,0:T(8,128)} %get-tuple-element.12), channel_id=1, replica_groups=mesh['gx'=16,'gy'=8,'gz'=2] {'gx'}, dimensions={0} | all-to-all | bytes 131072 | tf_op jit(solution)/shard_map/all_to_all | solution.py:305
  26.7 0.7 pad_maximum_fusion.1
  27.4 16.1 %all_to_all.26 = f32[16,16,128]{2,1,0:T(8,128)S(1)} all-to-all(f32[16,16,128]{2,1,0:T(8,128)S(1)} %broadcast_in_dim.9), channel_id=1, replica_groups=mesh['gx'=16,'gy'=8,'gz'=2] {'gy','gz'}, dimensions={0} | all-to-all | bytes 262144 | tf_op jit(solution)/shard_map/all_to_all | solution.py:305
  43.5 0.7 broadcast_in_dim.10
  44.2 3.5 %all-to-all-start.2 = ((f32[16,24,128]{2,1,0:T(8,128)}), f32[16,24,128]{2,1,0:T(8,128)S(1)}, u32[]{:S(2)}, u32[]{:S(2)}) async-start(f32[16,24,128]{2,1,0:T(8,128)} %broadcast_in_dim.10), calls=%async_computation.2 | async-start | bytes 393216 | tf_op jit(solution)/shard_map/all_to_all | solution.py:305
  47.7 0.0 copy-done.3
  47.8 0.6 slice.19.w_ref
  48.4 0.6 pad_add_fusion.idx_ref
  49.0 6.2 %all-to-all-done.2.r_ref = f32[16,24,128]{2,1,0:T(8,128)S(1)} async-done(((f32[16,24,128]{2,1,0:T(8,128)}), f32[16,24,128]{2,1,0:T(8,128)S(1)}, u32[]{:S(2)}, u32[]{:S(2)}) %all-to-all-start.2) | async-done | bytes 196640 | tf_op jit(solution)/shard_map/all_to_all | solution.py:305
  55.2 0.0 copy-start.1
  55.2 0.7 copy-done.1
  55.9 9.2 %second.1 = (bf16[1024,256]{1,0:T(8,128)(2,1)}, bf16[1024,256]{1,0:T(8,128)(2,1)}, f32[88,128]{1,0:T(8,128)}) custom-call(s32[3]{0:T(128)} %pad_add_fusion.idx_ref, f32[16,24,128]{2,1,0:T(8,128)} %copy-done.1, bf16[128,256]{1,0:T(8,128)(2,1)} %slice.19.w_ref, bf16[8,8,16,1024]{3,2,1,0:T(8,128)(2,1)} %get-tuple-element.13.vt_ref), custom_call_target="tpu_custom_call" | custom-call | tf_op jit(solution)/shard_map/second/pallas_call | solution.py:205
  65.1 2.2 %collective-permute-start = (bf16[1024,256]{1,0:T(8,128)(2,1)}, bf16[1024,256]{1,0:T(8,128)(2,1)S(1)}, u32[]{:S(2)}, u32[]{:S(2)}) collective-permute-start(bf16[1024,256]{1,0:T(8,128)(2,1)} %get-tuple-element.16), channel_id=1, source_target_pairs={{0,1},{1,0},{2,3},{3,2},{4,5},{5,4},{6,7},{7,6},{8,9},{9,8},{10,11... | collective-permute-start | bytes 1572872 | tf_op jit(solution)/shard_map/ppermute | solution.py:327
  67.2 1.7 %collective-permute-done = bf16[1024,256]{1,0:T(8,128)(2,1)S(1)} collective-permute-done((bf16[1024,256]{1,0:T(8,128)(2,1)}, bf16[1024,256]{1,0:T(8,128)(2,1)S(1)}, u32[]{:S(2)}, u32[]{:S(2)}) %collective-permute-start) | collective-permute-done | bytes 524320 | tf_op jit(solution)/shard_map/ppermute | solution.py:327
  69.0 1.2 fusion
  70.2 25.0 %all_to_all.27 = bf16[128,8,256]{2,1,0:T(8,128)(2,1)S(1)} all-to-all(bf16[128,8,256]{2,1,0:T(8,128)(2,1)S(1)} %fusion), channel_id=1, replica_groups=mesh['gx'=16,'gy'=8,'gz'=2] {'gx','gy'}, dimensions={0} | all-to-all | bytes 1048576 | tf_op jit(solution)/shard_map/all_to_all | solution.py:305
  95.2 0.1 reduce_sum.52
  95.4 23.6 %all_to_all.28 = bf16[128,8,256]{2,1,0:T(8,128)(2,1)S(1)} all-to-all(bf16[128,8,256]{2,1,0:T(8,128)(2,1)S(1)} %broadcast_in_dim.11), channel_id=1, replica_groups=mesh['gx'=16,'gy'=8,'gz'=2] {'gx','gy'}, dimensions={0} | all-to-all | bytes 1048576 | tf_op jit(solution)/shard_map/all_to_all | solution.py:305
  119.0 0.0 copy-start
  119.0 3.8 %collective-permute-start.1 = (bf16[1024,256]{1,0:T(8,128)(2,1)S(1)}, bf16[1024,256]{1,0:T(8,128)(2,1)S(1)}, u32[]{:S(2)}, u32[]{:S(2)}) collective-permute-start(bf16[1024,256]{1,0:T(8,128)(2,1)S(1)} %bitcast.8), channel_id=1, source_target_pairs={{0,1},{1,0},{2,3},{3,2},{4,5},{5,4},{6,7},{7,6},{8,9},{9,8},{10,11... | collective-permute-start | bytes 1572872 | tf_op jit(solution)/shard_map/ppermute | solution.py:333
  122.8 1.5 collective-permute-done.1.other_ref
  124.4 0.0 copy-start.2
  124.4 0.0 copy-done
  124.4 0.8 copy-done.2
  125.2 28.9 %third.1 = bf16[8,16,64,128]{3,2,1,0:T(8,128)(2,1)} custom-call(s32[3]{0:T(128)} %pad_add_fusion.idx_ref, f32[88,128]{1,0:T(8,128)} %get-tuple-element.14.q_ref, bf16[1024,256]{1,0:T(8,128)(2,1)} %bitcast.9, bf16[1024,256]{1,0:T(8,128)(2,1)} %copy-done.2, bf16[8,16,64,128]{3,2,1,0:T(8,128)(2,1)} %tok_ref.3, bf16[128,128]{1,0:T(8,128)(2,1)} %wo_ref.1, ...), custom_call_target="tpu_custom_call" | custom-call | tf_op jit(solution)/shard_map/third/pallas_call | solution.py:282
  (7 shorter events, 0.1 us)
Async XLA Ops:
  0.0 47.7 %copy-start.3 = (bf16[128,384]{1,0:T(8,128)(2,1)S(1)}, bf16[128,384]{1,0:T(8,128)(2,1)}, u32[]{:S(2)}) copy-start(bf16[128,384]{1,0:T(8,128)(2,1)} %param.6) | copy-start | bytes 294916
  44.2 11.0 %all-to-all-start.2 = ((f32[16,24,128]{2,1,0:T(8,128)}), f32[16,24,128]{2,1,0:T(8,128)S(1)}, u32[]{:S(2)}, u32[]{:S(2)}) async-start(f32[16,24,128]{2,1,0:T(8,128)} %broadcast_in_dim.10), calls=%async_computation.2 | async-start | bytes 393216 | tf_op jit(solution)/shard_map/all_to_all | solution.py:305
  55.2 0.7 copy-start.1
  65.1 3.9 %collective-permute-start = (bf16[1024,256]{1,0:T(8,128)(2,1)}, bf16[1024,256]{1,0:T(8,128)(2,1)S(1)}, u32[]{:S(2)}, u32[]{:S(2)}) collective-permute-start(bf16[1024,256]{1,0:T(8,128)(2,1)} %get-tuple-element.16), channel_id=1, source_target_pairs={{0,1},{1,0},{2,3},{3,2},{4,5},{5,4},{6,7},{7,6},{8,9},{9,8},{10,11... | collective-permute-start | bytes 1572872 | tf_op jit(solution)/shard_map/ppermute | solution.py:327
  119.0 5.3 %copy-start = (bf16[128,8,256]{2,1,0:T(8,128)(2,1)}, bf16[128,8,256]{2,1,0:T(8,128)(2,1)S(1)}, u32[]{:S(2)}) copy-start(bf16[128,8,256]{2,1,0:T(8,128)(2,1)S(1)} %all_to_all.28) | copy-start | bytes 1572868
  119.0 5.3 %collective-permute-start.1 = (bf16[1024,256]{1,0:T(8,128)(2,1)S(1)}, bf16[1024,256]{1,0:T(8,128)(2,1)S(1)}, u32[]{:S(2)}, u32[]{:S(2)}) collective-permute-start(bf16[1024,256]{1,0:T(8,128)(2,1)S(1)} %bitcast.8), channel_id=1, source_target_pairs={{0,1},{1,0},{2,3},{3,2},{4,5},{5,4},{6,7},{7,6},{8,9},{9,8},{10,11... | collective-permute-start | bytes 1572872 | tf_op jit(solution)/shard_map/ppermute | solution.py:333
  124.4 0.8 copy-start.2

commit v2 on v1

v2 whole, which is shorter than its diff:
```python
import functools
import math

import jax
import jax.numpy as jnp
from jax import lax
from jax.experimental import pallas as pl
from jax.experimental.pallas import tpu as pltpu
from jax.sharding import PartitionSpec as P

HEADS = 8
HD = 16
C = 128
FF = 512
EPS = 1e-05

BF = jnp.bfloat16
F32 = jnp.float32
NT = (((1,), (1,)), ((), ()))


def dot(a, b, dims=(((1,), (0,)), ((), ()))):
    return lax.dot_general(a, b, dims, preferred_element_type=F32)


def norm_rows(values):
    mean = jnp.mean(values, axis=-1, keepdims=True)
    centred = values - mean
    spread = jnp.mean(centred * centred, axis=-1, keepdims=True)
    return centred * lax.rsqrt(spread + EPS)


def halves(values):
    high = values.astype(BF)
    low = (values - high.astype(F32)).astype(BF)
    return jnp.concatenate([high, low], axis=1)


def twice(values):
    return jnp.concatenate([values, values], axis=0)


def iota2(shape, dim):
    return lax.broadcasted_iota(jnp.int32, shape, dim)


def ones_where(cond):
    return jnp.where(cond, 1.0, 0.0).astype(BF)


def first_kernel(tok_ref, wv_ref, vt_ref, pool_ref, sx_ref, sy_acc, sz_acc):
    step = pl.program_id(0)
    nb, ny, nz, _ = tok_ref.shape
    x = tok_ref[...].reshape(nb * ny * nz, C).astype(F32)
    normed = norm_rows(x).astype(BF)
    wvt = wv_ref[...].T
    n32 = normed.astype(F32).reshape(nb, ny, nz, C)
    sxy = jnp.sum(n32, axis=2)
    sy = jnp.sum(sxy, axis=0)
    sz = jnp.sum(jnp.sum(n32, axis=0), axis=0)
    sx_ref[0] = jnp.sum(sxy, axis=1)
    for i in range(nb):
        vt = dot(wvt, normed[i * ny * nz : (i + 1) * ny * nz], NT).astype(BF)
        vt_ref[:, i, :, :] = vt.reshape(HEADS, HD, ny * nz)

    @pl.when(step == 0)
    def _():
        sy_acc[...] = jnp.zeros_like(sy_acc)
        sz_acc[...] = jnp.zeros_like(sz_acc)

    sy_acc[...] += sy
    sz_acc[...] += sz

    @pl.when(step == pl.num_programs(0) - 1)
    def _():
        parts = pool_ref.shape[0]
        ry = ny // parts
        rz = nz // parts
        pool_ref[...] = jnp.zeros_like(pool_ref)
        pool_ref[:, 0:ry, :] = sy_acc[...].reshape(parts, ry, C)
        pool_ref[:, ry : ry + rz, :] = sz_acc[...].reshape(parts, rz, C)


def first(tokens, w_qkv, parts, block=4):
    nx, ny, nz, _ = tokens.shape
    rows = -(-(ny // parts + nz // parts) // 8) * 8
    return pl.pallas_call(
        first_kernel,
        grid=(nx // block,),
        in_specs=[
            pl.BlockSpec((block, ny, nz, C), lambda i: (i, 0, 0, 0)),
            pl.BlockSpec((C, C), lambda i: (0, 2)),
        ],
        out_specs=[
            pl.BlockSpec((HEADS, block, HD, ny * nz), lambda i: (0, i, 0, 0)),
            pl.BlockSpec((parts, rows, C), lambda i: (0, 0, 0)),
            pl.BlockSpec((1, block, C), lambda i: (i, 0, 0)),
        ],
        out_shape=[
            jax.ShapeDtypeStruct((HEADS, nx, HD, ny * nz), BF),
            jax.ShapeDtypeStruct((parts, rows, C), F32),
            jax.ShapeDtypeStruct((nx // block, block, C), F32),
        ],
        scratch_shapes=[pltpu.VMEM((ny, C), F32), pltpu.VMEM((nz, C), F32)],
        name="first",
    )(tokens, w_qkv)


def lane_expand(rows, head, fine):
    col = iota2((C, HD * HD), 1)
    pick = (col % HD) if fine else (col // HD)
    return dot(halves(rows), twice(ones_where(iota2((C, HD * HD), 0) == head * HD + pick)))


def outer_yz(ky, kz, head):
    wide_y = lane_expand(ky, head, False)
    wide_z = lane_expand(kz, head, True)
    ny = ky.shape[0]
    nz = kz.shape[0]
    both = wide_y.reshape(ny, 1, HD * HD) * wide_z.reshape(1, nz, HD * HD)
    return both.reshape(ny * nz, HD * HD).astype(BF)


def reorder(n, major):
    out, src = iota2((n * HD, n * HD), 0), iota2((n * HD, n * HD), 1)
    cx, xc = (out, src) if major else (src, out)
    return ones_where((cx // n == xc % HD) & (cx % n == xc // HD))


def second_kernel(
    idx_ref, r_ref, w_ref, vt_ref, send_ref, keep_ref, qo_ref, kx_ref, k_scr, *, sizes
):
    step = pl.program_id(0)
    nx, ny, nz = sizes
    px, rows, _ = r_ref.shape
    gx, gy, gz = idx_ref[0], idx_ref[1], idx_ref[2]
    ry = ny // px
    rz = nz // px
    pz = 2
    py = (rows - nx - pz * rz) // ry
    half = HEADS // pz

    @pl.when(step == 0)
    def _():
        pooled = r_ref[...].reshape(px * rows, C)
        qk = dot(halves(pooled), twice(w_ref[...])).reshape(px, rows, 2 * C)
        cuts = (0, nx, nx + py * ry, rows)
        scaled = []
        for axis in range(3):
            part = qk[:, cuts[axis] : cuts[axis + 1], :]
            length = px * (cuts[axis + 1] - cuts[axis])
            total = jnp.sum(jnp.sum(part * part, axis=0), axis=0, keepdims=True)
            mean_q = jnp.sum(total[:, :C], axis=1, keepdims=True) / (length * C)
            mean_k = jnp.sum(total[:, C:], axis=1, keepdims=True) / (length * C)
            root = 1.0 / math.sqrt(HD * length)
            scaled.append((lax.rsqrt(mean_q + 1e-06) * root, lax.rsqrt(mean_k + 1e-06)))
        all_x = qk[:, 0:nx, :].reshape(px * nx, 2 * C)
        owned = gz * half + gx // (px // half)
        query = all_x[:, :C] * scaled[0][0]
        key_part = all_x[:, C:] * scaled[0][1]
        key_part = jnp.where(iota2(key_part.shape, 1) // HD == owned, key_part, 0.0)
        q_terms, k_terms = halves(query), halves(key_part)
        q_terms = jnp.concatenate([q_terms, q_terms[:, :C]], axis=1)
        k_terms = jnp.concatenate([k_terms[:, :C], k_terms[:, :C], k_terms[:, C:]], axis=1)
        kx_ref[...] = dot(q_terms, k_terms, NT).astype(BF)
        own_y = jnp.zeros((px, ry, 2 * C), F32)
        for g in range(py):
            at = nx + g * ry
            own_y = jnp.where(gy == g, qk[:, at : at + ry, :], own_y)
        own_y = own_y.reshape(ny, 2 * C)
        own_z = jnp.zeros((px, rz, 2 * C), F32)
        for g in range(pz):
            at = nx + py * ry + g * rz
            own_z = jnp.where(gz == g, qk[:, at : at + rz, :], own_z)
        own_z = own_z.reshape(nz, 2 * C)
        at = 0
        for own, (scale_q, scale_k) in zip((own_y, own_z), scaled[1:]):
            n = own.shape[0]
            qo_ref[at : at + n, :] = own[:, :C] * scale_q
            k_scr[at : at + n, :] = own[:, C:] * scale_k
            at += n

    ky = k_scr[0:ny, :]
    kz = k_scr[ny : ny + nz, :]
    perm = reorder(nx, True)
    first_head = jnp.where(step == 0, (1 - gz) * half, gz * half)

    def contract(out_ref):
        for j in range(half):
            mixer = outer_yz(ky, kz, first_head + j)
            narrow = dot(vt_ref[j].reshape(nx * HD, ny * nz), mixer).astype(BF)
            narrow = dot(perm, narrow).astype(BF).reshape(HD, nx, HD * HD)
            for side in range(2):
                cut = narrow[:, :, side * C : (side + 1) * C]
                out_ref[j * HD : (j + 1) * HD, side] = cut

    @pl.when(step == 0)
    def _():
        contract(send_ref)

    @pl.when(step == 1)
    def _():
        contract(keep_ref)


def second(idx, pooled, w_qkv, vt, sizes):
    nx, ny, nz = sizes
    half = HEADS // 2
    core = (half * HD, 2, nx, C)
    return pl.pallas_call(
        functools.partial(second_kernel, sizes=sizes),
        grid_spec=pltpu.PrefetchScalarGridSpec(
            num_scalar_prefetch=1,
            grid=(2,),
            in_specs=[
                pl.BlockSpec(memory_space=pltpu.VMEM),
                pl.BlockSpec((C, 2 * C), lambda i, s: (0, 0)),
                pl.BlockSpec(
                    (half, nx, HD, ny * nz),
                    lambda i, s: (jnp.where(i == 0, 1 - s[2], s[2]), 0, 0, 0),
                ),
            ],
            out_specs=[
                pl.BlockSpec(core, lambda i, s: (0, 0, 0, 0)),
                pl.BlockSpec(core, lambda i, s: (0, 0, 0, 0)),
                pl.BlockSpec((ny + nz, C), lambda i, s: (0, 0)),
                pl.BlockSpec((C, C), lambda i, s: (0, 0)),
            ],
            scratch_shapes=[pltpu.VMEM((ny + nz, C), F32)],
        ),
        out_shape=[
            jax.ShapeDtypeStruct(core, BF),
            jax.ShapeDtypeStruct(core, BF),
            jax.ShapeDtypeStruct((ny + nz, C), F32),
            jax.ShapeDtypeStruct((C, C), BF),
        ],
        name="second",
    )(idx, pooled, w_qkv, vt)


def middle_kernel(g_ref, kx_ref, out_ref):
    px, py, nx, _ = g_ref.shape
    lines = jnp.sum(g_ref[...].astype(F32), axis=1).reshape(px * nx, C)
    high = lines.astype(BF)
    low = (lines - high.astype(F32)).astype(BF)
    kx = kx_ref[...]
    mixed = dot(jnp.concatenate([kx, kx], axis=1), jnp.concatenate([high, low], axis=0))
    mixed = mixed.astype(BF).reshape(px, 1, nx, C)
    out_ref[...] = jnp.broadcast_to(mixed, out_ref.shape)


def middle(gathered, kx):
    vmem = pl.BlockSpec(memory_space=pltpu.VMEM)
    return pl.pallas_call(
        middle_kernel,
        in_specs=[vmem, vmem],
        out_specs=vmem,
        out_shape=jax.ShapeDtypeStruct(gathered.shape, BF),
        name="middle",
    )(gathered, kx)


def third_kernel(
    idx_ref, q_ref, mine_ref, other_ref, tok_ref, wo_ref, wg_ref, wd_ref, out_ref, mix_scr
):
    step = pl.program_id(0)
    nb, ny, nz, _ = tok_ref.shape
    nx = mix_scr.shape[0]
    half = HEADS // 2
    gz = idx_ref[2]

    @pl.when(step == 0)
    def _():
        qy = q_ref[0:ny, :]
        qz = q_ref[ny : ny + nz, :]
        perm = reorder(nx, False)
        for j in range(HEADS):
            source = mine_ref if j < half else other_ref
            head = jnp.where(gz == 0, j, (j + half) % HEADS)
            at = j % half * HD
            mixer = outer_yz(qy, qz, head)
            sides = [source[at : at + HD, i].reshape(HD * nx, C) for i in range(2)]
            narrow = dot(perm, jnp.concatenate(sides, axis=1)).astype(BF)
            mixed = dot(narrow, mixer, NT).astype(BF)
            mix_scr[:, head, :, :] = mixed.reshape(nx, HD, ny * nz)

    mixed = [mix_scr[step * nb + i].reshape(C, ny * nz).T for i in range(nb)]
    mixed = jnp.concatenate(mixed, axis=0)
    tok = tok_ref[...].reshape(nb * ny * nz, C)
    resid = tok.astype(F32) + dot(mixed, wo_ref[...])
    inner = norm_rows(resid).astype(BF)
    both = dot(inner, wg_ref[...])
    hidden = (jax.nn.gelu(both[:, :FF]) * both[:, FF:]).astype(BF)
    result = (resid + dot(hidden, wd_ref[...])).astype(BF)
    out_ref[...] = result.reshape(nb, ny, nz, C)


def third(idx, q, mine, other, tokens, w_out, w_gate_up, w_down, block=2):
    nx, ny, nz, _ = tokens.shape
    full = lambda a: pl.BlockSpec(a.shape, lambda i, s: (0,) * a.ndim)
    slab = pl.BlockSpec((block, ny, nz, C), lambda i, s: (i, 0, 0, 0))
    vmem = pl.BlockSpec(memory_space=pltpu.VMEM)
    return pl.pallas_call(
        third_kernel,
        grid_spec=pltpu.PrefetchScalarGridSpec(
            num_scalar_prefetch=1,
            grid=(nx // block,),
            in_specs=[
                full(q),
                vmem,
                vmem,
                slab,
                full(w_out),
                full(w_gate_up),
                full(w_down),
            ],
            out_specs=slab,
            scratch_shapes=[pltpu.VMEM((nx, HEADS, HD, ny * nz), BF)],
        ),
        out_shape=jax.ShapeDtypeStruct(tokens.shape, BF),
        name="third",
    )(idx, q, mine, other, tokens, w_out, w_gate_up, w_down)


def a2a(values, axes):
    return lax.all_to_all(values, axes, 0, 0, tiled=True)


def body(tokens, w_qkv, w_out, w_gate_up, w_down):
    nx, ny, nz, _ = tokens.shape
    cx, cy, cz = (lax.axis_size(a) for a in ("gx", "gy", "gz"))
    idx = jnp.stack([lax.axis_index(a) for a in ("gx", "gy", "gz")]).astype(jnp.int32)
    ry = ny // cx
    rz = nz // cx
    vt, pool, sum_x = first(tokens, w_qkv, cx)
    sum_x = sum_x.reshape(nx, C)
    got = jnp.sum(a2a(pool, "gx"), axis=0)
    packed = jnp.concatenate([sum_x, got], axis=0)
    wide = jnp.broadcast_to(packed, (cy * cz,) + packed.shape)
    wide = a2a(wide, ("gy", "gz")).reshape(cy, cz, *packed.shape)
    total_x = jnp.sum(wide[:, :, :nx], axis=(0, 1))
    total_y = jnp.sum(wide[:, :, nx : nx + ry], axis=1).reshape(cy * ry, C)
    total_z = jnp.sum(wide[:, :, nx + ry : nx + ry + rz], axis=0).reshape(cz * rz, C)
    packed = jnp.concatenate([total_x, total_y, total_z], axis=0)
    pooled = a2a(jnp.broadcast_to(packed, (cx,) + packed.shape), "gx")

    send, keep, q, kx = second(idx, pooled, w_qkv, vt, (nx, ny, nz))
    swap = [(0, 1), (1, 0)]
    part = keep.astype(F32) + lax.ppermute(send, "gz", swap).astype(F32)
    part = part.astype(BF).reshape(cx * cy, nx, C)
    gathered = a2a(part, ("gx", "gy")).reshape(cx, cy, nx, C)
    spread = middle(gathered, kx).reshape(cx * cy, nx, C)
    mine = a2a(spread, ("gx", "gy")).reshape(keep.shape)
    other = lax.ppermute(mine, "gz", swap)
    return third(idx, q, mine, other, tokens, w_out, w_gate_up, w_down)


def solution(mesh):
    in_specs = (P("gx", "gy", "gz", None), P(), P(), P(), P())
    out_specs = P("gx", "gy", "gz", None)
    return jax.shard_map(body, mesh=mesh, in_specs=in_specs, out_specs=out_specs, check_vma=False)
```

time: 155 us -> 129 us (0.83)
  Pallas kernels: 45.9 us -> 33.1 us
  blocking collectives: 82.3 us -> 72.7 us
  local copies, waits for them, and re-layouts: 4.28 us -> 2.07 us
    pallas_call x2 -> x3, Pallas kernels: 36.7 us -> 25.6 us  [the longest x1 18.2 us: third(): pl.pallas_call(third_kernel, grid_spec=pltpu.PrefetchScalarGridSpec(num_s...]
    all_to_all x4, blocking collectives: 82.3 us -> 72.7 us  [a2a(): return lax.all_to_all(values, axes, 0, 0, tiled=True)]
    slice x2 -> x0, local copies, waits for them, and re-layouts: 2.05 us -> none  [the longest x1 1.43 us: body(): vt, pool, sum_x = first(tokens, w_qkv[:, 2 * C:], cx)]
    pallas_call x1, Pallas kernels: 9.21 us -> 7.51 us  [second(): pl.pallas_call(functools.partial(second_kernel, sizes=sizes), grid_spec=p...]
  transfers between devices with their start and end apart: 3 -> 3, of which waited for: 3 -> 3; matrix products, arithmetic and copies ran while one was open for 1% -> 0% of each run, Pallas kernels for 0% -> 0%
where the time goes in v2:
time: 129 us
  blocking collectives  72.7 us (56%)
  Pallas kernels  33.1 us (26%)
  waiting for transfers between devices  9.39 us (7%)
  starting transfers between devices  9.23 us (7%)
  other arithmetic  2.34 us (2%)
  local copies, waits for them, and re-layouts  2.07 us (2%)
    all_to_all x4, blocking collectives, a2a(): return lax.all_to_all(values, axes, 0, 0, tiled=True)  72.7 us
    pallas_call x1, Pallas kernels, third(): pl.pallas_call(third_kernel, grid_spec=pltpu.PrefetchScalarGridSpec(num_s...  18.2 us
    pallas_call x1, Pallas kernels, second(): pl.pallas_call(functools.partial(second_kernel, sizes=sizes), grid_spec=p...  7.51 us
    all_to_all x1, waiting for transfers between devices, a2a(): return lax.all_to_all(values, axes, 0, 0, tiled=True)  6.86 us
    pallas_call x1, Pallas kernels, first(): pl.pallas_call(first_kernel, grid=(nx // block,), in_specs=[pl.BlockSpec(...  5.53 us
    ppermute x1, starting transfers between devices, body(): other = lax.ppermute(mine, 'gz', swap)  3.53 us
    all_to_all x1, starting transfers between devices, a2a(): return lax.all_to_all(values, axes, 0, 0, tiled=True)  3.52 us
  transfers between devices with their start and end apart: 3, of which 3 were waited for; matrix products, arithmetic and copies ran while one was open for 0% of the time, Pallas kernels for 0%

profile of v2, /device:TPU:1, one launch (start us, length us, event | category | flops | bytes accessed | tf_op | source)
XLA Modules:
  0.0 128.9 jit_solution(11777286219665291197)
XLA Ops:
  0.0 5.5 %first.1 = (bf16[8,8,16,1024]{3,2,1,0:T(8,128)(2,1)}, f32[16,8,128]{2,1,0:T(8,128)}, f32[2,4,128]{2,1,0:T(4,128)}) custom-call(bf16[8,16,64,128]{3,2,1,0:T(8,128)(2,1)} %tok_ref.3, bf16[128,384]{1,0:T(8,128)(2,1)} %w_ref.1), custom_call_target="tpu_custom_call" | custom-call | tf_op jit(solution)/shard_map/first/pallas_call | solution.py:87
  5.5 17.5 %all_to_all.25 = f32[16,8,128]{2,1,0:T(8,128)S(1)} all-to-all(f32[16,8,128]{2,1,0:T(8,128)} %get-tuple-element.13), channel_id=1, replica_groups=mesh['gx'=16,'gy'=8,'gz'=2] {'gx'}, dimensions={0} | all-to-all | bytes 131072 | tf_op jit(solution)/shard_map/all_to_all | solution.py:326
  23.0 0.7 pad_maximum_fusion.1
  23.7 16.1 %all_to_all.26 = f32[16,16,128]{2,1,0:T(8,128)S(1)} all-to-all(f32[16,16,128]{2,1,0:T(8,128)S(1)} %broadcast_in_dim.6), channel_id=1, replica_groups=mesh['gx'=16,'gy'=8,'gz'=2] {'gy','gz'}, dimensions={0} | all-to-all | bytes 262144 | tf_op jit(solution)/shard_map/all_to_all | solution.py:326
  39.9 0.7 broadcast_in_dim.7
  40.6 3.5 %all-to-all-start.2 = ((f32[16,24,128]{2,1,0:T(8,128)}), f32[16,24,128]{2,1,0:T(8,128)S(1)}, u32[]{:S(2)}, u32[]{:S(2)}) async-start(f32[16,24,128]{2,1,0:T(8,128)} %broadcast_in_dim.7), calls=%async_computation.2 | async-start | bytes 393216 | tf_op jit(solution)/shard_map/all_to_all | solution.py:326
  44.1 0.6 pad_add_fusion.idx_ref
  44.7 6.9 %all-to-all-done.2.r_ref = f32[16,24,128]{2,1,0:T(8,128)S(1)} async-done(((f32[16,24,128]{2,1,0:T(8,128)}), f32[16,24,128]{2,1,0:T(8,128)S(1)}, u32[]{:S(2)}, u32[]{:S(2)}) %all-to-all-start.2) | async-done | bytes 196640 | tf_op jit(solution)/shard_map/all_to_all | solution.py:326
  51.6 0.0 copy-start.1
  51.6 0.7 copy-done.1
  52.2 7.5 %second.1 = (bf16[64,2,8,128]{3,2,1,0:T(8,128)(2,1)}, bf16[64,2,8,128]{3,2,1,0:T(8,128)(2,1)}, f32[80,128]{1,0:T(8,128)}, bf16[128,128]{1,0:T(8,128)(2,1)}) custom-call(s32[3]{0:T(128)} %pad_add_fusion.idx_ref, f32[16,24,128]{2,1,0:T(8,128)} %copy-done.1, bf16[128,384]{1,0:T(8,128)(2,1)} %w_ref.1, bf16[8,8,16,1024]{3,2,1,0:T(8,128)(2,1)} %get-tuple-element.14.vt_ref), custom_call_target="tpu_custom_call" | custom-call | tf_op jit(solution)/shard_map/second/pallas_call | solution.py:210
  59.7 2.2 %collective-permute-start = (bf16[64,2,8,128]{3,2,1,0:T(8,128)(2,1)}, bf16[64,2,8,128]{3,2,1,0:T(8,128)(2,1)S(1)}, u32[]{:S(2)}, u32[]{:S(2)}) collective-permute-start(bf16[64,2,8,128]{3,2,1,0:T(8,128)(2,1)} %get-tuple-element.17), channel_id=1, source_target_pairs={{0,1},{1,0},{2,3},{3,2},{4,5},{5,4},{6,7},{7,6},{8,9},{9,8},{10,11... | collective-permute-start | bytes 786440 | tf_op jit(solution)/shard_map/ppermute | solution.py:349
  61.9 1.4 %collective-permute-done = bf16[64,2,8,128]{3,2,1,0:T(8,128)(2,1)S(1)} collective-permute-done((bf16[64,2,8,128]{3,2,1,0:T(8,128)(2,1)}, bf16[64,2,8,128]{3,2,1,0:T(8,128)(2,1)S(1)}, u32[]{:S(2)}, u32[]{:S(2)}) %collective-permute-start) | collective-permute-done | bytes 262176 | tf_op jit(solution)/shard_map/ppermute | solution.py:349
  63.3 1.0 add_convert_fusion
  64.3 19.7 %all_to_all.27 = bf16[128,8,128]{2,1,0:T(8,128)(2,1)} all-to-all(bf16[128,8,128]{2,1,0:T(8,128)(2,1)S(1)} %bitcast.10), channel_id=1, replica_groups=mesh['gx'=16,'gy'=8,'gz'=2] {'gx','gy'}, dimensions={0} | all-to-all | bytes 524288 | tf_op jit(solution)/shard_map/all_to_all | solution.py:326
  84.0 1.8 %middle.1 = bf16[16,8,8,128]{3,2,1,0:T(8,128)(2,1)} custom-call(bf16[16,8,8,128]{3,2,1,0:T(8,128)(2,1)} %bitcast.11, bf16[128,128]{1,0:T(8,128)(2,1)} %get-tuple-element.18.kx_ref), custom_call_target="tpu_custom_call" | custom-call | tf_op jit(solution)/shard_map/middle/pallas_call | solution.py:254
  85.9 19.4 %all_to_all.28 = bf16[128,8,128]{2,1,0:T(8,128)(2,1)S(1)} all-to-all(bf16[128,8,128]{2,1,0:T(8,128)(2,1)} %bitcast.12), channel_id=1, replica_groups=mesh['gx'=16,'gy'=8,'gz'=2] {'gx','gy'}, dimensions={0} | all-to-all | bytes 524288 | tf_op jit(solution)/shard_map/all_to_all | solution.py:326
  105.3 0.0 copy-start
  105.3 3.5 %collective-permute-start.1 = (bf16[64,2,8,128]{3,2,1,0:T(8,128)(2,1)S(1)}, bf16[64,2,8,128]{3,2,1,0:T(8,128)(2,1)S(1)}, u32[]{:S(2)}, u32[]{:S(2)}) collective-permute-start(bf16[64,2,8,128]{3,2,1,0:T(8,128)(2,1)S(1)} %bitcast.13), channel_id=1, source_target_pairs={{0,1},{1,0},{2,3},{3,2},{4,5},{5,4},{6,7},{7,6},{8,9},{9,8},{10,11... | collective-permute-start | bytes 786440 | tf_op jit(solution)/shard_map/ppermute | solution.py:354
  108.8 1.2 collective-permute-done.1.other_ref
  110.0 0.0 copy-start.2
  110.0 0.0 copy-done
  110.0 0.7 copy-done.2
  110.7 18.2 %third.1 = bf16[8,16,64,128]{3,2,1,0:T(8,128)(2,1)} custom-call(s32[3]{0:T(128)} %pad_add_fusion.idx_ref, f32[80,128]{1,0:T(8,128)} %get-tuple-element.15.q_ref, bf16[64,2,8,128]{3,2,1,0:T(8,128)(2,1)} %bitcast.14, bf16[64,2,8,128]{3,2,1,0:T(8,128)(2,1)} %copy-done.2, bf16[8,16,64,128]{3,2,1,0:T(8,128)(2,1)} %tok_ref.3, bf16[128,128]{1,0:T(8,128)(2,1)} %wo_ref.1, ...), custom_call_target="tpu_custom_call" | custom-call | tf_op jit(solution)/shard_map/third/pallas_call | solution.py:303
  (6 shorter events, 0.1 us)
Async XLA Ops:
  40.6 11.0 %all-to-all-start.2 = ((f32[16,24,128]{2,1,0:T(8,128)}), f32[16,24,128]{2,1,0:T(8,128)S(1)}, u32[]{:S(2)}, u32[]{:S(2)}) async-start(f32[16,24,128]{2,1,0:T(8,128)} %broadcast_in_dim.7), calls=%async_computation.2 | async-start | bytes 393216 | tf_op jit(solution)/shard_map/all_to_all | solution.py:326
  51.6 0.7 copy-start.1
  59.7 3.6 %collective-permute-start = (bf16[64,2,8,128]{3,2,1,0:T(8,128)(2,1)}, bf16[64,2,8,128]{3,2,1,0:T(8,128)(2,1)S(1)}, u32[]{:S(2)}, u32[]{:S(2)}) collective-permute-start(bf16[64,2,8,128]{3,2,1,0:T(8,128)(2,1)} %get-tuple-element.17), channel_id=1, source_target_pairs={{0,1},{1,0},{2,3},{3,2},{4,5},{5,4},{6,7},{7,6},{8,9},{9,8},{10,11... | collective-permute-start | bytes 786440 | tf_op jit(solution)/shard_map/ppermute | solution.py:349
  105.3 4.7 %copy-start = (bf16[128,8,128]{2,1,0:T(8,128)(2,1)}, bf16[128,8,128]{2,1,0:T(8,128)(2,1)S(1)}, u32[]{:S(2)}) copy-start(bf16[128,8,128]{2,1,0:T(8,128)(2,1)S(1)} %all_to_all.28) | copy-start | bytes 786436
  105.3 4.7 %collective-permute-start.1 = (bf16[64,2,8,128]{3,2,1,0:T(8,128)(2,1)S(1)}, bf16[64,2,8,128]{3,2,1,0:T(8,128)(2,1)S(1)}, u32[]{:S(2)}, u32[]{:S(2)}) collective-permute-start(bf16[64,2,8,128]{3,2,1,0:T(8,128)(2,1)S(1)} %bitcast.13), channel_id=1, source_target_pairs={{0,1},{1,0},{2,3},{3,2},{4,5},{5,4},{6,7},{7,6},{8,9},{9,8},{10,11... | collective-permute-start | bytes 786440 | tf_op jit(solution)/shard_map/ppermute | solution.py:354
  110.0 0.7 copy-start.2

commit v3 on v2

--- a/solution.py
+++ b/solution.py
@@ -48,62 +48,112 @@
     return jnp.where(cond, 1.0, 0.0).astype(BF)
 
 
-def first_kernel(tok_ref, wv_ref, vt_ref, pool_ref, sx_ref, sy_acc, sz_acc):
+def first_kernel(tok_ref, normed_ref, xy_ref, sz_ref, sx_acc, sy_acc, sz_acc):
     step = pl.program_id(0)
     nb, ny, nz, _ = tok_ref.shape
+    nx = xy_ref.shape[0] - ny
     x = tok_ref[...].reshape(nb * ny * nz, C).astype(F32)
     normed = norm_rows(x).astype(BF)
-    wvt = wv_ref[...].T
+    normed_ref[...] = normed.reshape(nb, ny * nz, C)
     n32 = normed.astype(F32).reshape(nb, ny, nz, C)
     sxy = jnp.sum(n32, axis=2)
-    sy = jnp.sum(sxy, axis=0)
-    sz = jnp.sum(jnp.sum(n32, axis=0), axis=0)
-    sx_ref[0] = jnp.sum(sxy, axis=1)
-    for i in range(nb):
-        vt = dot(wvt, normed[i * ny * nz : (i + 1) * ny * nz], NT).astype(BF)
-        vt_ref[:, i, :, :] = vt.reshape(HEADS, HD, ny * nz)
+    sx_acc[step] = jnp.sum(sxy, axis=1)
 
     @pl.when(step == 0)
     def _():
         sy_acc[...] = jnp.zeros_like(sy_acc)
         sz_acc[...] = jnp.zeros_like(sz_acc)
 
-    sy_acc[...] += sy
-    sz_acc[...] += sz
+    sy_acc[...] += jnp.sum(sxy, axis=0)
+    sz_acc[...] += jnp.sum(jnp.sum(n32, axis=0), axis=0)
 
     @pl.when(step == pl.num_programs(0) - 1)
     def _():
-        parts = pool_ref.shape[0]
-        ry = ny // parts
-        rz = nz // parts
-        pool_ref[...] = jnp.zeros_like(pool_ref)
-        pool_ref[:, 0:ry, :] = sy_acc[...].reshape(parts, ry, C)
-        pool_ref[:, ry : ry + rz, :] = sz_acc[...].reshape(parts, rz, C)
-
-
-def first(tokens, w_qkv, parts, block=4):
+        xy_ref[0:nx, :] = sx_acc[...].reshape(nx, C)
+        xy_ref[nx:, :] = sy_acc[...]
+        sz_ref[...] = sz_acc[...]
+
+
+def first(tokens, block=4):
     nx, ny, nz, _ = tokens.shape
-    rows = -(-(ny // parts + nz // parts) // 8) * 8
     return pl.pallas_call(
         first_kernel,
         grid=(nx // block,),
+        in_specs=[pl.BlockSpec((block, ny, nz, C), lambda i: (i, 0, 0, 0))],
+        out_specs=[
+            pl.BlockSpec((block, ny * nz, C), lambda i: (i, 0, 0)),
+            pl.BlockSpec((nx + ny, C), lambda i: (0, 0)),
+            pl.BlockSpec((nz, C), lambda i: (0, 0)),
+        ],
+        out_shape=[
+            jax.ShapeDtypeStruct((nx, ny * nz, C), BF),
+            jax.ShapeDtypeStruct((nx + ny, C), F32),
+            jax.ShapeDtypeStruct((nz, C), F32),
+        ],
+        scratch_shapes=[
+            pltpu.VMEM((nx // block, block, C), F32),
+            pltpu.VMEM((ny, C), F32),
+            pltpu.VMEM((nz, C), F32),
+        ],
+        name="first",
+    )(tokens)
+
+
+def value_kernel(normed_ref, wv_ref, vt_ref):
+    wvt = wv_ref[...].T
+    nb, count, _ = normed_ref.shape
+    for i in range(nb):
+        vt = dot(wvt, normed_ref[i], NT).astype(BF)
+        vt_ref[:, i, :, :] = vt.reshape(HEADS, HD, count)
+
+
+def value_of(normed, w_qkv, block=4):
+    nx, count, _ = normed.shape
+    return pl.pallas_call(
+        value_kernel,
+        grid=(nx // block,),
         in_specs=[
-            pl.BlockSpec((block, ny, nz, C), lambda i: (i, 0, 0, 0)),
+            pl.BlockSpec((block, count, C), lambda i: (i, 0, 0)),
             pl.BlockSpec((C, C), lambda i: (0, 2)),
         ],
-        out_specs=[
-            pl.BlockSpec((HEADS, block, HD, ny * nz), lambda i: (0, i, 0, 0)),
-            pl.BlockSpec((parts, rows, C), lambda i: (0, 0, 0)),
-            pl.BlockSpec((1, block, C), lambda i: (i, 0, 0)),
-        ],
-        out_shape=[
-            jax.ShapeDtypeStruct((HEADS, nx, HD, ny * nz), BF),
-            jax.ShapeDtypeStruct((parts, rows, C), F32),
-            jax.ShapeDtypeStruct((nx // block, block, C), F32),
-        ],
-        scratch_shapes=[pltpu.VMEM((ny, C), F32), pltpu.VMEM((nz, C), F32)],
-        name="first",
-    )(tokens, w_qkv)
+        out_specs=pl.BlockSpec((HEADS, block, HD, count), lambda i: (0, i, 0, 0)),
+        out_shape=jax.ShapeDtypeStruct((HEADS, nx, HD, count), BF),
+        name="value",
+    )(normed, w_qkv)
+
+
+def in_vmem(kernel, out_shape, name, *operands):
+    vmem = pl.BlockSpec(memory_space=pltpu.VMEM)
+    return pl.pallas_call(
+        kernel,
+        in_specs=[vmem] * len(operands),
+        out_specs=jax.tree.map(lambda _: vmem, out_shape),
+        out_shape=out_shape,
+        name=name,
+    )(*operands)
+
+
+def pack_y_kernel(xy_ref, got_ref, sz_ref, wide_ref, sy_ref):
+    ny = sy_ref.shape[0]
+    nx = xy_ref.shape[0] - ny
+    both = xy_ref[...] + got_ref[...]
+    sy_ref[...] = both[nx:]
+    for i in range(wide_ref.shape[0]):
+        wide_ref[i, 0:nx, :] = both[:nx]
+        wide_ref[i, nx:, :] = sz_ref[...]
+
+
+def pack_x_kernel(g_ref, sy_ref, wide_ref):
+    ny = sy_ref.shape[0]
+    total = jnp.sum(g_ref[...], axis=0)
+    nx = wide_ref.shape[1] - ny - total.shape[0]
+    nz = total.shape[0] - nx
+    high = total[:nx].astype(BF)
+    low = (total[:nx] - high.astype(F32)).astype(BF)
+    parts = [total[nx:].astype(BF), sy_ref[...].astype(BF), high, low]
+    packed = jnp.concatenate(parts, axis=0)
+    for i in range(wide_ref.shape[0]):
+        wide_ref[i] = packed
 
 
 def lane_expand(rows, head, fine):
@@ -127,58 +177,58 @@
     return ones_where((cx // n == xc % HD) & (cx % n == xc // HD))
 
 
+def square_sums(rows):
+    total = jnp.sum(rows * rows, axis=0, keepdims=True)
+    return [jnp.sum(total[:, at : at + C], axis=1, keepdims=True) for at in (0, C)]
+
+
 def second_kernel(
-    idx_ref, r_ref, w_ref, vt_ref, send_ref, keep_ref, qo_ref, kx_ref, k_scr, *, sizes
+    idx_ref, r_ref, w_ref, vt_ref, send_ref, keep_ref, qo_ref, kx_ref, k_scr, *, sizes, count
 ):
     step = pl.program_id(0)
     nx, ny, nz = sizes
-    px, rows, _ = r_ref.shape
-    gx, gy, gz = idx_ref[0], idx_ref[1], idx_ref[2]
-    ry = ny // px
-    rz = nz // px
-    pz = 2
-    py = (rows - nx - pz * rz) // ry
-    half = HEADS // pz
+    px = r_ref.shape[0]
+    gx, gz = idx_ref[0], idx_ref[2]
+    half = HEADS // 2
 
     @pl.when(step == 0)
     def _():
-        pooled = r_ref[...].reshape(px * rows, C)
-        qk = dot(halves(pooled), twice(w_ref[...])).reshape(px, rows, 2 * C)
-        cuts = (0, nx, nx + py * ry, rows)
-        scaled = []
-        for axis in range(3):
-            part = qk[:, cuts[axis] : cuts[axis + 1], :]
-            length = px * (cuts[axis + 1] - cuts[axis])
-            total = jnp.sum(jnp.sum(part * part, axis=0), axis=0, keepdims=True)
-            mean_q = jnp.sum(total[:, :C], axis=1, keepdims=True) / (length * C)
-            mean_k = jnp.sum(total[:, C:], axis=1, keepdims=True) / (length * C)
-            root = 1.0 / math.sqrt(HD * length)
-            scaled.append((lax.rsqrt(mean_q + 1e-06) * root, lax.rsqrt(mean_k + 1e-06)))
-        all_x = qk[:, 0:nx, :].reshape(px * nx, 2 * C)
+        both = jnp.sum(r_ref[:, 0 : nz + ny, :].astype(F32), axis=0)
+        terms_x = [
+            r_ref[:, at : at + nx, :].reshape(px * nx, C) for at in (nz + ny, nz + ny + nx)
+        ]
+        weight = twice(w_ref[...])
+        all_x = dot(jnp.concatenate(terms_x, axis=1), weight)
+        own = dot(halves(both), weight) * (1.0 / count)
+        length = px * nx
+        sums = square_sums(all_x)
+        query = all_x[:, :C] * lax.rsqrt(sums[0] / (length * C) + 1e-06)
+        query = query * (1.0 / math.sqrt(HD * length))
+        key_part = all_x[:, C:] * lax.rsqrt(sums[1] / (length * C) + 1e-06)
         owned = gz * half + gx // (px // half)
-        query = all_x[:, :C] * scaled[0][0]
-        key_part = all_x[:, C:] * scaled[0][1]
         key_part = jnp.where(iota2(key_part.shape, 1) // HD == owned, key_part, 0.0)
         q_terms, k_terms = halves(query), halves(key_part)
         q_terms = jnp.concatenate([q_terms, q_terms[:, :C]], axis=1)
         k_terms = jnp.concatenate([k_terms[:, :C], k_terms[:, :C], k_terms[:, C:]], axis=1)
         kx_ref[...] = dot(q_terms, k_terms, NT).astype(BF)
-        own_y = jnp.zeros((px, ry, 2 * C), F32)
-        for g in range(py):
-            at = nx + g * ry
-            own_y = jnp.where(gy == g, qk[:, at : at + ry, :], own_y)
-        own_y = own_y.reshape(ny, 2 * C)
-        own_z = jnp.zeros((px, rz, 2 * C), F32)
-        for g in range(pz):
-            at = nx + py * ry + g * rz
-            own_z = jnp.where(gz == g, qk[:, at : at + rz, :], own_z)
-        own_z = own_z.reshape(nz, 2 * C)
-        at = 0
-        for own, (scale_q, scale_k) in zip((own_y, own_z), scaled[1:]):
-            n = own.shape[0]
-            qo_ref[at : at + n, :] = own[:, :C] * scale_q
-            k_scr[at : at + n, :] = own[:, C:] * scale_k
-            at += n
+        own_z, own_y = own[:nz], own[nz:]
+        qo_ref[0:ny, :] = own_y[:, :C]
+        qo_ref[ny:, :] = own_z[:, :C]
+        k_scr[0:ny, :] = own_y[:, C:]
+        k_scr[ny:, :] = own_z[:, C:]
+        lane = iota2((1, C), 1)
+        row_y = jnp.zeros((1, C), F32)
+        row_z = jnp.zeros((1, C), F32)
+        for i, (of_y, of_z) in enumerate(zip(square_sums(own_y), square_sums(own_z))):
+            for j in range(2):
+                row_y = jnp.where(lane == 2 * i + j, of_y.astype(BF).astype(F32), row_y)
+                at = 4 + 4 * gz + 2 * i + j
+                row_z = jnp.where(lane == at, of_z.astype(BF).astype(F32), row_z)
+                of_y = of_y - of_y.astype(BF).astype(F32)
+                of_z = of_z - of_z.astype(BF).astype(F32)
+        for ref, row in ((send_ref, row_z), (keep_ref, row_y + row_z)):
+            row = jnp.broadcast_to(row.astype(BF).reshape(1, 1, 1, C), ref.shape[:2] + (nx, C))
+            ref[:, :, nx:, :] = row
 
     ky = k_scr[0:ny, :]
     kz = k_scr[ny : ny + nz, :]
@@ -192,7 +242,7 @@
             narrow = dot(perm, narrow).astype(BF).reshape(HD, nx, HD * HD)
             for side in range(2):
                 cut = narrow[:, :, side * C : (side + 1) * C]
-                out_ref[j * HD : (j + 1) * HD, side] = cut
+                out_ref[j * HD : (j + 1) * HD, side, 0:nx, :] = cut
 
     @pl.when(step == 0)
     def _():
@@ -203,12 +253,12 @@
         contract(keep_ref)
 
 
-def second(idx, pooled, w_qkv, vt, sizes):
+def second(idx, pooled, w_qkv, vt, sizes, count):
     nx, ny, nz = sizes
     half = HEADS // 2
-    core = (half * HD, 2, nx, C)
+    core = (half * HD, 2, 2 * nx, C)
     return pl.pallas_call(
-        functools.partial(second_kernel, sizes=sizes),
+        functools.partial(second_kernel, sizes=sizes, count=count),
         grid_spec=pltpu.PrefetchScalarGridSpec(
             num_scalar_prefetch=1,
             grid=(2,),
@@ -238,26 +288,28 @@
     )(idx, pooled, w_qkv, vt)
 
 
-def middle_kernel(g_ref, kx_ref, out_ref):
-    px, py, nx, _ = g_ref.shape
-    lines = jnp.sum(g_ref[...].astype(F32), axis=1).reshape(px * nx, C)
+def middle_kernel(g_ref, kx_ref, out_ref, *, count, lengths):
+    px, py, rows, _ = g_ref.shape
+    nx = rows // 2
+    marks = g_ref[0, :, nx, :].astype(F32)
+    lane = iota2((1, C), 1)
+    factor = jnp.full((1, 1), 1.0 / (HD * math.sqrt(lengths[0] * lengths[1])), F32)
+    for axis, row in enumerate((jnp.sum(marks, axis=0, keepdims=True), marks[0:1])):
+        for i in range(2):
+            if axis == 0:
+                mask = lane // 2 == i
+            else:
+                mask = (lane // 4 >= 1) & (lane // 4 <= 2) & (lane % 4 // 2 == i)
+            total = jnp.sum(jnp.where(mask, row, 0.0), axis=1, keepdims=True)
+            mean = total * (float(count) * count / (lengths[axis] * C))
+            factor = factor * (lax.rsqrt(mean + 1e-06) * count)
+    lines = jnp.sum(g_ref[:, :, 0:nx, :].astype(F32), axis=1).reshape(px * nx, C) * factor
     high = lines.astype(BF)
     low = (lines - high.astype(F32)).astype(BF)
     kx = kx_ref[...]
     mixed = dot(jnp.concatenate([kx, kx], axis=1), jnp.concatenate([high, low], axis=0))
     mixed = mixed.astype(BF).reshape(px, 1, nx, C)
     out_ref[...] = jnp.broadcast_to(mixed, out_ref.shape)
-
-
-def middle(gathered, kx):
-    vmem = pl.BlockSpec(memory_space=pltpu.VMEM)
-    return pl.pallas_call(
-        middle_kernel,
-        in_specs=[vmem, vmem],
-        out_specs=vmem,
-        out_shape=jax.ShapeDtypeStruct(gathered.shape, BF),
-        name="middle",
-    )(gathered, kx)
 
 
 def third_kernel(
@@ -330,27 +382,28 @@
     nx, ny, nz, _ = tokens.shape
     cx, cy, cz = (lax.axis_size(a) for a in ("gx", "gy", "gz"))
     idx = jnp.stack([lax.axis_index(a) for a in ("gx", "gy", "gz")]).astype(jnp.int32)
-    ry = ny // cx
-    rz = nz // cx
-    vt, pool, sum_x = first(tokens, w_qkv, cx)
-    sum_x = sum_x.reshape(nx, C)
-    got = jnp.sum(a2a(pool, "gx"), axis=0)
-    packed = jnp.concatenate([sum_x, got], axis=0)
-    wide = jnp.broadcast_to(packed, (cy * cz,) + packed.shape)
-    wide = a2a(wide, ("gy", "gz")).reshape(cy, cz, *packed.shape)
-    total_x = jnp.sum(wide[:, :, :nx], axis=(0, 1))
-    total_y = jnp.sum(wide[:, :, nx : nx + ry], axis=1).reshape(cy * ry, C)
-    total_z = jnp.sum(wide[:, :, nx + ry : nx + ry + rz], axis=0).reshape(cz * rz, C)
-    packed = jnp.concatenate([total_x, total_y, total_z], axis=0)
-    pooled = a2a(jnp.broadcast_to(packed, (cx,) + packed.shape), "gx")
-
-    send, keep, q, kx = second(idx, pooled, w_qkv, vt, (nx, ny, nz))
+    line = nx * cx
     swap = [(0, 1), (1, 0)]
+    f32 = lambda *shape: jax.ShapeDtypeStruct(shape, F32)
+    bf16 = lambda *shape: jax.ShapeDtypeStruct(shape, BF)
+
+    normed, xy, sum_z = first(tokens)
+    got = lax.ppermute(xy, "gz", swap)
+    wide, sum_y = in_vmem(
+        pack_y_kernel, (f32(cy, nx + nz, C), f32(ny, C)), "pack_y", xy, got, sum_z
+    )
+    wide = a2a(wide, "gy")
+    vt = value_of(normed, w_qkv)
+    wide = in_vmem(pack_x_kernel, bf16(cx, nz + ny + 2 * nx, C), "pack_x", wide, sum_y)
+    pooled = a2a(wide, "gx")
+
+    send, keep, q, kx = second(idx, pooled, w_qkv, vt, (nx, ny, nz), line * line)
     part = keep.astype(F32) + lax.ppermute(send, "gz", swap).astype(F32)
-    part = part.astype(BF).reshape(cx * cy, nx, C)
-    gathered = a2a(part, ("gx", "gy")).reshape(cx, cy, nx, C)
-    spread = middle(gathered, kx).reshape(cx * cy, nx, C)
-    mine = a2a(spread, ("gx", "gy")).reshape(keep.shape)
+    part = part.astype(BF).reshape(cx * cy, 2 * nx, C)
+    gathered = a2a(part, ("gx", "gy")).reshape(cx, cy, 2 * nx, C)
+    kernel = functools.partial(middle_kernel, count=line * line, lengths=(ny * cy, nz * cz))
+    spread = in_vmem(kernel, bf16(cx, cy, nx, C), "middle", gathered, kx)
+    mine = a2a(spread.reshape(cx * cy, nx, C), ("gx", "gy")).reshape(-1, 2, nx, C)
     other = lax.ppermute(mine, "gz", swap)
     return third(idx, q, mine, other, tokens, w_out, w_gate_up, w_down)
 

time: 129 us -> 132 us (1.023)
  blocking collectives: 72.7 us -> 59 us
  starting transfers between devices: 9.23 us -> 17.7 us
  Pallas kernels: 33.1 us -> 39.4 us
  waiting for transfers between devices: 9.39 us -> 11.1 us
    all_to_all x4 -> x3, blocking collectives: 72.7 us -> 59 us  [a2a(): return lax.all_to_all(values, axes, 0, 0, tiled=True)]
    pallas_call x2 -> x5, Pallas kernels: 9.35 us -> 16.1 us  [the longest x1 7.67 us: second(): pl.pallas_call(functools.partial(second_kernel, sizes=sizes, count=count)...]
    all_to_all x1, starting transfers between devices: 3.52 us -> 8.4 us  [a2a(): return lax.all_to_all(values, axes, 0, 0, tiled=True)]
    ppermute x0 -> x1, starting transfers between devices: none -> 3.2 us  [body(): got = lax.ppermute(xy, 'gz', swap)]
  transfers between devices with their start and end apart: 3 -> 4, of which waited for: 3 -> 4; matrix products, arithmetic and copies ran while one was open for 0% -> 0% of each run, Pallas kernels for 0% -> 2%
where the time goes in v3:
time: 132 us; the launch traced here: 131 us
  blocking collectives  59 us (45%)
  Pallas kernels  39.4 us (30%)
  starting transfers between devices  17.7 us (13%)
  waiting for transfers between devices  11.1 us (8%)
  local copies, waits for them, and re-layouts  2.06 us (2%)
  other arithmetic  1.79 us (1%)
    all_to_all x3, blocking collectives, a2a(): return lax.all_to_all(values, axes, 0, 0, tiled=True)  59 us
    pallas_call x1, Pallas kernels, third(): pl.pallas_call(third_kernel, grid_spec=pltpu.PrefetchScalarGridSpec(num_s...  18.2 us
    all_to_all x1, starting transfers between devices, a2a(): return lax.all_to_all(values, axes, 0, 0, tiled=True)  8.4 us
    pallas_call x1, Pallas kernels, second(): pl.pallas_call(functools.partial(second_kernel, sizes=sizes, count=count)...  7.67 us
    all_to_all x1, waiting for transfers between devices, a2a(): return lax.all_to_all(values, axes, 0, 0, tiled=True)  7.13 us
    pallas_call x3, Pallas kernels, in_vmem(): pl.pallas_call(kernel, in_specs=[vmem] * len(operands), out_specs=jax.tre...  5.29 us
    pallas_call x1, Pallas kernels, first(): pl.pallas_call(first_kernel, grid=(nx // block,), in_specs=[pl.BlockSpec(...  5.08 us
    ppermute x1, starting transfers between devices, body(): other = lax.ppermute(mine, 'gz', swap)  3.49 us
  transfers between devices with their start and end apart: 4, of which 4 were waited for; matrix products, arithmetic and copies ran while one was open for 0% of the time, Pallas kernels for 2%

profile of v3, /device:TPU:1, one launch (start us, length us, event | category | flops | bytes accessed | tf_op | source)
XLA Modules:
  0.0 131.1 jit_solution(2943528991278404691)
XLA Ops:
  0.0 5.1 %first.1 = (bf16[8,1024,128]{2,1,0:T(8,128)(2,1)}, f32[24,128]{1,0:T(8,128)}, f32[64,128]{1,0:T(8,128)}) custom-call(bf16[8,16,64,128]{3,2,1,0:T(8,128)(2,1)} %tok_ref.3), custom_call_target="tpu_custom_call" | custom-call | tf_op jit(solution)/shard_map/first/pallas_call | solution.py:79
  5.1 3.2 %collective-permute-start = (f32[24,128]{1,0:T(8,128)}, f32[24,128]{1,0:T(8,128)S(1)}, u32[]{:S(2)}, u32[]{:S(2)}) collective-permute-start(f32[24,128]{1,0:T(8,128)} %get-tuple-element.14.xy_ref), channel_id=1, source_target_pairs={{0,1},{1,0},{2,3},{3,2},{4,5},{5,4},{6,7},{7,6},{8,9},{9,8},{10,11... | collective-permute-start | bytes 36872 | tf_op jit(solution)/shard_map/ppermute | solution.py:391
  8.3 1.0 collective-permute-done.got_ref
  9.3 0.0 copy-start.3
  9.3 0.6 copy-done.3
  9.9 1.5 %pack_y.1 = (f32[8,72,128]{2,1,0:T(8,128)}, f32[16,128]{1,0:T(8,128)}) custom-call(f32[24,128]{1,0:T(8,128)} %get-tuple-element.14.xy_ref, f32[24,128]{1,0:T(8,128)} %copy-done.3, f32[64,128]{1,0:T(8,128)} %get-tuple-element.15.sz_ref), custom_call_target="tpu_custom_call" | custom-call | tf_op jit(solution)/shard_map/pack_y/pallas_call | solution.py:127
  11.4 14.3 %all_to_all.20.g_ref = f32[8,72,128]{2,1,0:T(8,128)} all-to-all(f32[8,72,128]{2,1,0:T(8,128)} %get-tuple-element.16), channel_id=1, replica_groups=mesh['gx'=16,'gy'=8,'gz'=2] {'gy'}, dimensions={0} | all-to-all | bytes 589824 | tf_op jit(solution)/shard_map/all_to_all | solution.py:378
  25.7 1.8 %pack_x.1 = bf16[16,96,128]{2,1,0:T(8,128)(2,1)} custom-call(f32[8,72,128]{2,1,0:T(8,128)} %all_to_all.20.g_ref, f32[16,128]{1,0:T(8,128)} %get-tuple-element.17.sy_ref), custom_call_target="tpu_custom_call" | custom-call | tf_op jit(solution)/shard_map/pack_x/pallas_call | solution.py:127
  27.4 8.4 %all-to-all-start.1 = ((bf16[16,96,128]{2,1,0:T(8,128)(2,1)}), bf16[16,96,128]{2,1,0:T(8,128)(2,1)S(1)}, u32[]{:S(2)}, u32[]{:S(2)}) async-start(bf16[16,96,128]{2,1,0:T(8,128)(2,1)} %pack_x.1), calls=%async_computation.1 | async-start | bytes 786432 | tf_op jit(solution)/shard_map/all_to_all | solution.py:378
  35.9 3.2 %value.1.vt_ref = bf16[8,8,16,1024]{3,2,1,0:T(8,128)(2,1)} custom-call(bf16[8,1024,128]{2,1,0:T(8,128)(2,1)} %get-tuple-element.18.normed_ref, bf16[128,384]{1,0:T(8,128)(2,1)} %w_ref.1), custom_call_target="tpu_custom_call" | custom-call | tf_op jit(solution)/shard_map/value/pallas_call | solution.py:112
  39.1 0.6 pad_add_fusion.idx_ref
  39.7 7.1 %all-to-all-done.1.r_ref = bf16[16,96,128]{2,1,0:T(8,128)(2,1)S(1)} async-done(((bf16[16,96,128]{2,1,0:T(8,128)(2,1)}), bf16[16,96,128]{2,1,0:T(8,128)(2,1)S(1)}, u32[]{:S(2)}, u32[]{:S(2)}) %all-to-all-start.1) | async-done | bytes 393248 | tf_op jit(solution)/shard_map/all_to_all | solution.py:378
  46.8 0.0 copy-start
  46.8 0.8 copy-done
  47.6 7.7 %second.1 = (bf16[64,2,16,128]{3,2,1,0:T(8,128)(2,1)}, bf16[64,2,16,128]{3,2,1,0:T(8,128)(2,1)}, f32[80,128]{1,0:T(8,128)}, bf16[128,128]{1,0:T(8,128)(2,1)}) custom-call(s32[3]{0:T(128)} %pad_add_fusion.idx_ref, bf16[16,96,128]{2,1,0:T(8,128)(2,1)} %copy-done, bf16[128,384]{1,0:T(8,128)(2,1)} %w_ref.1, bf16[8,8,16,1024]{3,2,1,0:T(8,128)(2,1)} %value.1.vt_ref), custom_call_target="tpu_custom_call" | custom-call | tf_op jit(solution)/shard_map/second/pallas_call | solution.py:260
  55.2 2.6 %collective-permute-start.1 = (bf16[64,2,16,128]{3,2,1,0:T(8,128)(2,1)}, bf16[64,2,16,128]{3,2,1,0:T(8,128)(2,1)S(1)}, u32[]{:S(2)}, u32[]{:S(2)}) collective-permute-start(bf16[64,2,16,128]{3,2,1,0:T(8,128)(2,1)} %get-tuple-element.21), channel_id=1, source_target_pairs={{0,1},{1,0},{2,3},{3,2},{4,5},{5,4},{6,7},{7,6},{8,9},{9,8},{10,11... | collective-permute-start | bytes 1572872 | tf_op jit(solution)/shard_map/ppermute | solution.py:401
  57.9 1.7 %collective-permute-done.1 = bf16[64,2,16,128]{3,2,1,0:T(8,128)(2,1)S(1)} collective-permute-done((bf16[64,2,16,128]{3,2,1,0:T(8,128)(2,1)}, bf16[64,2,16,128]{3,2,1,0:T(8,128)(2,1)S(1)}, u32[]{:S(2)}, u32[]{:S(2)}) %collective-permute-start.1) | collective-permute-done | bytes 524320 | tf_op jit(solution)/shard_map/ppermute | solution.py:401
  59.6 1.2 add_convert_fusion
  60.8 25.3 %all_to_all.21 = bf16[128,16,128]{2,1,0:T(8,128)(2,1)} all-to-all(bf16[128,16,128]{2,1,0:T(8,128)(2,1)S(1)} %bitcast.7), channel_id=1, replica_groups=mesh['gx'=16,'gy'=8,'gz'=2] {'gx','gy'}, dimensions={0} | all-to-all | bytes 1048576 | tf_op jit(solution)/shard_map/all_to_all | solution.py:378
  86.1 2.0 %middle.1 = bf16[16,8,8,128]{3,2,1,0:T(8,128)(2,1)} custom-call(bf16[16,8,16,128]{3,2,1,0:T(8,128)(2,1)} %bitcast.8, bf16[128,128]{1,0:T(8,128)(2,1)} %get-tuple-element.22.kx_ref), custom_call_target="tpu_custom_call" | custom-call | tf_op jit(solution)/shard_map/middle/pallas_call | solution.py:127
  88.1 19.4 %all_to_all.22 = bf16[128,8,128]{2,1,0:T(8,128)(2,1)S(1)} all-to-all(bf16[128,8,128]{2,1,0:T(8,128)(2,1)} %bitcast.9), channel_id=1, replica_groups=mesh['gx'=16,'gy'=8,'gz'=2] {'gx','gy'}, dimensions={0} | all-to-all | bytes 524288 | tf_op jit(solution)/shard_map/all_to_all | solution.py:378
  107.5 0.0 copy-start.1
  107.5 3.5 %collective-permute-start.2 = (bf16[64,2,8,128]{3,2,1,0:T(8,128)(2,1)S(1)}, bf16[64,2,8,128]{3,2,1,0:T(8,128)(2,1)S(1)}, u32[]{:S(2)}, u32[]{:S(2)}) collective-permute-start(bf16[64,2,8,128]{3,2,1,0:T(8,128)(2,1)S(1)} %bitcast.10), channel_id=1, source_target_pairs={{0,1},{1,0},{2,3},{3,2},{4,5},{5,4},{6,7},{7,6},{8,9},{9,8},{10,11... | collective-permute-start | bytes 786440 | tf_op jit(solution)/shard_map/ppermute | solution.py:407
  111.0 1.2 collective-permute-done.2.other_ref
  112.2 0.0 copy-start.2
  112.2 0.0 copy-done.1
  112.2 0.7 copy-done.2
  112.9 18.2 %third.1 = bf16[8,16,64,128]{3,2,1,0:T(8,128)(2,1)} custom-call(s32[3]{0:T(128)} %pad_add_fusion.idx_ref, f32[80,128]{1,0:T(8,128)} %get-tuple-element.19.q_ref, bf16[64,2,8,128]{3,2,1,0:T(8,128)(2,1)} %bitcast.11, bf16[64,2,8,128]{3,2,1,0:T(8,128)(2,1)} %copy-done.2, bf16[8,16,64,128]{3,2,1,0:T(8,128)(2,1)} %tok_ref.3, bf16[128,128]{1,0:T(8,128)(2,1)} %wo_ref.1, ...), custom_call_target="tpu_custom_call" | custom-call | tf_op jit(solution)/shard_map/third/pallas_call | solution.py:355
Async XLA Ops:
  5.1 4.2 %collective-permute-start = (f32[24,128]{1,0:T(8,128)}, f32[24,128]{1,0:T(8,128)S(1)}, u32[]{:S(2)}, u32[]{:S(2)}) collective-permute-start(f32[24,128]{1,0:T(8,128)} %get-tuple-element.14.xy_ref), channel_id=1, source_target_pairs={{0,1},{1,0},{2,3},{3,2},{4,5},{5,4},{6,7},{7,6},{8,9},{9,8},{10,11... | collective-permute-start | bytes 36872 | tf_op jit(solution)/shard_map/ppermute | solution.py:391
  9.3 0.6 copy-start.3
  27.4 19.4 %all-to-all-start.1 = ((bf16[16,96,128]{2,1,0:T(8,128)(2,1)}), bf16[16,96,128]{2,1,0:T(8,128)(2,1)S(1)}, u32[]{:S(2)}, u32[]{:S(2)}) async-start(bf16[16,96,128]{2,1,0:T(8,128)(2,1)} %pack_x.1), calls=%async_computation.1 | async-start | bytes 786432 | tf_op jit(solution)/shard_map/all_to_all | solution.py:378
  46.8 0.8 copy-start
  55.2 4.4 %collective-permute-start.1 = (bf16[64,2,16,128]{3,2,1,0:T(8,128)(2,1)}, bf16[64,2,16,128]{3,2,1,0:T(8,128)(2,1)S(1)}, u32[]{:S(2)}, u32[]{:S(2)}) collective-permute-start(bf16[64,2,16,128]{3,2,1,0:T(8,128)(2,1)} %get-tuple-element.21), channel_id=1, source_target_pairs={{0,1},{1,0},{2,3},{3,2},{4,5},{5,4},{6,7},{7,6},{8,9},{9,8},{10,11... | collective-permute-start | bytes 1572872 | tf_op jit(solution)/shard_map/ppermute | solution.py:401
  107.5 4.7 %copy-start.1 = (bf16[128,8,128]{2,1,0:T(8,128)(2,1)}, bf16[128,8,128]{2,1,0:T(8,128)(2,1)S(1)}, u32[]{:S(2)}) copy-start(bf16[128,8,128]{2,1,0:T(8,128)(2,1)S(1)} %all_to_all.22) | copy-start | bytes 786436
  107.5 4.7 %collective-permute-start.2 = (bf16[64,2,8,128]{3,2,1,0:T(8,128)(2,1)S(1)}, bf16[64,2,8,128]{3,2,1,0:T(8,128)(2,1)S(1)}, u32[]{:S(2)}, u32[]{:S(2)}) collective-permute-start(bf16[64,2,8,128]{3,2,1,0:T(8,128)(2,1)S(1)} %bitcast.10), channel_id=1, source_target_pairs={{0,1},{1,0},{2,3},{3,2},{4,5},{5,4},{6,7},{7,6},{8,9},{9,8},{10,11... | collective-permute-start | bytes 786440 | tf_op jit(solution)/shard_map/ppermute | solution.py:407
  112.2 0.7 copy-start.2

commit v4 on v3

--- a/solution.py
+++ b/solution.py
@@ -48,16 +48,19 @@
     return jnp.where(cond, 1.0, 0.0).astype(BF)
 
 
-def first_kernel(tok_ref, normed_ref, xy_ref, sz_ref, sx_acc, sy_acc, sz_acc):
+def first_kernel(tok_ref, wv_ref, vt_ref, xy_ref, sz_ref, sx_acc, sy_acc, sz_acc):
     step = pl.program_id(0)
     nb, ny, nz, _ = tok_ref.shape
     nx = xy_ref.shape[0] - ny
     x = tok_ref[...].reshape(nb * ny * nz, C).astype(F32)
     normed = norm_rows(x).astype(BF)
-    normed_ref[...] = normed.reshape(nb, ny * nz, C)
+    wvt = wv_ref[...].T
     n32 = normed.astype(F32).reshape(nb, ny, nz, C)
     sxy = jnp.sum(n32, axis=2)
     sx_acc[step] = jnp.sum(sxy, axis=1)
+    for i in range(nb):
+        vt = dot(wvt, normed[i * ny * nz : (i + 1) * ny * nz], NT).astype(BF)
+        vt_ref[:, i, :, :] = vt.reshape(HEADS, HD, ny * nz)
 
     @pl.when(step == 0)
     def _():
@@ -74,19 +77,22 @@
         sz_ref[...] = sz_acc[...]
 
 
-def first(tokens, block=4):
+def first(tokens, w_qkv, block=4):
     nx, ny, nz, _ = tokens.shape
     return pl.pallas_call(
         first_kernel,
         grid=(nx // block,),
-        in_specs=[pl.BlockSpec((block, ny, nz, C), lambda i: (i, 0, 0, 0))],
+        in_specs=[
+            pl.BlockSpec((block, ny, nz, C), lambda i: (i, 0, 0, 0)),
+            pl.BlockSpec((C, C), lambda i: (0, 2)),
+        ],
         out_specs=[
-            pl.BlockSpec((block, ny * nz, C), lambda i: (i, 0, 0)),
+            pl.BlockSpec((HEADS, block, HD, ny * nz), lambda i: (0, i, 0, 0)),
             pl.BlockSpec((nx + ny, C), lambda i: (0, 0)),
             pl.BlockSpec((nz, C), lambda i: (0, 0)),
         ],
         out_shape=[
-            jax.ShapeDtypeStruct((nx, ny * nz, C), BF),
+            jax.ShapeDtypeStruct((HEADS, nx, HD, ny * nz), BF),
             jax.ShapeDtypeStruct((nx + ny, C), F32),
             jax.ShapeDtypeStruct((nz, C), F32),
         ],
@@ -96,62 +102,30 @@
             pltpu.VMEM((nz, C), F32),
         ],
         name="first",
-    )(tokens)
-
-
-def value_kernel(normed_ref, wv_ref, vt_ref):
-    wvt = wv_ref[...].T
-    nb, count, _ = normed_ref.shape
-    for i in range(nb):
-        vt = dot(wvt, normed_ref[i], NT).astype(BF)
-        vt_ref[:, i, :, :] = vt.reshape(HEADS, HD, count)
-
-
-def value_of(normed, w_qkv, block=4):
-    nx, count, _ = normed.shape
-    return pl.pallas_call(
-        value_kernel,
-        grid=(nx // block,),
-        in_specs=[
-            pl.BlockSpec((block, count, C), lambda i: (i, 0, 0)),
-            pl.BlockSpec((C, C), lambda i: (0, 2)),
-        ],
-        out_specs=pl.BlockSpec((HEADS, block, HD, count), lambda i: (0, i, 0, 0)),
-        out_shape=jax.ShapeDtypeStruct((HEADS, nx, HD, count), BF),
-        name="value",
-    )(normed, w_qkv)
+    )(tokens, w_qkv)
 
 
 def in_vmem(kernel, out_shape, name, *operands):
-    vmem = pl.BlockSpec(memory_space=pltpu.VMEM)
+    spaces = [pltpu.SMEM if o.dtype == jnp.int32 else pltpu.VMEM for o in operands]
     return pl.pallas_call(
         kernel,
-        in_specs=[vmem] * len(operands),
-        out_specs=jax.tree.map(lambda _: vmem, out_shape),
+        in_specs=[pl.BlockSpec(memory_space=space) for space in spaces],
+        out_specs=pl.BlockSpec(memory_space=pltpu.VMEM),
         out_shape=out_shape,
         name=name,
     )(*operands)
 
 
-def pack_y_kernel(xy_ref, got_ref, sz_ref, wide_ref, sy_ref):
-    ny = sy_ref.shape[0]
-    nx = xy_ref.shape[0] - ny
-    both = xy_ref[...] + got_ref[...]
-    sy_ref[...] = both[nx:]
-    for i in range(wide_ref.shape[0]):
-        wide_ref[i, 0:nx, :] = both[:nx]
-        wide_ref[i, nx:, :] = sz_ref[...]
-
-
-def pack_x_kernel(g_ref, sy_ref, wide_ref):
-    ny = sy_ref.shape[0]
-    total = jnp.sum(g_ref[...], axis=0)
-    nx = wide_ref.shape[1] - ny - total.shape[0]
-    nz = total.shape[0] - nx
-    high = total[:nx].astype(BF)
-    low = (total[:nx] - high.astype(F32)).astype(BF)
-    parts = [total[nx:].astype(BF), sy_ref[...].astype(BF), high, low]
-    packed = jnp.concatenate(parts, axis=0)
+def pack_kernel(idx_ref, g_ref, xy_ref, wide_ref, *, nx, cores):
+    ny = xy_ref.shape[0] - nx
+    count = g_ref.shape[0] // cores
+    sum_x = jnp.sum(g_ref[:, 0:nx, :], axis=0)
+    sum_z = jnp.sum(g_ref[:, nx + ny :, :], axis=0)
+    some_y = g_ref[pl.ds(idx_ref[2] * count, count), nx : nx + ny, :]
+    high = sum_x.astype(BF)
+    low = (sum_x - high.astype(F32)).astype(BF)
+    parts = [sum_z, xy_ref[nx:, :], some_y.reshape(count * ny, C)]
+    packed = jnp.concatenate([p.astype(BF) for p in parts] + [high, low], axis=0)
     for i in range(wide_ref.shape[0]):
         wide_ref[i] = packed
 
@@ -183,19 +157,31 @@
 
 
 def second_kernel(
-    idx_ref, r_ref, w_ref, vt_ref, send_ref, keep_ref, qo_ref, kx_ref, k_scr, *, sizes, count
+    idx_ref,
+    r_ref,
+    w_ref,
+    vt_ref,
+    send_ref,
+    keep_ref,
+    qo_ref,
+    kx_ref,
+    mark_ref,
+    k_scr,
+    *,
+    sizes,
+    count
 ):
     step = pl.program_id(0)
     nx, ny, nz = sizes
-    px = r_ref.shape[0]
+    px, rows, _ = r_ref.shape
     gx, gz = idx_ref[0], idx_ref[2]
     half = HEADS // 2
 
     @pl.when(step == 0)
     def _():
-        both = jnp.sum(r_ref[:, 0 : nz + ny, :].astype(F32), axis=0)
+        both = jnp.sum(r_ref[:, 0 : rows - 2 * nx, :].astype(F32), axis=0)
         terms_x = [
-            r_ref[:, at : at + nx, :].reshape(px * nx, C) for at in (nz + ny, nz + ny + nx)
+            r_ref[:, at : at + nx, :].reshape(px * nx, C) for at in (rows - 2 * nx, rows - nx)
         ]
         weight = twice(w_ref[...])
         all_x = dot(jnp.concatenate(terms_x, axis=1), weight)
@@ -211,24 +197,16 @@
         q_terms = jnp.concatenate([q_terms, q_terms[:, :C]], axis=1)
         k_terms = jnp.concatenate([k_terms[:, :C], k_terms[:, :C], k_terms[:, C:]], axis=1)
         kx_ref[...] = dot(q_terms, k_terms, NT).astype(BF)
-        own_z, own_y = own[:nz], own[nz:]
+        own_z, own_y, some_y = own[:nz], own[nz : nz + ny], own[nz + ny :]
         qo_ref[0:ny, :] = own_y[:, :C]
         qo_ref[ny:, :] = own_z[:, :C]
         k_scr[0:ny, :] = own_y[:, C:]
         k_scr[ny:, :] = own_z[:, C:]
-        lane = iota2((1, C), 1)
-        row_y = jnp.zeros((1, C), F32)
-        row_z = jnp.zeros((1, C), F32)
-        for i, (of_y, of_z) in enumerate(zip(square_sums(own_y), square_sums(own_z))):
-            for j in range(2):
-                row_y = jnp.where(lane == 2 * i + j, of_y.astype(BF).astype(F32), row_y)
-                at = 4 + 4 * gz + 2 * i + j
-                row_z = jnp.where(lane == at, of_z.astype(BF).astype(F32), row_z)
-                of_y = of_y - of_y.astype(BF).astype(F32)
-                of_z = of_z - of_z.astype(BF).astype(F32)
-        for ref, row in ((send_ref, row_z), (keep_ref, row_y + row_z)):
-            row = jnp.broadcast_to(row.astype(BF).reshape(1, 1, 1, C), ref.shape[:2] + (nx, C))
-            ref[:, :, nx:, :] = row
+        lane = iota2(mark_ref.shape, 1)
+        marks = jnp.zeros(mark_ref.shape, F32)
+        for i, total in enumerate(square_sums(some_y) + square_sums(own_z)):
+            marks = jnp.where(lane == i, total, marks)
+        mark_ref[...] = marks
 
     ky = k_scr[0:ny, :]
     kz = k_scr[ny : ny + nz, :]
@@ -242,7 +220,7 @@
             narrow = dot(perm, narrow).astype(BF).reshape(HD, nx, HD * HD)
             for side in range(2):
                 cut = narrow[:, :, side * C : (side + 1) * C]
-                out_ref[j * HD : (j + 1) * HD, side, 0:nx, :] = cut
+                out_ref[j * HD : (j + 1) * HD, side] = cut
 
     @pl.when(step == 0)
     def _():
@@ -256,7 +234,7 @@
 def second(idx, pooled, w_qkv, vt, sizes, count):
     nx, ny, nz = sizes
     half = HEADS // 2
-    core = (half * HD, 2, 2 * nx, C)
+    core = (half * HD, 2, nx, C)
     return pl.pallas_call(
         functools.partial(second_kernel, sizes=sizes, count=count),
         grid_spec=pltpu.PrefetchScalarGridSpec(
@@ -275,6 +253,7 @@
                 pl.BlockSpec(core, lambda i, s: (0, 0, 0, 0)),
                 pl.BlockSpec((ny + nz, C), lambda i, s: (0, 0)),
                 pl.BlockSpec((C, C), lambda i, s: (0, 0)),
+                pl.BlockSpec((8, C), lambda i, s: (0, 0)),
             ],
             scratch_shapes=[pltpu.VMEM((ny + nz, C), F32)],
         ),
@@ -283,27 +262,22 @@
             jax.ShapeDtypeStruct(core, BF),
             jax.ShapeDtypeStruct((ny + nz, C), F32),
             jax.ShapeDtypeStruct((C, C), BF),
+            jax.ShapeDtypeStruct((8, C), F32),
         ],
         name="second",
     )(idx, pooled, w_qkv, vt)
 
 
-def middle_kernel(g_ref, kx_ref, out_ref, *, count, lengths):
-    px, py, rows, _ = g_ref.shape
-    nx = rows // 2
-    marks = g_ref[0, :, nx, :].astype(F32)
+def middle_kernel(g_ref, kx_ref, mark_ref, mark2_ref, out_ref, *, count, lengths):
+    px, py, nx, _ = g_ref.shape
+    marks = mark_ref[0:1, :] + mark2_ref[0:1, :]
     lane = iota2((1, C), 1)
     factor = jnp.full((1, 1), 1.0 / (HD * math.sqrt(lengths[0] * lengths[1])), F32)
-    for axis, row in enumerate((jnp.sum(marks, axis=0, keepdims=True), marks[0:1])):
-        for i in range(2):
-            if axis == 0:
-                mask = lane // 2 == i
-            else:
-                mask = (lane // 4 >= 1) & (lane // 4 <= 2) & (lane % 4 // 2 == i)
-            total = jnp.sum(jnp.where(mask, row, 0.0), axis=1, keepdims=True)
-            mean = total * (float(count) * count / (lengths[axis] * C))
-            factor = factor * (lax.rsqrt(mean + 1e-06) * count)
-    lines = jnp.sum(g_ref[:, :, 0:nx, :].astype(F32), axis=1).reshape(px * nx, C) * factor
+    for i in range(4):
+        total = jnp.sum(jnp.where(lane == i, marks, 0.0), axis=1, keepdims=True)
+        mean = total * (float(count) * count / (lengths[i // 2] * C))
+        factor = factor * (lax.rsqrt(mean + 1e-06) * count)
+    lines = jnp.sum(g_ref[...].astype(F32), axis=1).reshape(px * nx, C) * factor
     high = lines.astype(BF)
     low = (lines - high.astype(F32)).astype(BF)
     kx = kx_ref[...]
@@ -384,25 +358,24 @@
     idx = jnp.stack([lax.axis_index(a) for a in ("gx", "gy", "gz")]).astype(jnp.int32)
     line = nx * cx
     swap = [(0, 1), (1, 0)]
-    f32 = lambda *shape: jax.ShapeDtypeStruct(shape, F32)
-    bf16 = lambda *shape: jax.ShapeDtypeStruct(shape, BF)
-
-    normed, xy, sum_z = first(tokens)
-    got = lax.ppermute(xy, "gz", swap)
-    wide, sum_y = in_vmem(
-        pack_y_kernel, (f32(cy, nx + nz, C), f32(ny, C)), "pack_y", xy, got, sum_z
-    )
-    wide = a2a(wide, "gy")
-    vt = value_of(normed, w_qkv)
-    wide = in_vmem(pack_x_kernel, bf16(cx, nz + ny + 2 * nx, C), "pack_x", wide, sum_y)
-    pooled = a2a(wide, "gx")
-
-    send, keep, q, kx = second(idx, pooled, w_qkv, vt, (nx, ny, nz), line * line)
+
+    vt, xy, sum_z = first(tokens, w_qkv)
+    xy = xy + lax.ppermute(xy, "gz", swap)
+    wide, idx = lax.optimization_barrier((jnp.concatenate([xy, sum_z], axis=0), idx))
+    wide = a2a(jnp.broadcast_to(wide, (cy,) + wide.shape), "gy")
+    kernel = functools.partial(pack_kernel, nx=nx, cores=cz)
+    shape = jax.ShapeDtypeStruct((cx, nz + ny + cy // cz * ny + 2 * nx, C), BF)
+    pooled = a2a(in_vmem(kernel, shape, "pack", idx, wide, xy), "gx")
+
+    sizes = (nx, ny, nz)
+    send, keep, q, kx, marks = second(idx, pooled, w_qkv, vt, sizes, line * line)
+    marks2 = lax.ppermute(marks, "gz", swap)
     part = keep.astype(F32) + lax.ppermute(send, "gz", swap).astype(F32)
-    part = part.astype(BF).reshape(cx * cy, 2 * nx, C)
-    gathered = a2a(part, ("gx", "gy")).reshape(cx, cy, 2 * nx, C)
+    part, marks2 = lax.optimization_barrier((part.astype(BF).reshape(cx * cy, nx, C), marks2))
+    gathered = a2a(part, ("gx", "gy")).reshape(cx, cy, nx, C)
     kernel = functools.partial(middle_kernel, count=line * line, lengths=(ny * cy, nz * cz))
-    spread = in_vmem(kernel, bf16(cx, cy, nx, C), "middle", gathered, kx)
+    shape = jax.ShapeDtypeStruct(gathered.shape, BF)
+    spread = in_vmem(kernel, shape, "middle", gathered, kx, marks, marks2)
     mine = a2a(spread.reshape(cx * cy, nx, C), ("gx", "gy")).reshape(-1, 2, nx, C)
     other = lax.ppermute(mine, "gz", swap)
     return third(idx, q, mine, other, tokens, w_out, w_gate_up, w_down)

time: 132 us -> 132 us (level)
  blocking collectives: 59 us -> 78.1 us
  waiting for transfers between devices: 11.1 us -> 2.89 us
  starting transfers between devices: 17.7 us -> 10.9 us
  Pallas kernels: 39.4 us -> 35.3 us
  local copies, waits for them, and re-layouts: 2.06 us -> 0.73 us
    all_to_all x3 -> x4, blocking collectives: 59 us -> 78.1 us  [a2a(): return lax.all_to_all(values, axes, 0, 0, tiled=True)]
    all_to_all x1 -> x0, starting transfers between devices: 8.4 us -> none  [a2a(): return lax.all_to_all(values, axes, 0, 0, tiled=True)]
    all_to_all x1 -> x0, waiting for transfers between devices: 7.13 us -> none  [a2a(): return lax.all_to_all(values, axes, 0, 0, tiled=True)]
    pallas_call x4 -> x2, Pallas kernels: 8.47 us -> 3.83 us  [in_vmem(): pl.pallas_call(kernel, in_specs=[pl.BlockSpec(memory_space=space) for spa...]
    ppermute x1, starting transfers between devices: 2.63 us -> 4.08 us  [body(): part = keep.astype(F32) + lax.ppermute(send, 'gz', swap).astype(F32)]
    unnamed x8, local copies, waits for them, and re-layouts: 2.06 us -> 0.71 us
    ppermute x1 -> x2, starting transfers between devices: 3.2 us -> 3.29 us  [the longest x1 3.2 us: body(): xy = xy + lax.ppermute(xy, 'gz', swap)]
  transfers between devices with their start and end apart: 4 -> 4, of which waited for: 4 -> 3; matrix products, arithmetic and copies ran while one was open for 0% -> 1% of each run, Pallas kernels for 2% -> 0%
where the time goes in v4:
time: 132 us; the launch traced here: 131 us
  blocking collectives  78.1 us (59%)
  Pallas kernels  35.3 us (27%)
  starting transfers between devices  10.9 us (8%)
  other arithmetic  3.1 us (2%)
  waiting for transfers between devices  2.89 us (2%)
    all_to_all x4, blocking collectives, a2a(): return lax.all_to_all(values, axes, 0, 0, tiled=True)  78.1 us
    pallas_call x1, Pallas kernels, third(): pl.pallas_call(third_kernel, grid_spec=pltpu.PrefetchScalarGridSpec(num_s...  18.2 us
    pallas_call x1, Pallas kernels, second(): pl.pallas_call(functools.partial(second_kernel, sizes=sizes, count=count)...  7.66 us
    pallas_call x1, Pallas kernels, first(): pl.pallas_call(first_kernel, grid=(nx // block,), in_specs=[pl.BlockSpec(...  5.6 us
    ppermute x1, starting transfers between devices, body(): part = keep.astype(F32) + lax.ppermute(send, 'gz', swap).astype(F32)  4.08 us
    pallas_call x2, Pallas kernels, in_vmem(): pl.pallas_call(kernel, in_specs=[pl.BlockSpec(memory_space=space) for spa...  3.83 us
    ppermute x1, starting transfers between devices, body(): other = lax.ppermute(mine, 'gz', swap)  3.53 us
    ppermute x1, starting transfers between devices, body(): xy = xy + lax.ppermute(xy, 'gz', swap)  3.2 us
  transfers between devices with their start and end apart: 4, of which 3 were waited for; matrix products, arithmetic and copies ran while one was open for 1% of the time, Pallas kernels for 0%

profile of v4, /device:TPU:1, one launch (start us, length us, event | category | flops | bytes accessed | tf_op | source)
XLA Modules:
  0.0 131.1 jit_solution(3780616770572120807)
XLA Ops:
  0.0 5.6 %first.1 = (bf16[8,8,16,1024]{3,2,1,0:T(8,128)(2,1)}, f32[24,128]{1,0:T(8,128)}, f32[64,128]{1,0:T(8,128)}) custom-call(bf16[8,16,64,128]{3,2,1,0:T(8,128)(2,1)} %tok_ref.3, bf16[128,384]{1,0:T(8,128)(2,1)} %w_ref.1), custom_call_target="tpu_custom_call" | custom-call | tf_op jit(solution)/shard_map/first/pallas_call | solution.py:82
  5.6 3.2 %collective-permute-start = (f32[24,128]{1,0:T(8,128)}, f32[24,128]{1,0:T(8,128)S(1)}, u32[]{:S(2)}, u32[]{:S(2)}) collective-permute-start(f32[24,128]{1,0:T(8,128)} %get-tuple-element.17), channel_id=1, source_target_pairs={{0,1},{1,0},{2,3},{3,2},{4,5},{5,4},{6,7},{7,6},{8,9},{9,8},{10,11... | collective-permute-start | bytes 36872 | tf_op jit(solution)/shard_map/ppermute | solution.py:363
  8.8 0.6 pad_add_fusion.idx_ref
  9.4 0.4 collective-permute-done
  9.9 0.7 add.6.xy_ref
  10.6 0.0 copy-start.2
  10.6 0.8 pad_maximum_fusion
  11.4 14.6 %all_to_all.20.g_ref = f32[8,88,128]{2,1,0:T(8,128)} all-to-all(f32[8,88,128]{2,1,0:T(8,128)S(1)} %broadcast_in_dim.3), channel_id=1, replica_groups=mesh['gx'=16,'gy'=8,'gz'=2] {'gy'}, dimensions={0} | all-to-all | bytes 720896 | tf_op jit(solution)/shard_map/all_to_all | solution.py:352
  25.9 0.0 copy-done.2
  25.9 1.9 %pack.1 = bf16[16,160,128]{2,1,0:T(8,128)(2,1)} custom-call(s32[3]{0:T(128)} %pad_add_fusion.idx_ref, f32[8,88,128]{2,1,0:T(8,128)} %all_to_all.20.g_ref, f32[24,128]{1,0:T(8,128)} %copy-done.2), custom_call_target="tpu_custom_call" | custom-call | tf_op jit(solution)/shard_map/pack/pallas_call | solution.py:110
  27.8 25.2 %all_to_all.21.r_ref = bf16[16,160,128]{2,1,0:T(8,128)(2,1)} all-to-all(bf16[16,160,128]{2,1,0:T(8,128)(2,1)} %pack.1), channel_id=1, replica_groups=mesh['gx'=16,'gy'=8,'gz'=2] {'gx'}, dimensions={0} | all-to-all | bytes 1310720 | tf_op jit(solution)/shard_map/all_to_all | solution.py:352
  53.1 7.7 %second.1 = (bf16[64,2,8,128]{3,2,1,0:T(8,128)(2,1)}, bf16[64,2,8,128]{3,2,1,0:T(8,128)(2,1)}, f32[80,128]{1,0:T(8,128)}, bf16[128,128]{1,0:T(8,128)(2,1)}, f32[8,128]{1,0:T(8,128)}) custom-call(s32[3]{0:T(128)} %pad_add_fusion.idx_ref, bf16[16,160,128]{2,1,0:T(8,128)(2,1)} %all_to_all.21.r_ref, bf16[128,384]{1,0:T(8,128)(2,1)} %w_ref.1, ...), custom_call_target="tpu_custom_call" | custom-call | tf_op jit(solution)/shard_map/second/pallas_call | solution.py:238
  60.7 4.1 %collective-permute-start.1 = (bf16[64,2,8,128]{3,2,1,0:T(8,128)(2,1)}, bf16[64,2,8,128]{3,2,1,0:T(8,128)(2,1)S(1)}, u32[]{:S(2)}, u32[]{:S(2)}) collective-permute-start(bf16[64,2,8,128]{3,2,1,0:T(8,128)(2,1)} %get-tuple-element.24), channel_id=1, source_target_pairs={{0,1},{1,0},{2,3},{3,2},{4,5},{5,4},{6,7},{7,6},{8,9},{9,8},{10,11... | collective-permute-start | bytes 786440 | tf_op jit(solution)/shard_map/ppermute | solution.py:373
  64.8 0.1 collective-permute-start.2
  64.9 1.3 collective-permute-done.1
  66.2 1.0 add_convert_fusion
  67.2 0.0 collective-permute-done.2.mark2_ref
  67.2 0.0 copy-start.3
  67.2 19.0 %all_to_all.22 = bf16[128,8,128]{2,1,0:T(8,128)(2,1)} all-to-all(bf16[128,8,128]{2,1,0:T(8,128)(2,1)S(1)} %bitcast.7), channel_id=1, replica_groups=mesh['gx'=16,'gy'=8,'gz'=2] {'gx','gy'}, dimensions={0} | all-to-all | bytes 524288 | tf_op jit(solution)/shard_map/all_to_all | solution.py:352
  86.2 0.0 copy-done.3
  86.2 1.9 %middle.1 = bf16[16,8,8,128]{3,2,1,0:T(8,128)(2,1)} custom-call(bf16[16,8,8,128]{3,2,1,0:T(8,128)(2,1)} %bitcast.8, bf16[128,128]{1,0:T(8,128)(2,1)} %get-tuple-element.27.kx_ref, f32[8,128]{1,0:T(8,128)} %get-tuple-element.25.mark_ref, f32[8,128]{1,0:T(8,128)} %copy-done.3), custom_call_target="tpu_custom_call" | custom-call | tf_op jit(solution)/shard_map/middle/pallas_call | solution.py:110
  88.2 19.3 %all_to_all.23 = bf16[128,8,128]{2,1,0:T(8,128)(2,1)S(1)} all-to-all(bf16[128,8,128]{2,1,0:T(8,128)(2,1)} %bitcast.9), channel_id=1, replica_groups=mesh['gx'=16,'gy'=8,'gz'=2] {'gx','gy'}, dimensions={0} | all-to-all | bytes 524288 | tf_op jit(solution)/shard_map/all_to_all | solution.py:352
  107.5 0.0 copy-start
  107.5 3.5 %collective-permute-start.3 = (bf16[64,2,8,128]{3,2,1,0:T(8,128)(2,1)S(1)}, bf16[64,2,8,128]{3,2,1,0:T(8,128)(2,1)S(1)}, u32[]{:S(2)}, u32[]{:S(2)}) collective-permute-start(bf16[64,2,8,128]{3,2,1,0:T(8,128)(2,1)S(1)} %bitcast.10), channel_id=1, source_target_pairs={{0,1},{1,0},{2,3},{3,2},{4,5},{5,4},{6,7},{7,6},{8,9},{9,8},{10,11... | collective-permute-start | bytes 786440 | tf_op jit(solution)/shard_map/ppermute | solution.py:380
  111.0 1.2 collective-permute-done.3.other_ref
  112.2 0.0 copy-start.1
  112.2 0.0 copy-done
  112.2 0.7 copy-done.1
  112.9 18.2 %third.1 = bf16[8,16,64,128]{3,2,1,0:T(8,128)(2,1)} custom-call(s32[3]{0:T(128)} %pad_add_fusion.idx_ref, f32[80,128]{1,0:T(8,128)} %get-tuple-element.22.q_ref, bf16[64,2,8,128]{3,2,1,0:T(8,128)(2,1)} %bitcast.11, bf16[64,2,8,128]{3,2,1,0:T(8,128)(2,1)} %copy-done.1, bf16[8,16,64,128]{3,2,1,0:T(8,128)(2,1)} %tok_ref.3, bf16[128,128]{1,0:T(8,128)(2,1)} %wo_ref.1, ...), custom_call_target="tpu_custom_call" | custom-call | tf_op jit(solution)/shard_map/third/pallas_call | solution.py:329
  (1 shorter events, 0.0 us)
Async XLA Ops:
  5.6 4.2 %collective-permute-start = (f32[24,128]{1,0:T(8,128)}, f32[24,128]{1,0:T(8,128)S(1)}, u32[]{:S(2)}, u32[]{:S(2)}) collective-permute-start(f32[24,128]{1,0:T(8,128)} %get-tuple-element.17), channel_id=1, source_target_pairs={{0,1},{1,0},{2,3},{3,2},{4,5},{5,4},{6,7},{7,6},{8,9},{9,8},{10,11... | collective-permute-start | bytes 36872 | tf_op jit(solution)/shard_map/ppermute | solution.py:363
  10.6 15.4 %copy-start.2 = (f32[24,128]{1,0:T(8,128)}, f32[24,128]{1,0:T(8,128)S(1)}, u32[]{:S(2)}) copy-start(f32[24,128]{1,0:T(8,128)S(1)} %add.6.xy_ref) | copy-start | bytes 36868
  60.7 5.5 %collective-permute-start.1 = (bf16[64,2,8,128]{3,2,1,0:T(8,128)(2,1)}, bf16[64,2,8,128]{3,2,1,0:T(8,128)(2,1)S(1)}, u32[]{:S(2)}, u32[]{:S(2)}) collective-permute-start(bf16[64,2,8,128]{3,2,1,0:T(8,128)(2,1)} %get-tuple-element.24), channel_id=1, source_target_pairs={{0,1},{1,0},{2,3},{3,2},{4,5},{5,4},{6,7},{7,6},{8,9},{9,8},{10,11... | collective-permute-start | bytes 786440 | tf_op jit(solution)/shard_map/ppermute | solution.py:373
  64.8 2.4 %collective-permute-start.2 = (f32[8,128]{1,0:T(8,128)}, f32[8,128]{1,0:T(8,128)S(1)}, u32[]{:S(2)}, u32[]{:S(2)}) collective-permute-start(f32[8,128]{1,0:T(8,128)} %get-tuple-element.25.mark_ref), channel_id=1, source_target_pairs={{0,1},{1,0},{2,3},{3,2},{4,5},{5,4},{6,7},{7,6},{8,9},{9,8},{10,11... | collective-permute-start | bytes 12296 | tf_op jit(solution)/shard_map/ppermute | solution.py:372
  67.2 19.0 %copy-start.3 = (f32[8,128]{1,0:T(8,128)}, f32[8,128]{1,0:T(8,128)S(1)}, u32[]{:S(2)}) copy-start(f32[8,128]{1,0:T(8,128)S(1)} %collective-permute-done.2.mark2_ref) | copy-start | bytes 12292
  107.5 4.7 %copy-start = (bf16[128,8,128]{2,1,0:T(8,128)(2,1)}, bf16[128,8,128]{2,1,0:T(8,128)(2,1)S(1)}, u32[]{:S(2)}) copy-start(bf16[128,8,128]{2,1,0:T(8,128)(2,1)S(1)} %all_to_all.23) | copy-start | bytes 786436
  107.5 4.7 %collective-permute-start.3 = (bf16[64,2,8,128]{3,2,1,0:T(8,128)(2,1)S(1)}, bf16[64,2,8,128]{3,2,1,0:T(8,128)(2,1)S(1)}, u32[]{:S(2)}, u32[]{:S(2)}) collective-permute-start(bf16[64,2,8,128]{3,2,1,0:T(8,128)(2,1)S(1)} %bitcast.10), channel_id=1, source_target_pairs={{0,1},{1,0},{2,3},{3,2},{4,5},{5,4},{6,7},{7,6},{8,9},{9,8},{10,11... | collective-permute-start | bytes 786440 | tf_op jit(solution)/shard_map/ppermute | solution.py:380
  112.2 0.7 copy-start.1

commit v5 on v2

--- a/solution.py
+++ b/solution.py
@@ -23,6 +23,10 @@
     return lax.dot_general(a, b, dims, preferred_element_type=F32)
 
 
+def dot(a, b, dims=(((1,), (0,)), ((), ()))):
+    return lax.dot_general(a, b, dims, preferred_element_type=F32)
+
+
 def norm_rows(values):
     mean = jnp.mean(values, axis=-1, keepdims=True)
     centred = values - mean
@@ -40,6 +44,13 @@
     return jnp.concatenate([values, values], axis=0)
 
 
+def norm_rows_matmul(values):
+    centred = values - jnp.mean(values, axis=-1, keepdims=True)
+    mean_of = jnp.full((C, C), 1.0 / C, BF)
+    spread = dot((centred * centred).astype(BF), mean_of)
+    return centred * lax.rsqrt(spread + EPS)
+
+
 def iota2(shape, dim):
     return lax.broadcasted_iota(jnp.int32, shape, dim)
 
@@ -52,7 +63,7 @@
     step = pl.program_id(0)
     nb, ny, nz, _ = tok_ref.shape
     x = tok_ref[...].reshape(nb * ny * nz, C).astype(F32)
-    normed = norm_rows(x).astype(BF)
+    normed = norm_rows_matmul(x).astype(BF)
     wvt = wv_ref[...].T
     n32 = normed.astype(F32).reshape(nb, ny, nz, C)
     sxy = jnp.sum(n32, axis=2)
@@ -121,14 +132,19 @@
     return both.reshape(ny * nz, HD * HD).astype(BF)
 
 
-def reorder(n, major):
-    out, src = iota2((n * HD, n * HD), 0), iota2((n * HD, n * HD), 1)
-    cx, xc = (out, src) if major else (src, out)
-    return ones_where((cx // n == xc % HD) & (cx % n == xc // HD))
-
-
 def second_kernel(
-    idx_ref, r_ref, w_ref, vt_ref, send_ref, keep_ref, qo_ref, kx_ref, k_scr, *, sizes
+    idx_ref,
+    r_ref,
+    w_ref,
+    vt_ref,
+    send_ref,
+    keep_ref,
+    qo_ref,
+    kx_ref,
+    k_scr,
+    row_scr,
+    *,
+    sizes
 ):
     step = pl.program_id(0)
     nx, ny, nz = sizes
@@ -182,17 +198,17 @@
 
     ky = k_scr[0:ny, :]
     kz = k_scr[ny : ny + nz, :]
-    perm = reorder(nx, True)
     first_head = jnp.where(step == 0, (1 - gz) * half, gz * half)
 
     def contract(out_ref):
         for j in range(half):
             mixer = outer_yz(ky, kz, first_head + j)
-            narrow = dot(vt_ref[j].reshape(nx * HD, ny * nz), mixer).astype(BF)
-            narrow = dot(perm, narrow).astype(BF).reshape(HD, nx, HD * HD)
+            narrow = dot(vt_ref[j].reshape(nx * HD, ny * nz), mixer)
             for side in range(2):
-                cut = narrow[:, :, side * C : (side + 1) * C]
-                out_ref[j * HD : (j + 1) * HD, side] = cut
+                row_scr[j, side] = narrow[:, side * C : (side + 1) * C]
+                for channel in range(HD):
+                    rows = row_scr[j, side, pl.ds(channel, nx, stride=HD), :]
+                    out_ref[j * HD + channel, side] = rows.astype(BF)
 
     @pl.when(step == 0)
     def _():
@@ -226,7 +242,10 @@
                 pl.BlockSpec((ny + nz, C), lambda i, s: (0, 0)),
                 pl.BlockSpec((C, C), lambda i, s: (0, 0)),
             ],
-            scratch_shapes=[pltpu.VMEM((ny + nz, C), F32)],
+            scratch_shapes=[
+                pltpu.VMEM((ny + nz, C), F32),
+                pltpu.VMEM((half, 2, nx * HD, C), F32),
+            ],
         ),
         out_shape=[
             jax.ShapeDtypeStruct(core, BF),
@@ -261,7 +280,7 @@
 
 
 def third_kernel(
-    idx_ref, q_ref, mine_ref, other_ref, tok_ref, wo_ref, wg_ref, wd_ref, out_ref, mix_scr
+    idx_ref, q_ref, mine_ref, other_ref, tok_ref, wo_ref, wg_ref, wd_ref, out_ref, mix_scr, row_scr
 ):
     step = pl.program_id(0)
     nb, ny, nz, _ = tok_ref.shape
@@ -273,14 +292,23 @@
     def _():
         qy = q_ref[0:ny, :]
         qz = q_ref[ny : ny + nz, :]
-        perm = reorder(nx, False)
         for j in range(HEADS):
             source = mine_ref if j < half else other_ref
             head = jnp.where(gz == 0, j, (j + half) % HEADS)
             at = j % half * HD
             mixer = outer_yz(qy, qz, head)
-            sides = [source[at : at + HD, i].reshape(HD * nx, C) for i in range(2)]
-            narrow = dot(perm, jnp.concatenate(sides, axis=1)).astype(BF)
+            for i in range(2):
+                rows = source[at : at + HD, i].astype(F32).reshape(HD * nx, C)
+                row_scr[j, i] = rows
+            narrow = jnp.concatenate(
+                [
+                    jnp.concatenate(
+                        [row_scr[j, i, pl.ds(k, HD, stride=nx), :] for k in range(nx)], axis=0
+                    )
+                    for i in range(2)
+                ],
+                axis=1,
+            ).astype(BF)
             mixed = dot(narrow, mixer, NT).astype(BF)
             mix_scr[:, head, :, :] = mixed.reshape(nx, HD, ny * nz)
 
@@ -288,9 +316,13 @@
     mixed = jnp.concatenate(mixed, axis=0)
     tok = tok_ref[...].reshape(nb * ny * nz, C)
     resid = tok.astype(F32) + dot(mixed, wo_ref[...])
-    inner = norm_rows(resid).astype(BF)
-    both = dot(inner, wg_ref[...])
-    hidden = (jax.nn.gelu(both[:, :FF]) * both[:, FF:]).astype(BF)
+    inner = norm_rows_matmul(resid).astype(BF)
+    both = dot(inner, wg_ref[...]).astype(BF)
+    gate = both[:, :FF]
+    root = math.sqrt(2.0 / math.pi)
+    inside = gate * (BF(root) + BF(root * 0.044715) * (gate * gate))
+    half_gate = gate * BF(0.5)
+    hidden = (half_gate + half_gate * jnp.tanh(inside)) * both[:, FF:]
     result = (resid + dot(hidden, wd_ref[...])).astype(BF)
     out_ref[...] = result.reshape(nb, ny, nz, C)
 
@@ -315,7 +347,10 @@
                 full(w_down),
             ],
             out_specs=slab,
-            scratch_shapes=[pltpu.VMEM((nx, HEADS, HD, ny * nz), BF)],
+            scratch_shapes=[
+                pltpu.VMEM((nx, HEADS, HD, ny * nz), BF),
+                pltpu.VMEM((HEADS, 2, nx * HD, C), F32),
+            ],
         ),
         out_shape=jax.ShapeDtypeStruct(tokens.shape, BF),
         name="third",
@@ -334,6 +369,7 @@
     rz = nz // cx
     vt, pool, sum_x = first(tokens, w_qkv, cx)
     sum_x = sum_x.reshape(nx, C)
+    pool, idx = lax.optimization_barrier((pool, idx))
     got = jnp.sum(a2a(pool, "gx"), axis=0)
     packed = jnp.concatenate([sum_x, got], axis=0)
     wide = jnp.broadcast_to(packed, (cy * cz,) + packed.shape)

time: 129 us -> 123 us (0.953)
  blocking collectives: 72.7 us -> 83.5 us
  waiting for transfers between devices: 9.39 us -> 2.53 us
  Pallas kernels: 33.1 us -> 27.3 us
  starting transfers between devices: 9.23 us -> 5.7 us
  local copies, waits for them, and re-layouts: 2.07 us -> 0.73 us
    all_to_all x4 -> x5, blocking collectives: 72.7 us -> 83.5 us  [a2a(): return lax.all_to_all(values, axes, 0, 0, tiled=True)]
    all_to_all x1 -> x0, waiting for transfers between devices: 6.86 us -> none  [a2a(): return lax.all_to_all(values, axes, 0, 0, tiled=True)]
    all_to_all x1 -> x0, starting transfers between devices: 3.52 us -> none  [a2a(): return lax.all_to_all(values, axes, 0, 0, tiled=True)]
    pallas_call x1, Pallas kernels: 18.2 us -> 15.3 us  [third(): pl.pallas_call(third_kernel, grid_spec=pltpu.PrefetchScalarGridSpec(num_s...]
    pallas_call x1, Pallas kernels: 7.51 us -> 5.44 us  [second(): pl.pallas_call(functools.partial(second_kernel, sizes=sizes), grid_spec=p...]
  transfers between devices with their start and end apart: 3 -> 2, of which waited for: 3 -> 2; matrix products, arithmetic and copies ran while one was open for 0% -> 0% of each run, Pallas kernels for 0% -> 0%
where the time goes in v5:
time: 123 us; the launch traced here: 122 us
  blocking collectives  83.5 us (68%)
  Pallas kernels  27.3 us (22%)
  starting transfers between devices  5.7 us (5%)
  waiting for transfers between devices  2.53 us (2%)
  other arithmetic  2.33 us (2%)
    all_to_all x5, blocking collectives, a2a(): return lax.all_to_all(values, axes, 0, 0, tiled=True)  83.5 us
    pallas_call x1, Pallas kernels, third(): pl.pallas_call(third_kernel, grid_spec=pltpu.PrefetchScalarGridSpec(num_s...  15.3 us
    pallas_call x1, Pallas kernels, second(): pl.pallas_call(functools.partial(second_kernel, sizes=sizes), grid_spec=p...  5.44 us
    pallas_call x1, Pallas kernels, first(): pl.pallas_call(first_kernel, grid=(nx // block,), in_specs=[pl.BlockSpec(...  4.71 us
    ppermute x1, starting transfers between devices, body(): other = lax.ppermute(mine, 'gz', swap)  3.52 us
  transfers between devices with their start and end apart: 2, of which 2 were waited for; matrix products, arithmetic and copies ran while one was open for 0% of the time, Pallas kernels for 0%

profile of v5, /device:TPU:1, one launch (start us, length us, event | category | flops | bytes accessed | tf_op | source)
XLA Modules:
  0.0 122.1 jit_solution(4140834171936508158)
XLA Ops:
  0.0 4.7 %first.1 = (bf16[8,8,16,1024]{3,2,1,0:T(8,128)(2,1)}, f32[16,8,128]{2,1,0:T(8,128)}, f32[2,4,128]{2,1,0:T(4,128)}) custom-call(bf16[8,16,64,128]{3,2,1,0:T(8,128)(2,1)} %tok_ref.3, bf16[128,384]{1,0:T(8,128)(2,1)} %w_ref.1), custom_call_target="tpu_custom_call" | custom-call | tf_op jit(solution)/shard_map/first/pallas_call | solution.py:98
  4.7 0.6 pad_add_fusion.idx_ref
  5.3 17.5 %all_to_all.25 = f32[16,8,128]{2,1,0:T(8,128)S(1)} all-to-all(f32[16,8,128]{2,1,0:T(8,128)} %get-tuple-element.17), channel_id=1, replica_groups=mesh['gx'=16,'gy'=8,'gz'=2] {'gx'}, dimensions={0} | all-to-all | bytes 131072 | tf_op jit(solution)/shard_map/all_to_all | solution.py:361
  22.8 0.7 pad_maximum_fusion.1
  23.5 16.1 %all_to_all.26 = f32[16,16,128]{2,1,0:T(8,128)S(1)} all-to-all(f32[16,16,128]{2,1,0:T(8,128)S(1)} %broadcast_in_dim.6), channel_id=1, replica_groups=mesh['gx'=16,'gy'=8,'gz'=2] {'gy','gz'}, dimensions={0} | all-to-all | bytes 262144 | tf_op jit(solution)/shard_map/all_to_all | solution.py:361
  39.7 10.7 %all_to_all.27.r_ref = f32[16,24,128]{2,1,0:T(8,128)} all-to-all(f32[16,24,128]{2,1,0:T(8,128)S(1)} %broadcast_in_dim.7), channel_id=1, replica_groups=mesh['gx'=16,'gy'=8,'gz'=2] {'gx'}, dimensions={0} | all-to-all | bytes 393216 | tf_op jit(solution)/shard_map/all_to_all | solution.py:361
  50.4 5.4 %second.1 = (bf16[64,2,8,128]{3,2,1,0:T(8,128)(2,1)}, bf16[64,2,8,128]{3,2,1,0:T(8,128)(2,1)}, f32[80,128]{1,0:T(8,128)}, bf16[128,128]{1,0:T(8,128)(2,1)}) custom-call(s32[3]{0:T(128)} %pad_add_fusion.idx_ref, f32[16,24,128]{2,1,0:T(8,128)} %all_to_all.27.r_ref, bf16[128,384]{1,0:T(8,128)(2,1)} %w_ref.1, bf16[8,8,16,1024]{3,2,1,0:T(8,128)(2,1)} %get-tuple-element.18.vt_ref), custom_call_target="tpu_custom_call" | custom-call | tf_op jit(solution)/shard_map/second/pallas_call | solution.py:226
  55.8 2.2 %collective-permute-start = (bf16[64,2,8,128]{3,2,1,0:T(8,128)(2,1)}, bf16[64,2,8,128]{3,2,1,0:T(8,128)(2,1)S(1)}, u32[]{:S(2)}, u32[]{:S(2)}) collective-permute-start(bf16[64,2,8,128]{3,2,1,0:T(8,128)(2,1)} %get-tuple-element.21), channel_id=1, source_target_pairs={{0,1},{1,0},{2,3},{3,2},{4,5},{5,4},{6,7},{7,6},{8,9},{9,8},{10,11... | collective-permute-start | bytes 786440 | tf_op jit(solution)/shard_map/ppermute | solution.py:385
  58.0 1.4 %collective-permute-done = bf16[64,2,8,128]{3,2,1,0:T(8,128)(2,1)S(1)} collective-permute-done((bf16[64,2,8,128]{3,2,1,0:T(8,128)(2,1)}, bf16[64,2,8,128]{3,2,1,0:T(8,128)(2,1)S(1)}, u32[]{:S(2)}, u32[]{:S(2)}) %collective-permute-start) | collective-permute-done | bytes 262176 | tf_op jit(solution)/shard_map/ppermute | solution.py:385
  59.4 1.0 add_convert_fusion
  60.4 19.7 %all_to_all.28 = bf16[128,8,128]{2,1,0:T(8,128)(2,1)} all-to-all(bf16[128,8,128]{2,1,0:T(8,128)(2,1)S(1)} %bitcast.10), channel_id=1, replica_groups=mesh['gx'=16,'gy'=8,'gz'=2] {'gx','gy'}, dimensions={0} | all-to-all | bytes 524288 | tf_op jit(solution)/shard_map/all_to_all | solution.py:361
  80.1 1.8 %middle.1 = bf16[16,8,8,128]{3,2,1,0:T(8,128)(2,1)} custom-call(bf16[16,8,8,128]{3,2,1,0:T(8,128)(2,1)} %bitcast.11, bf16[128,128]{1,0:T(8,128)(2,1)} %get-tuple-element.22.kx_ref), custom_call_target="tpu_custom_call" | custom-call | tf_op jit(solution)/shard_map/middle/pallas_call | solution.py:273
  82.0 19.4 %all_to_all.29 = bf16[128,8,128]{2,1,0:T(8,128)(2,1)S(1)} all-to-all(bf16[128,8,128]{2,1,0:T(8,128)(2,1)} %bitcast.12), channel_id=1, replica_groups=mesh['gx'=16,'gy'=8,'gz'=2] {'gx','gy'}, dimensions={0} | all-to-all | bytes 524288 | tf_op jit(solution)/shard_map/all_to_all | solution.py:361
  101.4 0.0 copy-start
  101.4 3.5 %collective-permute-start.1 = (bf16[64,2,8,128]{3,2,1,0:T(8,128)(2,1)S(1)}, bf16[64,2,8,128]{3,2,1,0:T(8,128)(2,1)S(1)}, u32[]{:S(2)}, u32[]{:S(2)}) collective-permute-start(bf16[64,2,8,128]{3,2,1,0:T(8,128)(2,1)S(1)} %bitcast.13), channel_id=1, source_target_pairs={{0,1},{1,0},{2,3},{3,2},{4,5},{5,4},{6,7},{7,6},{8,9},{9,8},{10,11... | collective-permute-start | bytes 786440 | tf_op jit(solution)/shard_map/ppermute | solution.py:390
  104.9 1.2 collective-permute-done.1.other_ref
  106.1 0.0 copy-start.1
  106.1 0.0 copy-done
  106.1 0.7 copy-done.1
  106.8 15.3 %third.1 = bf16[8,16,64,128]{3,2,1,0:T(8,128)(2,1)} custom-call(s32[3]{0:T(128)} %pad_add_fusion.idx_ref, f32[80,128]{1,0:T(8,128)} %get-tuple-element.19.q_ref, bf16[64,2,8,128]{3,2,1,0:T(8,128)(2,1)} %bitcast.14, bf16[64,2,8,128]{3,2,1,0:T(8,128)(2,1)} %copy-done.1, bf16[8,16,64,128]{3,2,1,0:T(8,128)(2,1)} %tok_ref.3, bf16[128,128]{1,0:T(8,128)(2,1)} %wo_ref.1, ...), custom_call_target="tpu_custom_call" | custom-call | tf_op jit(solution)/shard_map/third/pallas_call | solution.py:335
  (7 shorter events, 0.1 us)
Async XLA Ops:
  55.8 3.6 %collective-permute-start = (bf16[64,2,8,128]{3,2,1,0:T(8,128)(2,1)}, bf16[64,2,8,128]{3,2,1,0:T(8,128)(2,1)S(1)}, u32[]{:S(2)}, u32[]{:S(2)}) collective-permute-start(bf16[64,2,8,128]{3,2,1,0:T(8,128)(2,1)} %get-tuple-element.21), channel_id=1, source_target_pairs={{0,1},{1,0},{2,3},{3,2},{4,5},{5,4},{6,7},{7,6},{8,9},{9,8},{10,11... | collective-permute-start | bytes 786440 | tf_op jit(solution)/shard_map/ppermute | solution.py:385
  101.4 4.7 %copy-start = (bf16[128,8,128]{2,1,0:T(8,128)(2,1)}, bf16[128,8,128]{2,1,0:T(8,128)(2,1)S(1)}, u32[]{:S(2)}) copy-start(bf16[128,8,128]{2,1,0:T(8,128)(2,1)S(1)} %all_to_all.29) | copy-start | bytes 786436
  101.4 4.7 %collective-permute-start.1 = (bf16[64,2,8,128]{3,2,1,0:T(8,128)(2,1)S(1)}, bf16[64,2,8,128]{3,2,1,0:T(8,128)(2,1)S(1)}, u32[]{:S(2)}, u32[]{:S(2)}) collective-permute-start(bf16[64,2,8,128]{3,2,1,0:T(8,128)(2,1)S(1)} %bitcast.13), channel_id=1, source_target_pairs={{0,1},{1,0},{2,3},{3,2},{4,5},{5,4},{6,7},{7,6},{8,9},{9,8},{10,11... | collective-permute-start | bytes 786440 | tf_op jit(solution)/shard_map/ppermute | solution.py:390
  106.1 0.7 copy-start.1

commit v6 on v5

--- a/solution.py
+++ b/solution.py
@@ -59,7 +59,9 @@
     return jnp.where(cond, 1.0, 0.0).astype(BF)
 
 
-def first_kernel(tok_ref, wv_ref, vt_ref, pool_ref, sx_ref, sy_acc, sz_acc):
+def first_kernel(
+    idx_ref, tok_ref, wv_ref, keep_ref, send_ref, pool_ref, sx_ref, sy_acc, sz_acc
+):
     step = pl.program_id(0)
     nb, ny, nz, _ = tok_ref.shape
     x = tok_ref[...].reshape(nb * ny * nz, C).astype(F32)
@@ -72,7 +74,11 @@
     sx_ref[0] = jnp.sum(sxy, axis=1)
     for i in range(nb):
         vt = dot(wvt, normed[i * ny * nz : (i + 1) * ny * nz], NT).astype(BF)
-        vt_ref[:, i, :, :] = vt.reshape(HEADS, HD, ny * nz)
+        low, high = vt[: C // 2], vt[C // 2 :]
+        lower = idx_ref[2] == 0
+        shape = (HEADS // 2, HD, ny * nz)
+        keep_ref[:, i, :, :] = jnp.where(lower, low, high).reshape(shape)
+        send_ref[:, i, :, :] = jnp.where(lower, high, low).reshape(shape)
 
     @pl.when(step == 0)
     def _():
@@ -92,29 +98,36 @@
         pool_ref[:, ry : ry + rz, :] = sz_acc[...].reshape(parts, rz, C)
 
 
-def first(tokens, w_qkv, parts, block=4):
+def first(idx, tokens, w_qkv, parts, block=4):
     nx, ny, nz, _ = tokens.shape
     rows = -(-(ny // parts + nz // parts) // 8) * 8
+    half = HEADS // 2
+    value = pl.BlockSpec((half, block, HD, ny * nz), lambda i, s: (0, i, 0, 0))
     return pl.pallas_call(
         first_kernel,
-        grid=(nx // block,),
-        in_specs=[
-            pl.BlockSpec((block, ny, nz, C), lambda i: (i, 0, 0, 0)),
-            pl.BlockSpec((C, C), lambda i: (0, 2)),
-        ],
-        out_specs=[
-            pl.BlockSpec((HEADS, block, HD, ny * nz), lambda i: (0, i, 0, 0)),
-            pl.BlockSpec((parts, rows, C), lambda i: (0, 0, 0)),
-            pl.BlockSpec((1, block, C), lambda i: (i, 0, 0)),
-        ],
+        grid_spec=pltpu.PrefetchScalarGridSpec(
+            num_scalar_prefetch=1,
+            grid=(nx // block,),
+            in_specs=[
+                pl.BlockSpec((block, ny, nz, C), lambda i, s: (i, 0, 0, 0)),
+                pl.BlockSpec((C, C), lambda i, s: (0, 2)),
+            ],
+            out_specs=[
+                value,
+                value,
+                pl.BlockSpec((parts, rows, C), lambda i, s: (0, 0, 0)),
+                pl.BlockSpec((1, block, C), lambda i, s: (i, 0, 0)),
+            ],
+            scratch_shapes=[pltpu.VMEM((ny, C), F32), pltpu.VMEM((nz, C), F32)],
+        ),
         out_shape=[
-            jax.ShapeDtypeStruct((HEADS, nx, HD, ny * nz), BF),
+            jax.ShapeDtypeStruct((half, nx, HD, ny * nz), BF),
+            jax.ShapeDtypeStruct((half, nx, HD, ny * nz), BF),
             jax.ShapeDtypeStruct((parts, rows, C), F32),
             jax.ShapeDtypeStruct((nx // block, block, C), F32),
         ],
-        scratch_shapes=[pltpu.VMEM((ny, C), F32), pltpu.VMEM((nz, C), F32)],
         name="first",
-    )(tokens, w_qkv)
+    )(idx, tokens, w_qkv)
 
 
 def lane_expand(rows, head, fine):
@@ -136,9 +149,9 @@
     idx_ref,
     r_ref,
     w_ref,
-    vt_ref,
-    send_ref,
-    keep_ref,
+    mine_ref,
+    got_ref,
+    out_ref,
     qo_ref,
     kx_ref,
     k_scr,
@@ -184,77 +197,67 @@
             at = nx + g * ry
             own_y = jnp.where(gy == g, qk[:, at : at + ry, :], own_y)
         own_y = own_y.reshape(ny, 2 * C)
-        own_z = jnp.zeros((px, rz, 2 * C), F32)
-        for g in range(pz):
-            at = nx + py * ry + g * rz
-            own_z = jnp.where(gz == g, qk[:, at : at + rz, :], own_z)
-        own_z = own_z.reshape(nz, 2 * C)
-        at = 0
-        for own, (scale_q, scale_k) in zip((own_y, own_z), scaled[1:]):
-            n = own.shape[0]
-            qo_ref[at : at + n, :] = own[:, :C] * scale_q
-            k_scr[at : at + n, :] = own[:, C:] * scale_k
-            at += n
-
-    ky = k_scr[0:ny, :]
-    kz = k_scr[ny : ny + nz, :]
-    first_head = jnp.where(step == 0, (1 - gz) * half, gz * half)
-
-    def contract(out_ref):
-        for j in range(half):
-            mixer = outer_yz(ky, kz, first_head + j)
-            narrow = dot(vt_ref[j].reshape(nx * HD, ny * nz), mixer)
-            for side in range(2):
-                row_scr[j, side] = narrow[:, side * C : (side + 1) * C]
-                for channel in range(HD):
-                    rows = row_scr[j, side, pl.ds(channel, nx, stride=HD), :]
-                    out_ref[j * HD + channel, side] = rows.astype(BF)
-
-    @pl.when(step == 0)
-    def _():
-        contract(send_ref)
-
-    @pl.when(step == 1)
-    def _():
-        contract(keep_ref)
-
-
-def second(idx, pooled, w_qkv, vt, sizes):
+        at = nx + py * ry
+        low = qk[:, at : at + rz, :].reshape(nz, 2 * C)
+        high = qk[:, at + rz : at + 2 * rz, :].reshape(nz, 2 * C)
+        own_z = jnp.where(gz == 0, low, high)
+        other_z = jnp.where(gz == 0, high, low)
+        qo_ref[0:ny, :] = own_y[:, :C] * scaled[1][0]
+        qo_ref[ny:, :] = own_z[:, :C] * scaled[2][0]
+        k_scr[0:ny, :] = own_y[:, C:] * scaled[1][1]
+        k_scr[ny : ny + nz, :] = own_z[:, C:] * scaled[2][1]
+        k_scr[ny + nz :, :] = other_z[:, C:] * scaled[2][1]
+
+    heads = mine_ref.shape[0]
+    for j in range(heads):
+        head = gz * half + step * heads + j
+        wide_y = lane_expand(k_scr[0:ny, :], head, False).reshape(ny, 1, HD * HD)
+        wide_z = lane_expand(k_scr[ny:, :], head, True)
+        narrow = jnp.zeros((nx * HD, HD * HD), F32)
+        for i, source in enumerate((mine_ref, got_ref)):
+            mixer = wide_y * wide_z[i * nz : (i + 1) * nz].reshape(1, nz, HD * HD)
+            mixer = mixer.reshape(ny * nz, HD * HD).astype(BF)
+            narrow = narrow + dot(source[j].reshape(nx * HD, ny * nz), mixer)
+        for side in range(2):
+            row_scr[j, side] = narrow[:, side * C : (side + 1) * C]
+            for channel in range(HD):
+                rows = row_scr[j, side, pl.ds(channel, nx, stride=HD), :]
+                out_ref[j * HD + channel, side] = rows.astype(BF)
+
+
+def second(idx, pooled, w_qkv, mine, got, sizes, steps=2):
     nx, ny, nz = sizes
     half = HEADS // 2
-    core = (half * HD, 2, nx, C)
+    heads = half // steps
+    value = pl.BlockSpec((heads, nx, HD, ny * nz), lambda i, s: (i, 0, 0, 0))
     return pl.pallas_call(
         functools.partial(second_kernel, sizes=sizes),
         grid_spec=pltpu.PrefetchScalarGridSpec(
             num_scalar_prefetch=1,
-            grid=(2,),
+            grid=(steps,),
             in_specs=[
                 pl.BlockSpec(memory_space=pltpu.VMEM),
                 pl.BlockSpec((C, 2 * C), lambda i, s: (0, 0)),
-                pl.BlockSpec(
-                    (half, nx, HD, ny * nz),
-                    lambda i, s: (jnp.where(i == 0, 1 - s[2], s[2]), 0, 0, 0),
-                ),
+                value,
+                value,
             ],
             out_specs=[
-                pl.BlockSpec(core, lambda i, s: (0, 0, 0, 0)),
-                pl.BlockSpec(core, lambda i, s: (0, 0, 0, 0)),
+                pl.BlockSpec((heads * HD, 2, nx, C), lambda i, s: (i, 0, 0, 0)),
                 pl.BlockSpec((ny + nz, C), lambda i, s: (0, 0)),
                 pl.BlockSpec((C, C), lambda i, s: (0, 0)),
             ],
             scratch_shapes=[
-                pltpu.VMEM((ny + nz, C), F32),
-                pltpu.VMEM((half, 2, nx * HD, C), F32),
+                pltpu.VMEM((ny + 2 * nz, C), F32),
+                pltpu.VMEM((heads, 2, nx * HD, C), F32),
             ],
         ),
         out_shape=[
-            jax.ShapeDtypeStruct(core, BF),
-            jax.ShapeDtypeStruct(core, BF),
+            jax.ShapeDtypeStruct((half * HD, 2, nx, C), BF),
             jax.ShapeDtypeStruct((ny + nz, C), F32),
             jax.ShapeDtypeStruct((C, C), BF),
         ],
         name="second",
-    )(idx, pooled, w_qkv, vt)
+    )(idx, pooled, w_qkv, mine, got)
 
 
 def middle_kernel(g_ref, kx_ref, out_ref):
@@ -367,9 +370,9 @@
     idx = jnp.stack([lax.axis_index(a) for a in ("gx", "gy", "gz")]).astype(jnp.int32)
     ry = ny // cx
     rz = nz // cx
-    vt, pool, sum_x = first(tokens, w_qkv, cx)
+    keep, send, pool, sum_x = first(idx, tokens, w_qkv, cx)
+    got_value = lax.ppermute(send, "gz", [(0, 1), (1, 0)])
     sum_x = sum_x.reshape(nx, C)
-    pool, idx = lax.optimization_barrier((pool, idx))
     got = jnp.sum(a2a(pool, "gx"), axis=0)
     packed = jnp.concatenate([sum_x, got], axis=0)
     wide = jnp.broadcast_to(packed, (cy * cz,) + packed.shape)
@@ -378,15 +381,14 @@
     total_y = jnp.sum(wide[:, :, nx : nx + ry], axis=1).reshape(cy * ry, C)
     total_z = jnp.sum(wide[:, :, nx + ry : nx + ry + rz], axis=0).reshape(cz * rz, C)
     packed = jnp.concatenate([total_x, total_y, total_z], axis=0)
+    packed, got_value = lax.optimization_barrier((packed, got_value))
     pooled = a2a(jnp.broadcast_to(packed, (cx,) + packed.shape), "gx")
 
-    send, keep, q, kx = second(idx, pooled, w_qkv, vt, (nx, ny, nz))
+    part, q, kx = second(idx, pooled, w_qkv, keep, got_value, (nx, ny, nz))
     swap = [(0, 1), (1, 0)]
-    part = keep.astype(F32) + lax.ppermute(send, "gz", swap).astype(F32)
-    part = part.astype(BF).reshape(cx * cy, nx, C)
-    gathered = a2a(part, ("gx", "gy")).reshape(cx, cy, nx, C)
+    gathered = a2a(part.reshape(cx * cy, nx, C), ("gx", "gy")).reshape(cx, cy, nx, C)
     spread = middle(gathered, kx).reshape(cx * cy, nx, C)
-    mine = a2a(spread, ("gx", "gy")).reshape(keep.shape)
+    mine = a2a(spread, ("gx", "gy")).reshape(part.shape)
     other = lax.ppermute(mine, "gz", swap)
     return third(idx, q, mine, other, tokens, w_out, w_gate_up, w_down)
 

time: 123 us -> 120 us (0.976)
  blocking collectives: 83.5 us -> 81.7 us
  waiting for transfers between devices: 2.53 us -> 1.16 us
    all_to_all x5, blocking collectives: 83.5 us -> 81.7 us  [a2a(): return lax.all_to_all(values, axes, 0, 0, tiled=True)]
    ppermute x1, waiting for transfers between devices: 1.37 us -> 0.01 us  [body(): got_value = lax.ppermute(send, 'gz', [(0, 1), (1, 0)])]
  transfers between devices with their start and end apart: 2 -> 2, of which waited for: 2 -> 1; matrix products, arithmetic and copies ran while one was open for 0% -> 1% of each run, Pallas kernels for 0% -> 0%
where the time goes in v6:
time: 120 us; the launch traced here: 119 us
  blocking collectives  81.7 us (68%)
  Pallas kernels  27.5 us (23%)
  starting transfers between devices  6.76 us (6%)
  other arithmetic  1.41 us (1%)
    all_to_all x5, blocking collectives, a2a(): return lax.all_to_all(values, axes, 0, 0, tiled=True)  81.7 us
    pallas_call x1, Pallas kernels, third(): pl.pallas_call(third_kernel, grid_spec=pltpu.PrefetchScalarGridSpec(num_s...  15.3 us
    pallas_call x1, Pallas kernels, first(): pl.pallas_call(first_kernel, grid_spec=pltpu.PrefetchScalarGridSpec(num_s...  5.52 us
    pallas_call x1, Pallas kernels, second(): pl.pallas_call(functools.partial(second_kernel, sizes=sizes), grid_spec=p...  4.89 us
    ppermute x1, starting transfers between devices, body(): other = lax.ppermute(mine, 'gz', swap)  3.49 us
    ppermute x1, starting transfers between devices, body(): got_value = lax.ppermute(send, 'gz', [(0, 1), (1, 0)])  3.27 us
  transfers between devices with their start and end apart: 2, of which 1 were waited for; matrix products, arithmetic and copies ran while one was open for 1% of the time, Pallas kernels for 0%

profile of v6, /device:TPU:1, one launch (start us, length us, event | category | flops | bytes accessed | tf_op | source)
XLA Modules:
  0.0 119.3 jit_solution(10548186126951936551)
XLA Ops:
  0.0 0.7 pad_add_fusion.idx_ref
  0.7 5.5 %first.1 = (bf16[4,8,16,1024]{3,2,1,0:T(8,128)(2,1)}, bf16[4,8,16,1024]{3,2,1,0:T(8,128)(2,1)}, f32[16,8,128]{2,1,0:T(8,128)}, f32[2,4,128]{2,1,0:T(4,128)}) custom-call(s32[3]{0:T(128)} %pad_add_fusion.idx_ref, bf16[8,16,64,128]{3,2,1,0:T(8,128)(2,1)} %tok_ref.3, bf16[128,384]{1,0:T(8,128)(2,1)} %w_ref.1), custom_call_target="tpu_custom_call" | custom-call | tf_op jit(solution)/shard_map/first/pallas_call | solution.py:106
  6.2 3.3 %collective-permute-start = (bf16[4,8,16,1024]{3,2,1,0:T(8,128)(2,1)}, bf16[4,8,16,1024]{3,2,1,0:T(8,128)(2,1)S(1)}, u32[]{:S(2)}, u32[]{:S(2)}) collective-permute-start(bf16[4,8,16,1024]{3,2,1,0:T(8,128)(2,1)} %get-tuple-element.16), channel_id=1, source_target_pairs={{0,1},{1,0},{2,3},{3,2},{4,5},{5,4},{6,7},{7,6},{8,9},{9,8},{10,11... | collective-permute-start | bytes 3145736 | tf_op jit(solution)/shard_map/ppermute | solution.py:374
  9.4 15.1 %all_to_all.25 = f32[16,8,128]{2,1,0:T(8,128)S(1)} all-to-all(f32[16,8,128]{2,1,0:T(8,128)} %get-tuple-element.15), channel_id=1, replica_groups=mesh['gx'=16,'gy'=8,'gz'=2] {'gx'}, dimensions={0} | all-to-all | bytes 131072 | tf_op jit(solution)/shard_map/all_to_all | solution.py:364
  24.5 0.7 pad_maximum_fusion.1
  25.2 15.4 %all_to_all.26 = f32[16,16,128]{2,1,0:T(8,128)S(1)} all-to-all(f32[16,16,128]{2,1,0:T(8,128)S(1)} %broadcast_in_dim.6), channel_id=1, replica_groups=mesh['gx'=16,'gy'=8,'gz'=2] {'gy','gz'}, dimensions={0} | all-to-all | bytes 262144 | tf_op jit(solution)/shard_map/all_to_all | solution.py:364
  40.7 0.0 collective-permute-done.got_ref
  40.7 0.0 copy-start
  40.7 10.7 %all_to_all.27.r_ref = f32[16,24,128]{2,1,0:T(8,128)} all-to-all(f32[16,24,128]{2,1,0:T(8,128)S(1)} %broadcast_in_dim.7), channel_id=1, replica_groups=mesh['gx'=16,'gy'=8,'gz'=2] {'gx'}, dimensions={0} | all-to-all | bytes 393216 | tf_op jit(solution)/shard_map/all_to_all | solution.py:364
  51.4 0.0 copy-done
  51.4 4.9 %second.1 = (bf16[64,2,8,128]{3,2,1,0:T(8,128)(2,1)}, f32[80,128]{1,0:T(8,128)}, bf16[128,128]{1,0:T(8,128)(2,1)}) custom-call(s32[3]{0:T(128)} %pad_add_fusion.idx_ref, f32[16,24,128]{2,1,0:T(8,128)} %all_to_all.27.r_ref, bf16[128,384]{1,0:T(8,128)(2,1)} %w_ref.1, bf16[4,8,16,1024]{3,2,1,0:T(8,128)(2,1)} %get-tuple-element.18.mine_ref, ...), custom_call_target="tpu_custom_call" | custom-call | tf_op jit(solution)/shard_map/second/pallas_call | solution.py:233
  56.3 20.7 %all_to_all.28 = bf16[128,8,128]{2,1,0:T(8,128)(2,1)} all-to-all(bf16[128,8,128]{2,1,0:T(8,128)(2,1)} %bitcast.17), channel_id=1, replica_groups=mesh['gx'=16,'gy'=8,'gz'=2] {'gx','gy'}, dimensions={0} | all-to-all | bytes 524288 | tf_op jit(solution)/shard_map/all_to_all | solution.py:364
  77.0 1.8 %middle.1 = bf16[16,8,8,128]{3,2,1,0:T(8,128)(2,1)} custom-call(bf16[16,8,8,128]{3,2,1,0:T(8,128)(2,1)} %bitcast.10, bf16[128,128]{1,0:T(8,128)(2,1)} %get-tuple-element.22.kx_ref), custom_call_target="tpu_custom_call" | custom-call | tf_op jit(solution)/shard_map/middle/pallas_call | solution.py:276
  78.9 19.8 %all_to_all.29 = bf16[128,8,128]{2,1,0:T(8,128)(2,1)S(1)} all-to-all(bf16[128,8,128]{2,1,0:T(8,128)(2,1)} %bitcast.11), channel_id=1, replica_groups=mesh['gx'=16,'gy'=8,'gz'=2] {'gx','gy'}, dimensions={0} | all-to-all | bytes 524288 | tf_op jit(solution)/shard_map/all_to_all | solution.py:364
  98.7 0.0 copy-start.1
  98.7 3.5 %collective-permute-start.1 = (bf16[64,2,8,128]{3,2,1,0:T(8,128)(2,1)S(1)}, bf16[64,2,8,128]{3,2,1,0:T(8,128)(2,1)S(1)}, u32[]{:S(2)}, u32[]{:S(2)}) collective-permute-start(bf16[64,2,8,128]{3,2,1,0:T(8,128)(2,1)S(1)} %bitcast.12), channel_id=1, source_target_pairs={{0,1},{1,0},{2,3},{3,2},{4,5},{5,4},{6,7},{7,6},{8,9},{9,8},{10,11... | collective-permute-start | bytes 786440 | tf_op jit(solution)/shard_map/ppermute | solution.py:392
  102.2 1.2 collective-permute-done.1.other_ref
  103.3 0.0 copy-start.2
  103.3 0.0 copy-done.1
  103.3 0.7 copy-done.2
  104.0 15.3 %third.1 = bf16[8,16,64,128]{3,2,1,0:T(8,128)(2,1)} custom-call(s32[3]{0:T(128)} %pad_add_fusion.idx_ref, f32[80,128]{1,0:T(8,128)} %get-tuple-element.20.q_ref, bf16[64,2,8,128]{3,2,1,0:T(8,128)(2,1)} %bitcast.13, bf16[64,2,8,128]{3,2,1,0:T(8,128)(2,1)} %copy-done.2, bf16[8,16,64,128]{3,2,1,0:T(8,128)(2,1)} %tok_ref.3, bf16[128,128]{1,0:T(8,128)(2,1)} %wo_ref.1, ...), custom_call_target="tpu_custom_call" | custom-call | tf_op jit(solution)/shard_map/third/pallas_call | solution.py:338
  (7 shorter events, 0.1 us)
Async XLA Ops:
  6.2 34.5 %collective-permute-start = (bf16[4,8,16,1024]{3,2,1,0:T(8,128)(2,1)}, bf16[4,8,16,1024]{3,2,1,0:T(8,128)(2,1)S(1)}, u32[]{:S(2)}, u32[]{:S(2)}) collective-permute-start(bf16[4,8,16,1024]{3,2,1,0:T(8,128)(2,1)} %get-tuple-element.16), channel_id=1, source_target_pairs={{0,1},{1,0},{2,3},{3,2},{4,5},{5,4},{6,7},{7,6},{8,9},{9,8},{10,11... | collective-permute-start | bytes 3145736 | tf_op jit(solution)/shard_map/ppermute | solution.py:374
  40.7 10.8 %copy-start = (bf16[4,8,16,1024]{3,2,1,0:T(8,128)(2,1)}, bf16[4,8,16,1024]{3,2,1,0:T(8,128)(2,1)S(1)}, u32[]{:S(2)}) copy-start(bf16[4,8,16,1024]{3,2,1,0:T(8,128)(2,1)S(1)} %collective-permute-done.got_ref) | copy-start | bytes 3145732
  98.7 4.7 %copy-start.1 = (bf16[128,8,128]{2,1,0:T(8,128)(2,1)}, bf16[128,8,128]{2,1,0:T(8,128)(2,1)S(1)}, u32[]{:S(2)}) copy-start(bf16[128,8,128]{2,1,0:T(8,128)(2,1)S(1)} %all_to_all.29) | copy-start | bytes 786436
  98.7 4.7 %collective-permute-start.1 = (bf16[64,2,8,128]{3,2,1,0:T(8,128)(2,1)S(1)}, bf16[64,2,8,128]{3,2,1,0:T(8,128)(2,1)S(1)}, u32[]{:S(2)}, u32[]{:S(2)}) collective-permute-start(bf16[64,2,8,128]{3,2,1,0:T(8,128)(2,1)S(1)} %bitcast.12), channel_id=1, source_target_pairs={{0,1},{1,0},{2,3},{3,2},{4,5},{5,4},{6,7},{7,6},{8,9},{9,8},{10,11... | collective-permute-start | bytes 786440 | tf_op jit(solution)/shard_map/ppermute | solution.py:392
  103.3 0.7 copy-start.2

commit v7 on v6

--- a/solution.py
+++ b/solution.py
@@ -60,13 +60,15 @@
 
 
 def first_kernel(
-    idx_ref, tok_ref, wv_ref, keep_ref, send_ref, pool_ref, sx_ref, sy_acc, sz_acc
+    core_ref, tok_ref, wv_ref, keep_ref, send_ref, pool_ref, sx_ref, sy_acc, sz_acc
 ):
     step = pl.program_id(0)
     nb, ny, nz, _ = tok_ref.shape
     x = tok_ref[...].reshape(nb * ny * nz, C).astype(F32)
     normed = norm_rows_matmul(x).astype(BF)
     wvt = wv_ref[...].T
+    turned = jnp.concatenate([wvt[C // 2 :], wvt[: C // 2]], axis=0)
+    wvt = jnp.where(core_ref[0] == 0, wvt, turned)
     n32 = normed.astype(F32).reshape(nb, ny, nz, C)
     sxy = jnp.sum(n32, axis=2)
     sy = jnp.sum(sxy, axis=0)
@@ -74,11 +76,9 @@
     sx_ref[0] = jnp.sum(sxy, axis=1)
     for i in range(nb):
         vt = dot(wvt, normed[i * ny * nz : (i + 1) * ny * nz], NT).astype(BF)
-        low, high = vt[: C // 2], vt[C // 2 :]
-        lower = idx_ref[2] == 0
         shape = (HEADS // 2, HD, ny * nz)
-        keep_ref[:, i, :, :] = jnp.where(lower, low, high).reshape(shape)
-        send_ref[:, i, :, :] = jnp.where(lower, high, low).reshape(shape)
+        keep_ref[:, i, :, :] = vt[: C // 2].reshape(shape)
+        send_ref[:, i, :, :] = vt[C // 2 :].reshape(shape)
 
     @pl.when(step == 0)
     def _():
@@ -98,7 +98,7 @@
         pool_ref[:, ry : ry + rz, :] = sz_acc[...].reshape(parts, rz, C)
 
 
-def first(idx, tokens, w_qkv, parts, block=4):
+def first(core, tokens, w_qkv, parts, block=4):
     nx, ny, nz, _ = tokens.shape
     rows = -(-(ny // parts + nz // parts) // 8) * 8
     half = HEADS // 2
@@ -127,26 +127,28 @@
             jax.ShapeDtypeStruct((nx // block, block, C), F32),
         ],
         name="first",
-    )(idx, tokens, w_qkv)
-
-
-def lane_expand(rows, head, fine):
-    col = iota2((C, HD * HD), 1)
-    pick = (col % HD) if fine else (col // HD)
-    return dot(halves(rows), twice(ones_where(iota2((C, HD * HD), 0) == head * HD + pick)))
-
-
-def outer_yz(ky, kz, head):
-    wide_y = lane_expand(ky, head, False)
-    wide_z = lane_expand(kz, head, True)
-    ny = ky.shape[0]
-    nz = kz.shape[0]
-    both = wide_y.reshape(ny, 1, HD * HD) * wide_z.reshape(1, nz, HD * HD)
+    )(core, tokens, w_qkv)
+
+
+def lane_expand(rows, first_head, heads, fine):
+    shape = (C, heads * HD * HD)
+    col = iota2(shape, 1)
+    pick = (col % HD) if fine else (col % (HD * HD) // HD)
+    channel = (first_head + col // (HD * HD)) * HD + pick
+    return dot(halves(rows), twice(ones_where(iota2(shape, 0) == channel)))
+
+
+def outer_yz(wide_y, wide_z, at):
+    ny, nz = wide_y.shape[0], wide_z.shape[0]
+    cut = slice(at * HD * HD, (at + 1) * HD * HD)
+    both = wide_y[:, cut].reshape(ny, 1, HD * HD) * wide_z[:, cut].reshape(1, nz, HD * HD)
     return both.reshape(ny * nz, HD * HD).astype(BF)
 
 
 def second_kernel(
-    idx_ref,
+    x_ref,
+    y_ref,
+    core_ref,
     r_ref,
     w_ref,
     mine_ref,
@@ -162,7 +164,7 @@
     step = pl.program_id(0)
     nx, ny, nz = sizes
     px, rows, _ = r_ref.shape
-    gx, gy, gz = idx_ref[0], idx_ref[1], idx_ref[2]
+    gx, gy, gz = x_ref[0], y_ref[0], core_ref[0]
     ry = ny // px
     rz = nz // px
     pz = 2
@@ -209,14 +211,13 @@
         k_scr[ny + nz :, :] = other_z[:, C:] * scaled[2][1]
 
     heads = mine_ref.shape[0]
+    first_head = gz * half + step * heads
+    wide_y = lane_expand(k_scr[0:ny, :], first_head, heads, False)
+    wide_z = lane_expand(k_scr[ny:, :], first_head, heads, True)
     for j in range(heads):
-        head = gz * half + step * heads + j
-        wide_y = lane_expand(k_scr[0:ny, :], head, False).reshape(ny, 1, HD * HD)
-        wide_z = lane_expand(k_scr[ny:, :], head, True)
         narrow = jnp.zeros((nx * HD, HD * HD), F32)
         for i, source in enumerate((mine_ref, got_ref)):
-            mixer = wide_y * wide_z[i * nz : (i + 1) * nz].reshape(1, nz, HD * HD)
-            mixer = mixer.reshape(ny * nz, HD * HD).astype(BF)
+            mixer = outer_yz(wide_y, wide_z[i * nz : (i + 1) * nz], j)
             narrow = narrow + dot(source[j].reshape(nx * HD, ny * nz), mixer)
         for side in range(2):
             row_scr[j, side] = narrow[:, side * C : (side + 1) * C]
@@ -225,26 +226,26 @@
                 out_ref[j * HD + channel, side] = rows.astype(BF)
 
 
-def second(idx, pooled, w_qkv, mine, got, sizes, steps=2):
+def second(where, pooled, w_qkv, mine, got, sizes, steps=1):
     nx, ny, nz = sizes
     half = HEADS // 2
     heads = half // steps
-    value = pl.BlockSpec((heads, nx, HD, ny * nz), lambda i, s: (i, 0, 0, 0))
+    value = pl.BlockSpec((heads, nx, HD, ny * nz), lambda i, *s: (i, 0, 0, 0))
     return pl.pallas_call(
         functools.partial(second_kernel, sizes=sizes),
         grid_spec=pltpu.PrefetchScalarGridSpec(
-            num_scalar_prefetch=1,
+            num_scalar_prefetch=len(where),
             grid=(steps,),
             in_specs=[
                 pl.BlockSpec(memory_space=pltpu.VMEM),
-                pl.BlockSpec((C, 2 * C), lambda i, s: (0, 0)),
+                pl.BlockSpec((C, 2 * C), lambda i, *s: (0, 0)),
                 value,
                 value,
             ],
             out_specs=[
-                pl.BlockSpec((heads * HD, 2, nx, C), lambda i, s: (i, 0, 0, 0)),
-                pl.BlockSpec((ny + nz, C), lambda i, s: (0, 0)),
-                pl.BlockSpec((C, C), lambda i, s: (0, 0)),
+                pl.BlockSpec((heads * HD, 2, nx, C), lambda i, *s: (i, 0, 0, 0)),
+                pl.BlockSpec((ny + nz, C), lambda i, *s: (0, 0)),
+                pl.BlockSpec((C, C), lambda i, *s: (0, 0)),
             ],
             scratch_shapes=[
                 pltpu.VMEM((ny + 2 * nz, C), F32),
@@ -257,7 +258,7 @@
             jax.ShapeDtypeStruct((C, C), BF),
         ],
         name="second",
-    )(idx, pooled, w_qkv, mine, got)
+    )(*where, pooled, w_qkv, mine, got)
 
 
 def middle_kernel(g_ref, kx_ref, out_ref):
@@ -283,23 +284,27 @@
 
 
 def third_kernel(
-    idx_ref, q_ref, mine_ref, other_ref, tok_ref, wo_ref, wg_ref, wd_ref, out_ref, mix_scr, row_scr
+    core_ref, q_ref, mine_ref, other_ref, tok_ref, wo_ref, wg_ref, wd_ref, out_ref, mix_scr, row_scr
 ):
     step = pl.program_id(0)
     nb, ny, nz, _ = tok_ref.shape
     nx = mix_scr.shape[0]
     half = HEADS // 2
-    gz = idx_ref[2]
+    gz = core_ref[0]
 
     @pl.when(step == 0)
     def _():
         qy = q_ref[0:ny, :]
         qz = q_ref[ny : ny + nz, :]
+        wides = []
+        for head in (gz * half, (1 - gz) * half):
+            wide_y = lane_expand(qy, head, half, False)
+            wides.append((wide_y, lane_expand(qz, head, half, True)))
         for j in range(HEADS):
             source = mine_ref if j < half else other_ref
             head = jnp.where(gz == 0, j, (j + half) % HEADS)
             at = j % half * HD
-            mixer = outer_yz(qy, qz, head)
+            mixer = outer_yz(*wides[j // half], j % half)
             for i in range(2):
                 rows = source[at : at + HD, i].astype(F32).reshape(HD * nx, C)
                 row_scr[j, i] = rows
@@ -330,7 +335,7 @@
     out_ref[...] = result.reshape(nb, ny, nz, C)
 
 
-def third(idx, q, mine, other, tokens, w_out, w_gate_up, w_down, block=2):
+def third(core, q, mine, other, tokens, w_out, w_gate_up, w_down, block=2):
     nx, ny, nz, _ = tokens.shape
     full = lambda a: pl.BlockSpec(a.shape, lambda i, s: (0,) * a.ndim)
     slab = pl.BlockSpec((block, ny, nz, C), lambda i, s: (i, 0, 0, 0))
@@ -357,7 +362,7 @@
         ),
         out_shape=jax.ShapeDtypeStruct(tokens.shape, BF),
         name="third",
-    )(idx, q, mine, other, tokens, w_out, w_gate_up, w_down)
+    )(core, q, mine, other, tokens, w_out, w_gate_up, w_down)
 
 
 def a2a(values, axes):
@@ -367,12 +372,13 @@
 def body(tokens, w_qkv, w_out, w_gate_up, w_down):
     nx, ny, nz, _ = tokens.shape
     cx, cy, cz = (lax.axis_size(a) for a in ("gx", "gy", "gz"))
-    idx = jnp.stack([lax.axis_index(a) for a in ("gx", "gy", "gz")]).astype(jnp.int32)
+    where = [lax.axis_index(a).astype(jnp.int32).reshape(1) for a in ("gx", "gy", "gz")]
     ry = ny // cx
     rz = nz // cx
-    keep, send, pool, sum_x = first(idx, tokens, w_qkv, cx)
+    keep, send, pool, sum_x = first(where[2], tokens, w_qkv, cx)
     got_value = lax.ppermute(send, "gz", [(0, 1), (1, 0)])
     sum_x = sum_x.reshape(nx, C)
+    pool, where = lax.optimization_barrier((pool, where))
     got = jnp.sum(a2a(pool, "gx"), axis=0)
     packed = jnp.concatenate([sum_x, got], axis=0)
     wide = jnp.broadcast_to(packed, (cy * cz,) + packed.shape)
@@ -384,13 +390,13 @@
     packed, got_value = lax.optimization_barrier((packed, got_value))
     pooled = a2a(jnp.broadcast_to(packed, (cx,) + packed.shape), "gx")
 
-    part, q, kx = second(idx, pooled, w_qkv, keep, got_value, (nx, ny, nz))
+    part, q, kx = second(where, pooled, w_qkv, keep, got_value, (nx, ny, nz))
     swap = [(0, 1), (1, 0)]
     gathered = a2a(part.reshape(cx * cy, nx, C), ("gx", "gy")).reshape(cx, cy, nx, C)
     spread = middle(gathered, kx).reshape(cx * cy, nx, C)
     mine = a2a(spread, ("gx", "gy")).reshape(part.shape)
     other = lax.ppermute(mine, "gz", swap)
-    return third(idx, q, mine, other, tokens, w_out, w_gate_up, w_down)
+    return third(where[2], q, mine, other, tokens, w_out, w_gate_up, w_down)
 
 
 def solution(mesh):

time: 120 us -> 116 us (0.967)
  Pallas kernels: 27.5 us -> 24.7 us
    pallas_call x1, Pallas kernels: 15.3 us -> 13.9 us  [third(): pl.pallas_call(third_kernel, grid_spec=pltpu.PrefetchScalarGridSpec(num_s...]
where the time goes in v7:
time: 116 us
  blocking collectives  81.7 us (70%)
  Pallas kernels  24.7 us (21%)
  starting transfers between devices  6.76 us (6%)
  waiting for transfers between devices  1.16 us (1%)
    all_to_all x5, blocking collectives, a2a(): return lax.all_to_all(values, axes, 0, 0, tiled=True)  81.7 us
    pallas_call x1, Pallas kernels, third(): pl.pallas_call(third_kernel, grid_spec=pltpu.PrefetchScalarGridSpec(num_s...  13.9 us
    pallas_call x1, Pallas kernels, first(): pl.pallas_call(first_kernel, grid_spec=pltpu.PrefetchScalarGridSpec(num_s...  4.72 us
    pallas_call x1, Pallas kernels, second(): pl.pallas_call(functools.partial(second_kernel, sizes=sizes), grid_spec=p...  4.2 us
    ppermute x1, starting transfers between devices, body(): other = lax.ppermute(mine, 'gz', swap)  3.49 us
    ppermute x1, starting transfers between devices, body(): got_value = lax.ppermute(send, 'gz', [(0, 1), (1, 0)])  3.27 us
  transfers between devices with their start and end apart: 2, of which 1 were waited for; matrix products, arithmetic and copies ran while one was open for 1% of the time, Pallas kernels for 0%

profile of v7, /device:TPU:1, one launch (start us, length us, event | category | flops | bytes accessed | tf_op | source)
XLA Modules:
  0.0 115.8 jit_solution(3566874670926525983)
XLA Ops:
  0.0 4.7 %first.1 = (bf16[4,8,16,1024]{3,2,1,0:T(8,128)(2,1)}, bf16[4,8,16,1024]{3,2,1,0:T(8,128)(2,1)}, f32[16,8,128]{2,1,0:T(8,128)}, f32[2,4,128]{2,1,0:T(4,128)}) custom-call(s32[1]{0:T(128)} %bitcast.core_ref, bf16[8,16,64,128]{3,2,1,0:T(8,128)(2,1)} %tok_ref.3, bf16[128,384]{1,0:T(8,128)(2,1)} %w_ref.1), custom_call_target="tpu_custom_call" | custom-call | tf_op jit(solution)/shard_map/first/pallas_call | solution.py:106
  4.7 3.3 %collective-permute-start = (bf16[4,8,16,1024]{3,2,1,0:T(8,128)(2,1)}, bf16[4,8,16,1024]{3,2,1,0:T(8,128)(2,1)S(1)}, u32[]{:S(2)}, u32[]{:S(2)}) collective-permute-start(bf16[4,8,16,1024]{3,2,1,0:T(8,128)(2,1)} %get-tuple-element.24), channel_id=1, source_target_pairs={{0,1},{1,0},{2,3},{3,2},{4,5},{5,4},{6,7},{7,6},{8,9},{9,8},{10,11... | collective-permute-start | bytes 3145736 | tf_op jit(solution)/shard_map/ppermute | solution.py:379
  8.0 15.1 %all_to_all.25 = f32[16,8,128]{2,1,0:T(8,128)S(1)} all-to-all(f32[16,8,128]{2,1,0:T(8,128)} %get-tuple-element.23), channel_id=1, replica_groups=mesh['gx'=16,'gy'=8,'gz'=2] {'gx'}, dimensions={0} | all-to-all | bytes 131072 | tf_op jit(solution)/shard_map/all_to_all | solution.py:369
  23.1 0.7 pad_maximum_fusion.1
  23.8 15.4 %all_to_all.26 = f32[16,16,128]{2,1,0:T(8,128)S(1)} all-to-all(f32[16,16,128]{2,1,0:T(8,128)S(1)} %broadcast_in_dim.6), channel_id=1, replica_groups=mesh['gx'=16,'gy'=8,'gz'=2] {'gy','gz'}, dimensions={0} | all-to-all | bytes 262144 | tf_op jit(solution)/shard_map/all_to_all | solution.py:369
  39.2 0.0 collective-permute-done.got_ref
  39.2 0.0 copy-start
  39.2 10.7 %all_to_all.27.r_ref = f32[16,24,128]{2,1,0:T(8,128)} all-to-all(f32[16,24,128]{2,1,0:T(8,128)S(1)} %broadcast_in_dim.7), channel_id=1, replica_groups=mesh['gx'=16,'gy'=8,'gz'=2] {'gx'}, dimensions={0} | all-to-all | bytes 393216 | tf_op jit(solution)/shard_map/all_to_all | solution.py:369
  50.0 0.0 copy-done
  50.0 4.2 %second.1 = (bf16[64,2,8,128]{3,2,1,0:T(8,128)(2,1)}, f32[80,128]{1,0:T(8,128)}, bf16[128,128]{1,0:T(8,128)(2,1)}) custom-call(s32[1]{0:T(128)} %bitcast.1.x_ref, s32[1]{0:T(128)} %bitcast.2.y_ref, s32[1]{0:T(128)} %bitcast.core_ref, f32[16,24,128]{2,1,0:T(8,128)} %all_to_all.27.r_ref, bf16[128,384]{1,0:T(8,128)(2,1)} %w_ref.1, ...), custom_call_target="tpu_custom_call" | custom-call | tf_op jit(solution)/shard_map/second/pallas_call | solution.py:234
  54.2 20.7 %all_to_all.28 = bf16[128,8,128]{2,1,0:T(8,128)(2,1)} all-to-all(bf16[128,8,128]{2,1,0:T(8,128)(2,1)} %bitcast.17), channel_id=1, replica_groups=mesh['gx'=16,'gy'=8,'gz'=2] {'gx','gy'}, dimensions={0} | all-to-all | bytes 524288 | tf_op jit(solution)/shard_map/all_to_all | solution.py:369
  74.9 1.8 %middle.1 = bf16[16,8,8,128]{3,2,1,0:T(8,128)(2,1)} custom-call(bf16[16,8,8,128]{3,2,1,0:T(8,128)(2,1)} %bitcast.10, bf16[128,128]{1,0:T(8,128)(2,1)} %get-tuple-element.30.kx_ref), custom_call_target="tpu_custom_call" | custom-call | tf_op jit(solution)/shard_map/middle/pallas_call | solution.py:277
  76.7 19.8 %all_to_all.29 = bf16[128,8,128]{2,1,0:T(8,128)(2,1)S(1)} all-to-all(bf16[128,8,128]{2,1,0:T(8,128)(2,1)} %bitcast.11), channel_id=1, replica_groups=mesh['gx'=16,'gy'=8,'gz'=2] {'gx','gy'}, dimensions={0} | all-to-all | bytes 524288 | tf_op jit(solution)/shard_map/all_to_all | solution.py:369
  96.6 0.0 copy-start.1
  96.6 3.5 %collective-permute-start.1 = (bf16[64,2,8,128]{3,2,1,0:T(8,128)(2,1)S(1)}, bf16[64,2,8,128]{3,2,1,0:T(8,128)(2,1)S(1)}, u32[]{:S(2)}, u32[]{:S(2)}) collective-permute-start(bf16[64,2,8,128]{3,2,1,0:T(8,128)(2,1)S(1)} %bitcast.12), channel_id=1, source_target_pairs={{0,1},{1,0},{2,3},{3,2},{4,5},{5,4},{6,7},{7,6},{8,9},{9,8},{10,11... | collective-permute-start | bytes 786440 | tf_op jit(solution)/shard_map/ppermute | solution.py:398
  100.0 1.2 %collective-permute-done.1.other_ref = bf16[64,2,8,128]{3,2,1,0:T(8,128)(2,1)S(1)} collective-permute-done((bf16[64,2,8,128]{3,2,1,0:T(8,128)(2,1)S(1)}, bf16[64,2,8,128]{3,2,1,0:T(8,128)(2,1)S(1)}, u32[]{:S(2)}, u32[]{:S(2)}) %collective-permute-start.1) | collective-permute-done | bytes 262176 | tf_op jit(solution)/shard_map/ppermute | solution.py:398
  101.2 0.0 copy-start.2
  101.2 0.0 copy-done.1
  101.2 0.7 copy-done.2
  101.9 13.9 %third.1 = bf16[8,16,64,128]{3,2,1,0:T(8,128)(2,1)} custom-call(s32[1]{0:T(128)} %bitcast.core_ref, f32[80,128]{1,0:T(8,128)} %get-tuple-element.28.q_ref, bf16[64,2,8,128]{3,2,1,0:T(8,128)(2,1)} %bitcast.13, bf16[64,2,8,128]{3,2,1,0:T(8,128)(2,1)} %copy-done.2, bf16[8,16,64,128]{3,2,1,0:T(8,128)(2,1)} %tok_ref.3, bf16[128,128]{1,0:T(8,128)(2,1)} %wo_ref.1, ...), custom_call_target="tpu_custom_call" | custom-call | tf_op jit(solution)/shard_map/third/pallas_call | solution.py:343
  (7 shorter events, 0.1 us)
Async XLA Ops:
  4.7 34.5 %collective-permute-start = (bf16[4,8,16,1024]{3,2,1,0:T(8,128)(2,1)}, bf16[4,8,16,1024]{3,2,1,0:T(8,128)(2,1)S(1)}, u32[]{:S(2)}, u32[]{:S(2)}) collective-permute-start(bf16[4,8,16,1024]{3,2,1,0:T(8,128)(2,1)} %get-tuple-element.24), channel_id=1, source_target_pairs={{0,1},{1,0},{2,3},{3,2},{4,5},{5,4},{6,7},{7,6},{8,9},{9,8},{10,11... | collective-permute-start | bytes 3145736 | tf_op jit(solution)/shard_map/ppermute | solution.py:379
  39.2 10.8 %copy-start = (bf16[4,8,16,1024]{3,2,1,0:T(8,128)(2,1)}, bf16[4,8,16,1024]{3,2,1,0:T(8,128)(2,1)S(1)}, u32[]{:S(2)}) copy-start(bf16[4,8,16,1024]{3,2,1,0:T(8,128)(2,1)S(1)} %collective-permute-done.got_ref) | copy-start | bytes 3145732
  96.6 4.7 %copy-start.1 = (bf16[128,8,128]{2,1,0:T(8,128)(2,1)}, bf16[128,8,128]{2,1,0:T(8,128)(2,1)S(1)}, u32[]{:S(2)}) copy-start(bf16[128,8,128]{2,1,0:T(8,128)(2,1)S(1)} %all_to_all.29) | copy-start | bytes 786436
  96.6 4.7 %collective-permute-start.1 = (bf16[64,2,8,128]{3,2,1,0:T(8,128)(2,1)S(1)}, bf16[64,2,8,128]{3,2,1,0:T(8,128)(2,1)S(1)}, u32[]{:S(2)}, u32[]{:S(2)}) collective-permute-start(bf16[64,2,8,128]{3,2,1,0:T(8,128)(2,1)S(1)} %bitcast.12), channel_id=1, source_target_pairs={{0,1},{1,0},{2,3},{3,2},{4,5},{5,4},{6,7},{7,6},{8,9},{9,8},{10,11... | collective-permute-start | bytes 786440 | tf_op jit(solution)/shard_map/ppermute | solution.py:398
  101.2 0.7 copy-start.2

commit v8 on v7

--- a/solution.py
+++ b/solution.py
@@ -328,9 +328,8 @@
     both = dot(inner, wg_ref[...]).astype(BF)
     gate = both[:, :FF]
     root = math.sqrt(2.0 / math.pi)
-    inside = gate * (BF(root) + BF(root * 0.044715) * (gate * gate))
-    half_gate = gate * BF(0.5)
-    hidden = (half_gate + half_gate * jnp.tanh(inside)) * both[:, FF:]
+    inside = gate * (BF(2 * root) + BF(2 * root * 0.044715) * (gate * gate))
+    hidden = gate * jax.nn.sigmoid(inside) * both[:, FF:]
     result = (resid + dot(hidden, wd_ref[...])).astype(BF)
     out_ref[...] = result.reshape(nb, ny, nz, C)
 

time: 116 us -> 116 us (level)
  no operation moved by 1% of the time
where the time goes in v8:
time: 116 us
  blocking collectives  81.7 us (70%)
  Pallas kernels  24.7 us (21%)
  starting transfers between devices  6.76 us (6%)
  waiting for transfers between devices  1.16 us (1%)
    all_to_all x5, blocking collectives, a2a(): return lax.all_to_all(values, axes, 0, 0, tiled=True)  81.7 us
    pallas_call x1, Pallas kernels, third(): pl.pallas_call(third_kernel, grid_spec=pltpu.PrefetchScalarGridSpec(num_s...  13.9 us
    pallas_call x1, Pallas kernels, first(): pl.pallas_call(first_kernel, grid_spec=pltpu.PrefetchScalarGridSpec(num_s...  4.72 us
    pallas_call x1, Pallas kernels, second(): pl.pallas_call(functools.partial(second_kernel, sizes=sizes), grid_spec=p...  4.2 us
    ppermute x1, starting transfers between devices, body(): other = lax.ppermute(mine, 'gz', swap)  3.49 us
    ppermute x1, starting transfers between devices, body(): got_value = lax.ppermute(send, 'gz', [(0, 1), (1, 0)])  3.27 us
  transfers between devices with their start and end apart: 2, of which 1 were waited for; matrix products, arithmetic and copies ran while one was open for 1% of the time, Pallas kernels for 0%

profile of v8, /device:TPU:1, one launch (start us, length us, event | category | flops | bytes accessed | tf_op | source)
XLA Modules:
  0.0 115.8 jit_solution(16230319020968321684)
XLA Ops:
  0.0 4.7 %first.1 = (bf16[4,8,16,1024]{3,2,1,0:T(8,128)(2,1)}, bf16[4,8,16,1024]{3,2,1,0:T(8,128)(2,1)}, f32[16,8,128]{2,1,0:T(8,128)}, f32[2,4,128]{2,1,0:T(4,128)}) custom-call(s32[1]{0:T(128)} %bitcast.core_ref, bf16[8,16,64,128]{3,2,1,0:T(8,128)(2,1)} %tok_ref.3, bf16[128,384]{1,0:T(8,128)(2,1)} %w_ref.1), custom_call_target="tpu_custom_call" | custom-call | tf_op jit(solution)/shard_map/first/pallas_call | solution.py:106
  4.7 3.3 %collective-permute-start = (bf16[4,8,16,1024]{3,2,1,0:T(8,128)(2,1)}, bf16[4,8,16,1024]{3,2,1,0:T(8,128)(2,1)S(1)}, u32[]{:S(2)}, u32[]{:S(2)}) collective-permute-start(bf16[4,8,16,1024]{3,2,1,0:T(8,128)(2,1)} %get-tuple-element.24), channel_id=1, source_target_pairs={{0,1},{1,0},{2,3},{3,2},{4,5},{5,4},{6,7},{7,6},{8,9},{9,8},{10,11... | collective-permute-start | bytes 3145736 | tf_op jit(solution)/shard_map/ppermute | solution.py:378
  8.0 15.1 %all_to_all.25 = f32[16,8,128]{2,1,0:T(8,128)S(1)} all-to-all(f32[16,8,128]{2,1,0:T(8,128)} %get-tuple-element.23), channel_id=1, replica_groups=mesh['gx'=16,'gy'=8,'gz'=2] {'gx'}, dimensions={0} | all-to-all | bytes 131072 | tf_op jit(solution)/shard_map/all_to_all | solution.py:368
  23.1 0.7 pad_maximum_fusion.1
  23.8 15.4 %all_to_all.26 = f32[16,16,128]{2,1,0:T(8,128)S(1)} all-to-all(f32[16,16,128]{2,1,0:T(8,128)S(1)} %broadcast_in_dim.6), channel_id=1, replica_groups=mesh['gx'=16,'gy'=8,'gz'=2] {'gy','gz'}, dimensions={0} | all-to-all | bytes 262144 | tf_op jit(solution)/shard_map/all_to_all | solution.py:368
  39.2 0.0 collective-permute-done.got_ref
  39.2 0.0 copy-start
  39.2 10.7 %all_to_all.27.r_ref = f32[16,24,128]{2,1,0:T(8,128)} all-to-all(f32[16,24,128]{2,1,0:T(8,128)S(1)} %broadcast_in_dim.7), channel_id=1, replica_groups=mesh['gx'=16,'gy'=8,'gz'=2] {'gx'}, dimensions={0} | all-to-all | bytes 393216 | tf_op jit(solution)/shard_map/all_to_all | solution.py:368
  50.0 0.0 copy-done
  50.0 4.2 %second.1 = (bf16[64,2,8,128]{3,2,1,0:T(8,128)(2,1)}, f32[80,128]{1,0:T(8,128)}, bf16[128,128]{1,0:T(8,128)(2,1)}) custom-call(s32[1]{0:T(128)} %bitcast.1.x_ref, s32[1]{0:T(128)} %bitcast.2.y_ref, s32[1]{0:T(128)} %bitcast.core_ref, f32[16,24,128]{2,1,0:T(8,128)} %all_to_all.27.r_ref, bf16[128,384]{1,0:T(8,128)(2,1)} %w_ref.1, ...), custom_call_target="tpu_custom_call" | custom-call | tf_op jit(solution)/shard_map/second/pallas_call | solution.py:234
  54.2 20.7 %all_to_all.28 = bf16[128,8,128]{2,1,0:T(8,128)(2,1)} all-to-all(bf16[128,8,128]{2,1,0:T(8,128)(2,1)} %bitcast.17), channel_id=1, replica_groups=mesh['gx'=16,'gy'=8,'gz'=2] {'gx','gy'}, dimensions={0} | all-to-all | bytes 524288 | tf_op jit(solution)/shard_map/all_to_all | solution.py:368
  74.9 1.8 %middle.1 = bf16[16,8,8,128]{3,2,1,0:T(8,128)(2,1)} custom-call(bf16[16,8,8,128]{3,2,1,0:T(8,128)(2,1)} %bitcast.10, bf16[128,128]{1,0:T(8,128)(2,1)} %get-tuple-element.30.kx_ref), custom_call_target="tpu_custom_call" | custom-call | tf_op jit(solution)/shard_map/middle/pallas_call | solution.py:277
  76.7 19.8 %all_to_all.29 = bf16[128,8,128]{2,1,0:T(8,128)(2,1)S(1)} all-to-all(bf16[128,8,128]{2,1,0:T(8,128)(2,1)} %bitcast.11), channel_id=1, replica_groups=mesh['gx'=16,'gy'=8,'gz'=2] {'gx','gy'}, dimensions={0} | all-to-all | bytes 524288 | tf_op jit(solution)/shard_map/all_to_all | solution.py:368
  96.6 0.0 copy-start.1
  96.6 3.5 %collective-permute-start.1 = (bf16[64,2,8,128]{3,2,1,0:T(8,128)(2,1)S(1)}, bf16[64,2,8,128]{3,2,1,0:T(8,128)(2,1)S(1)}, u32[]{:S(2)}, u32[]{:S(2)}) collective-permute-start(bf16[64,2,8,128]{3,2,1,0:T(8,128)(2,1)S(1)} %bitcast.12), channel_id=1, source_target_pairs={{0,1},{1,0},{2,3},{3,2},{4,5},{5,4},{6,7},{7,6},{8,9},{9,8},{10,11... | collective-permute-start | bytes 786440 | tf_op jit(solution)/shard_map/ppermute | solution.py:397
  100.0 1.2 %collective-permute-done.1.other_ref = bf16[64,2,8,128]{3,2,1,0:T(8,128)(2,1)S(1)} collective-permute-done((bf16[64,2,8,128]{3,2,1,0:T(8,128)(2,1)S(1)}, bf16[64,2,8,128]{3,2,1,0:T(8,128)(2,1)S(1)}, u32[]{:S(2)}, u32[]{:S(2)}) %collective-permute-start.1) | collective-permute-done | bytes 262176 | tf_op jit(solution)/shard_map/ppermute | solution.py:397
  101.2 0.0 copy-start.2
  101.2 0.0 copy-done.1
  101.2 0.7 copy-done.2
  101.9 13.9 %third.1 = bf16[8,16,64,128]{3,2,1,0:T(8,128)(2,1)} custom-call(s32[1]{0:T(128)} %bitcast.core_ref, f32[80,128]{1,0:T(8,128)} %get-tuple-element.28.q_ref, bf16[64,2,8,128]{3,2,1,0:T(8,128)(2,1)} %bitcast.13, bf16[64,2,8,128]{3,2,1,0:T(8,128)(2,1)} %copy-done.2, bf16[8,16,64,128]{3,2,1,0:T(8,128)(2,1)} %tok_ref.3, bf16[128,128]{1,0:T(8,128)(2,1)} %wo_ref.1, ...), custom_call_target="tpu_custom_call" | custom-call | tf_op jit(solution)/shard_map/third/pallas_call | solution.py:342
  (7 shorter events, 0.1 us)
Async XLA Ops:
  4.7 34.5 %collective-permute-start = (bf16[4,8,16,1024]{3,2,1,0:T(8,128)(2,1)}, bf16[4,8,16,1024]{3,2,1,0:T(8,128)(2,1)S(1)}, u32[]{:S(2)}, u32[]{:S(2)}) collective-permute-start(bf16[4,8,16,1024]{3,2,1,0:T(8,128)(2,1)} %get-tuple-element.24), channel_id=1, source_target_pairs={{0,1},{1,0},{2,3},{3,2},{4,5},{5,4},{6,7},{7,6},{8,9},{9,8},{10,11... | collective-permute-start | bytes 3145736 | tf_op jit(solution)/shard_map/ppermute | solution.py:378
  39.2 10.8 %copy-start = (bf16[4,8,16,1024]{3,2,1,0:T(8,128)(2,1)}, bf16[4,8,16,1024]{3,2,1,0:T(8,128)(2,1)S(1)}, u32[]{:S(2)}) copy-start(bf16[4,8,16,1024]{3,2,1,0:T(8,128)(2,1)S(1)} %collective-permute-done.got_ref) | copy-start | bytes 3145732
  96.6 4.7 %copy-start.1 = (bf16[128,8,128]{2,1,0:T(8,128)(2,1)}, bf16[128,8,128]{2,1,0:T(8,128)(2,1)S(1)}, u32[]{:S(2)}) copy-start(bf16[128,8,128]{2,1,0:T(8,128)(2,1)S(1)} %all_to_all.29) | copy-start | bytes 786436
  96.6 4.7 %collective-permute-start.1 = (bf16[64,2,8,128]{3,2,1,0:T(8,128)(2,1)S(1)}, bf16[64,2,8,128]{3,2,1,0:T(8,128)(2,1)S(1)}, u32[]{:S(2)}, u32[]{:S(2)}) collective-permute-start(bf16[64,2,8,128]{3,2,1,0:T(8,128)(2,1)S(1)} %bitcast.12), channel_id=1, source_target_pairs={{0,1},{1,0},{2,3},{3,2},{4,5},{5,4},{6,7},{7,6},{8,9},{9,8},{10,11... | collective-permute-start | bytes 786440 | tf_op jit(solution)/shard_map/ppermute | solution.py:397
  101.2 0.7 copy-start.2

commit v9 on v7

--- a/solution.py
+++ b/solution.py
@@ -138,11 +138,15 @@
     return dot(halves(rows), twice(ones_where(iota2(shape, 0) == channel)))
 
 
-def outer_yz(wide_y, wide_z, at):
+def outer_yz(wide_y, wide_z, at, narrow=False):
     ny, nz = wide_y.shape[0], wide_z.shape[0]
     cut = slice(at * HD * HD, (at + 1) * HD * HD)
-    both = wide_y[:, cut].reshape(ny, 1, HD * HD) * wide_z[:, cut].reshape(1, nz, HD * HD)
-    return both.reshape(ny * nz, HD * HD).astype(BF)
+    wide_y = wide_y[:, cut].reshape(ny, 1, HD * HD)
+    wide_z = wide_z[:, cut].reshape(1, nz, HD * HD)
+    if narrow:
+        wide_y = jnp.broadcast_to(wide_y.astype(BF), (ny, nz, HD * HD))
+        wide_z = wide_z.astype(BF)
+    return (wide_y * wide_z).reshape(ny * nz, HD * HD).astype(BF)
 
 
 def second_kernel(
@@ -217,7 +221,7 @@
     for j in range(heads):
         narrow = jnp.zeros((nx * HD, HD * HD), F32)
         for i, source in enumerate((mine_ref, got_ref)):
-            mixer = outer_yz(wide_y, wide_z[i * nz : (i + 1) * nz], j)
+            mixer = outer_yz(wide_y, wide_z[i * nz : (i + 1) * nz], j, narrow=True)
             narrow = narrow + dot(source[j].reshape(nx * HD, ny * nz), mixer)
         for side in range(2):
             row_scr[j, side] = narrow[:, side * C : (side + 1) * C]

time: 116 us -> 116 us (level)
  no operation moved by 1% of the time
where the time goes in v9:
time: 116 us
  blocking collectives  81.7 us (70%)
  Pallas kernels  24.4 us (21%)
  starting transfers between devices  6.76 us (6%)
  waiting for transfers between devices  1.16 us (1%)
    all_to_all x5, blocking collectives, a2a(): return lax.all_to_all(values, axes, 0, 0, tiled=True)  81.7 us
    pallas_call x1, Pallas kernels, third(): pl.pallas_call(third_kernel, grid_spec=pltpu.PrefetchScalarGridSpec(num_s...  13.9 us
    pallas_call x1, Pallas kernels, first(): pl.pallas_call(first_kernel, grid_spec=pltpu.PrefetchScalarGridSpec(num_s...  4.72 us
    pallas_call x1, Pallas kernels, second(): pl.pallas_call(functools.partial(second_kernel, sizes=sizes), grid_spec=p...  3.98 us
    ppermute x1, starting transfers between devices, body(): other = lax.ppermute(mine, 'gz', swap)  3.49 us
    ppermute x1, starting transfers between devices, body(): got_value = lax.ppermute(send, 'gz', [(0, 1), (1, 0)])  3.27 us
  transfers between devices with their start and end apart: 2, of which 1 were waited for; matrix products, arithmetic and copies ran while one was open for 1% of the time, Pallas kernels for 0%

profile of v9, /device:TPU:1, one launch (start us, length us, event | category | flops | bytes accessed | tf_op | source)
XLA Modules:
  0.0 115.6 jit_solution(10408366163297213899)
XLA Ops:
  0.0 4.7 %first.1 = (bf16[4,8,16,1024]{3,2,1,0:T(8,128)(2,1)}, bf16[4,8,16,1024]{3,2,1,0:T(8,128)(2,1)}, f32[16,8,128]{2,1,0:T(8,128)}, f32[2,4,128]{2,1,0:T(4,128)}) custom-call(s32[1]{0:T(128)} %bitcast.core_ref, bf16[8,16,64,128]{3,2,1,0:T(8,128)(2,1)} %tok_ref.3, bf16[128,384]{1,0:T(8,128)(2,1)} %w_ref.1), custom_call_target="tpu_custom_call" | custom-call | tf_op jit(solution)/shard_map/first/pallas_call | solution.py:106
  4.7 3.3 %collective-permute-start = (bf16[4,8,16,1024]{3,2,1,0:T(8,128)(2,1)}, bf16[4,8,16,1024]{3,2,1,0:T(8,128)(2,1)S(1)}, u32[]{:S(2)}, u32[]{:S(2)}) collective-permute-start(bf16[4,8,16,1024]{3,2,1,0:T(8,128)(2,1)} %get-tuple-element.24), channel_id=1, source_target_pairs={{0,1},{1,0},{2,3},{3,2},{4,5},{5,4},{6,7},{7,6},{8,9},{9,8},{10,11... | collective-permute-start | bytes 3145736 | tf_op jit(solution)/shard_map/ppermute | solution.py:383
  8.0 15.1 %all_to_all.25 = f32[16,8,128]{2,1,0:T(8,128)S(1)} all-to-all(f32[16,8,128]{2,1,0:T(8,128)} %get-tuple-element.23), channel_id=1, replica_groups=mesh['gx'=16,'gy'=8,'gz'=2] {'gx'}, dimensions={0} | all-to-all | bytes 131072 | tf_op jit(solution)/shard_map/all_to_all | solution.py:373
  23.1 0.7 pad_maximum_fusion.1
  23.8 15.4 %all_to_all.26 = f32[16,16,128]{2,1,0:T(8,128)S(1)} all-to-all(f32[16,16,128]{2,1,0:T(8,128)S(1)} %broadcast_in_dim.6), channel_id=1, replica_groups=mesh['gx'=16,'gy'=8,'gz'=2] {'gy','gz'}, dimensions={0} | all-to-all | bytes 262144 | tf_op jit(solution)/shard_map/all_to_all | solution.py:373
  39.2 0.0 collective-permute-done.got_ref
  39.2 0.0 copy-start
  39.2 10.7 %all_to_all.27.r_ref = f32[16,24,128]{2,1,0:T(8,128)} all-to-all(f32[16,24,128]{2,1,0:T(8,128)S(1)} %broadcast_in_dim.7), channel_id=1, replica_groups=mesh['gx'=16,'gy'=8,'gz'=2] {'gx'}, dimensions={0} | all-to-all | bytes 393216 | tf_op jit(solution)/shard_map/all_to_all | solution.py:373
  50.0 0.0 copy-done
  50.0 4.0 %second.1 = (bf16[64,2,8,128]{3,2,1,0:T(8,128)(2,1)}, f32[80,128]{1,0:T(8,128)}, bf16[128,128]{1,0:T(8,128)(2,1)}) custom-call(s32[1]{0:T(128)} %bitcast.1.x_ref, s32[1]{0:T(128)} %bitcast.2.y_ref, s32[1]{0:T(128)} %bitcast.core_ref, f32[16,24,128]{2,1,0:T(8,128)} %all_to_all.27.r_ref, bf16[128,384]{1,0:T(8,128)(2,1)} %w_ref.1, ...), custom_call_target="tpu_custom_call" | custom-call | tf_op jit(solution)/shard_map/second/pallas_call | solution.py:238
  54.0 20.7 %all_to_all.28 = bf16[128,8,128]{2,1,0:T(8,128)(2,1)} all-to-all(bf16[128,8,128]{2,1,0:T(8,128)(2,1)} %bitcast.17), channel_id=1, replica_groups=mesh['gx'=16,'gy'=8,'gz'=2] {'gx','gy'}, dimensions={0} | all-to-all | bytes 524288 | tf_op jit(solution)/shard_map/all_to_all | solution.py:373
  74.7 1.8 %middle.1 = bf16[16,8,8,128]{3,2,1,0:T(8,128)(2,1)} custom-call(bf16[16,8,8,128]{3,2,1,0:T(8,128)(2,1)} %bitcast.10, bf16[128,128]{1,0:T(8,128)(2,1)} %get-tuple-element.30.kx_ref), custom_call_target="tpu_custom_call" | custom-call | tf_op jit(solution)/shard_map/middle/pallas_call | solution.py:281
  76.5 19.8 %all_to_all.29 = bf16[128,8,128]{2,1,0:T(8,128)(2,1)S(1)} all-to-all(bf16[128,8,128]{2,1,0:T(8,128)(2,1)} %bitcast.11), channel_id=1, replica_groups=mesh['gx'=16,'gy'=8,'gz'=2] {'gx','gy'}, dimensions={0} | all-to-all | bytes 524288 | tf_op jit(solution)/shard_map/all_to_all | solution.py:373
  96.3 0.0 copy-start.1
  96.3 3.5 %collective-permute-start.1 = (bf16[64,2,8,128]{3,2,1,0:T(8,128)(2,1)S(1)}, bf16[64,2,8,128]{3,2,1,0:T(8,128)(2,1)S(1)}, u32[]{:S(2)}, u32[]{:S(2)}) collective-permute-start(bf16[64,2,8,128]{3,2,1,0:T(8,128)(2,1)S(1)} %bitcast.12), channel_id=1, source_target_pairs={{0,1},{1,0},{2,3},{3,2},{4,5},{5,4},{6,7},{7,6},{8,9},{9,8},{10,11... | collective-permute-start | bytes 786440 | tf_op jit(solution)/shard_map/ppermute | solution.py:402
  99.8 1.2 %collective-permute-done.1.other_ref = bf16[64,2,8,128]{3,2,1,0:T(8,128)(2,1)S(1)} collective-permute-done((bf16[64,2,8,128]{3,2,1,0:T(8,128)(2,1)S(1)}, bf16[64,2,8,128]{3,2,1,0:T(8,128)(2,1)S(1)}, u32[]{:S(2)}, u32[]{:S(2)}) %collective-permute-start.1) | collective-permute-done | bytes 262176 | tf_op jit(solution)/shard_map/ppermute | solution.py:402
  101.0 0.0 copy-start.2
  101.0 0.0 copy-done.1
  101.0 0.7 copy-done.2
  101.7 13.9 %third.1 = bf16[8,16,64,128]{3,2,1,0:T(8,128)(2,1)} custom-call(s32[1]{0:T(128)} %bitcast.core_ref, f32[80,128]{1,0:T(8,128)} %get-tuple-element.28.q_ref, bf16[64,2,8,128]{3,2,1,0:T(8,128)(2,1)} %bitcast.13, bf16[64,2,8,128]{3,2,1,0:T(8,128)(2,1)} %copy-done.2, bf16[8,16,64,128]{3,2,1,0:T(8,128)(2,1)} %tok_ref.3, bf16[128,128]{1,0:T(8,128)(2,1)} %wo_ref.1, ...), custom_call_target="tpu_custom_call" | custom-call | tf_op jit(solution)/shard_map/third/pallas_call | solution.py:347
  (7 shorter events, 0.1 us)
Async XLA Ops:
  4.7 34.5 %collective-permute-start = (bf16[4,8,16,1024]{3,2,1,0:T(8,128)(2,1)}, bf16[4,8,16,1024]{3,2,1,0:T(8,128)(2,1)S(1)}, u32[]{:S(2)}, u32[]{:S(2)}) collective-permute-start(bf16[4,8,16,1024]{3,2,1,0:T(8,128)(2,1)} %get-tuple-element.24), channel_id=1, source_target_pairs={{0,1},{1,0},{2,3},{3,2},{4,5},{5,4},{6,7},{7,6},{8,9},{9,8},{10,11... | collective-permute-start | bytes 3145736 | tf_op jit(solution)/shard_map/ppermute | solution.py:383
  39.2 10.8 %copy-start = (bf16[4,8,16,1024]{3,2,1,0:T(8,128)(2,1)}, bf16[4,8,16,1024]{3,2,1,0:T(8,128)(2,1)S(1)}, u32[]{:S(2)}) copy-start(bf16[4,8,16,1024]{3,2,1,0:T(8,128)(2,1)S(1)} %collective-permute-done.got_ref) | copy-start | bytes 3145732
  96.3 4.7 %copy-start.1 = (bf16[128,8,128]{2,1,0:T(8,128)(2,1)}, bf16[128,8,128]{2,1,0:T(8,128)(2,1)S(1)}, u32[]{:S(2)}) copy-start(bf16[128,8,128]{2,1,0:T(8,128)(2,1)S(1)} %all_to_all.29) | copy-start | bytes 786436
  96.3 4.7 %collective-permute-start.1 = (bf16[64,2,8,128]{3,2,1,0:T(8,128)(2,1)S(1)}, bf16[64,2,8,128]{3,2,1,0:T(8,128)(2,1)S(1)}, u32[]{:S(2)}, u32[]{:S(2)}) collective-permute-start(bf16[64,2,8,128]{3,2,1,0:T(8,128)(2,1)S(1)} %bitcast.12), channel_id=1, source_target_pairs={{0,1},{1,0},{2,3},{3,2},{4,5},{5,4},{6,7},{7,6},{8,9},{9,8},{10,11... | collective-permute-start | bytes 786440 | tf_op jit(solution)/shard_map/ppermute | solution.py:402
  101.0 0.7 copy-start.2

commit v10 on v7

--- a/solution.py
+++ b/solution.py
@@ -329,9 +329,8 @@
     gate = both[:, :FF]
     root = math.sqrt(2.0 / math.pi)
     inside = gate * (BF(root) + BF(root * 0.044715) * (gate * gate))
-    half_gate = gate * BF(0.5)
-    hidden = (half_gate + half_gate * jnp.tanh(inside)) * both[:, FF:]
-    result = (resid + dot(hidden, wd_ref[...])).astype(BF)
+    hidden = (gate + gate * jnp.tanh(inside)) * both[:, FF:]
+    result = (resid + dot(hidden, wd_ref[...] * BF(0.5))).astype(BF)
     out_ref[...] = result.reshape(nb, ny, nz, C)
 
 

time: 116 us -> 116 us (level)
  no operation moved by 1% of the time
where the time goes in v10:
time: 116 us
  blocking collectives  81.7 us (70%)
  Pallas kernels  24.7 us (21%)
  starting transfers between devices  6.76 us (6%)
  waiting for transfers between devices  1.16 us (1%)
    all_to_all x5, blocking collectives, a2a(): return lax.all_to_all(values, axes, 0, 0, tiled=True)  81.7 us
    pallas_call x1, Pallas kernels, third(): pl.pallas_call(third_kernel, grid_spec=pltpu.PrefetchScalarGridSpec(num_s...  13.9 us
    pallas_call x1, Pallas kernels, first(): pl.pallas_call(first_kernel, grid_spec=pltpu.PrefetchScalarGridSpec(num_s...  4.72 us
    pallas_call x1, Pallas kernels, second(): pl.pallas_call(functools.partial(second_kernel, sizes=sizes), grid_spec=p...  4.2 us
    ppermute x1, starting transfers between devices, body(): other = lax.ppermute(mine, 'gz', swap)  3.49 us
    ppermute x1, starting transfers between devices, body(): got_value = lax.ppermute(send, 'gz', [(0, 1), (1, 0)])  3.27 us
  transfers between devices with their start and end apart: 2, of which 1 were waited for; matrix products, arithmetic and copies ran while one was open for 1% of the time, Pallas kernels for 0%

profile of v10, /device:TPU:1, one launch (start us, length us, event | category | flops | bytes accessed | tf_op | source)
XLA Modules:
  0.0 115.8 jit_solution(12046237801097350787)
XLA Ops:
  0.0 4.7 %first.1 = (bf16[4,8,16,1024]{3,2,1,0:T(8,128)(2,1)}, bf16[4,8,16,1024]{3,2,1,0:T(8,128)(2,1)}, f32[16,8,128]{2,1,0:T(8,128)}, f32[2,4,128]{2,1,0:T(4,128)}) custom-call(s32[1]{0:T(128)} %bitcast.core_ref, bf16[8,16,64,128]{3,2,1,0:T(8,128)(2,1)} %tok_ref.3, bf16[128,384]{1,0:T(8,128)(2,1)} %w_ref.1), custom_call_target="tpu_custom_call" | custom-call | tf_op jit(solution)/shard_map/first/pallas_call | solution.py:106
  4.7 3.3 %collective-permute-start = (bf16[4,8,16,1024]{3,2,1,0:T(8,128)(2,1)}, bf16[4,8,16,1024]{3,2,1,0:T(8,128)(2,1)S(1)}, u32[]{:S(2)}, u32[]{:S(2)}) collective-permute-start(bf16[4,8,16,1024]{3,2,1,0:T(8,128)(2,1)} %get-tuple-element.24), channel_id=1, source_target_pairs={{0,1},{1,0},{2,3},{3,2},{4,5},{5,4},{6,7},{7,6},{8,9},{9,8},{10,11... | collective-permute-start | bytes 3145736 | tf_op jit(solution)/shard_map/ppermute | solution.py:378
  8.0 15.1 %all_to_all.25 = f32[16,8,128]{2,1,0:T(8,128)S(1)} all-to-all(f32[16,8,128]{2,1,0:T(8,128)} %get-tuple-element.23), channel_id=1, replica_groups=mesh['gx'=16,'gy'=8,'gz'=2] {'gx'}, dimensions={0} | all-to-all | bytes 131072 | tf_op jit(solution)/shard_map/all_to_all | solution.py:368
  23.1 0.7 pad_maximum_fusion.1
  23.8 15.4 %all_to_all.26 = f32[16,16,128]{2,1,0:T(8,128)S(1)} all-to-all(f32[16,16,128]{2,1,0:T(8,128)S(1)} %broadcast_in_dim.6), channel_id=1, replica_groups=mesh['gx'=16,'gy'=8,'gz'=2] {'gy','gz'}, dimensions={0} | all-to-all | bytes 262144 | tf_op jit(solution)/shard_map/all_to_all | solution.py:368
  39.2 0.0 collective-permute-done.got_ref
  39.2 0.0 copy-start
  39.2 10.7 %all_to_all.27.r_ref = f32[16,24,128]{2,1,0:T(8,128)} all-to-all(f32[16,24,128]{2,1,0:T(8,128)S(1)} %broadcast_in_dim.7), channel_id=1, replica_groups=mesh['gx'=16,'gy'=8,'gz'=2] {'gx'}, dimensions={0} | all-to-all | bytes 393216 | tf_op jit(solution)/shard_map/all_to_all | solution.py:368
  50.0 0.0 copy-done
  50.0 4.2 %second.1 = (bf16[64,2,8,128]{3,2,1,0:T(8,128)(2,1)}, f32[80,128]{1,0:T(8,128)}, bf16[128,128]{1,0:T(8,128)(2,1)}) custom-call(s32[1]{0:T(128)} %bitcast.1.x_ref, s32[1]{0:T(128)} %bitcast.2.y_ref, s32[1]{0:T(128)} %bitcast.core_ref, f32[16,24,128]{2,1,0:T(8,128)} %all_to_all.27.r_ref, bf16[128,384]{1,0:T(8,128)(2,1)} %w_ref.1, ...), custom_call_target="tpu_custom_call" | custom-call | tf_op jit(solution)/shard_map/second/pallas_call | solution.py:234
  54.2 20.7 %all_to_all.28 = bf16[128,8,128]{2,1,0:T(8,128)(2,1)} all-to-all(bf16[128,8,128]{2,1,0:T(8,128)(2,1)} %bitcast.17), channel_id=1, replica_groups=mesh['gx'=16,'gy'=8,'gz'=2] {'gx','gy'}, dimensions={0} | all-to-all | bytes 524288 | tf_op jit(solution)/shard_map/all_to_all | solution.py:368
  74.9 1.8 %middle.1 = bf16[16,8,8,128]{3,2,1,0:T(8,128)(2,1)} custom-call(bf16[16,8,8,128]{3,2,1,0:T(8,128)(2,1)} %bitcast.10, bf16[128,128]{1,0:T(8,128)(2,1)} %get-tuple-element.30.kx_ref), custom_call_target="tpu_custom_call" | custom-call | tf_op jit(solution)/shard_map/middle/pallas_call | solution.py:277
  76.7 19.8 %all_to_all.29 = bf16[128,8,128]{2,1,0:T(8,128)(2,1)S(1)} all-to-all(bf16[128,8,128]{2,1,0:T(8,128)(2,1)} %bitcast.11), channel_id=1, replica_groups=mesh['gx'=16,'gy'=8,'gz'=2] {'gx','gy'}, dimensions={0} | all-to-all | bytes 524288 | tf_op jit(solution)/shard_map/all_to_all | solution.py:368
  96.6 0.0 copy-start.1
  96.6 3.5 %collective-permute-start.1 = (bf16[64,2,8,128]{3,2,1,0:T(8,128)(2,1)S(1)}, bf16[64,2,8,128]{3,2,1,0:T(8,128)(2,1)S(1)}, u32[]{:S(2)}, u32[]{:S(2)}) collective-permute-start(bf16[64,2,8,128]{3,2,1,0:T(8,128)(2,1)S(1)} %bitcast.12), channel_id=1, source_target_pairs={{0,1},{1,0},{2,3},{3,2},{4,5},{5,4},{6,7},{7,6},{8,9},{9,8},{10,11... | collective-permute-start | bytes 786440 | tf_op jit(solution)/shard_map/ppermute | solution.py:397
  100.0 1.2 %collective-permute-done.1.other_ref = bf16[64,2,8,128]{3,2,1,0:T(8,128)(2,1)S(1)} collective-permute-done((bf16[64,2,8,128]{3,2,1,0:T(8,128)(2,1)S(1)}, bf16[64,2,8,128]{3,2,1,0:T(8,128)(2,1)S(1)}, u32[]{:S(2)}, u32[]{:S(2)}) %collective-permute-start.1) | collective-permute-done | bytes 262176 | tf_op jit(solution)/shard_map/ppermute | solution.py:397
  101.2 0.0 copy-start.2
  101.2 0.0 copy-done.1
  101.2 0.7 copy-done.2
  101.9 13.9 %third.1 = bf16[8,16,64,128]{3,2,1,0:T(8,128)(2,1)} custom-call(s32[1]{0:T(128)} %bitcast.core_ref, f32[80,128]{1,0:T(8,128)} %get-tuple-element.28.q_ref, bf16[64,2,8,128]{3,2,1,0:T(8,128)(2,1)} %bitcast.13, bf16[64,2,8,128]{3,2,1,0:T(8,128)(2,1)} %copy-done.2, bf16[8,16,64,128]{3,2,1,0:T(8,128)(2,1)} %tok_ref.3, bf16[128,128]{1,0:T(8,128)(2,1)} %wo_ref.1, ...), custom_call_target="tpu_custom_call" | custom-call | tf_op jit(solution)/shard_map/third/pallas_call | solution.py:342
  (7 shorter events, 0.1 us)
Async XLA Ops:
  4.7 34.5 %collective-permute-start = (bf16[4,8,16,1024]{3,2,1,0:T(8,128)(2,1)}, bf16[4,8,16,1024]{3,2,1,0:T(8,128)(2,1)S(1)}, u32[]{:S(2)}, u32[]{:S(2)}) collective-permute-start(bf16[4,8,16,1024]{3,2,1,0:T(8,128)(2,1)} %get-tuple-element.24), channel_id=1, source_target_pairs={{0,1},{1,0},{2,3},{3,2},{4,5},{5,4},{6,7},{7,6},{8,9},{9,8},{10,11... | collective-permute-start | bytes 3145736 | tf_op jit(solution)/shard_map/ppermute | solution.py:378
  39.2 10.8 %copy-start = (bf16[4,8,16,1024]{3,2,1,0:T(8,128)(2,1)}, bf16[4,8,16,1024]{3,2,1,0:T(8,128)(2,1)S(1)}, u32[]{:S(2)}) copy-start(bf16[4,8,16,1024]{3,2,1,0:T(8,128)(2,1)S(1)} %collective-permute-done.got_ref) | copy-start | bytes 3145732
  96.6 4.7 %copy-start.1 = (bf16[128,8,128]{2,1,0:T(8,128)(2,1)}, bf16[128,8,128]{2,1,0:T(8,128)(2,1)S(1)}, u32[]{:S(2)}) copy-start(bf16[128,8,128]{2,1,0:T(8,128)(2,1)S(1)} %all_to_all.29) | copy-start | bytes 786436
  96.6 4.7 %collective-permute-start.1 = (bf16[64,2,8,128]{3,2,1,0:T(8,128)(2,1)S(1)}, bf16[64,2,8,128]{3,2,1,0:T(8,128)(2,1)S(1)}, u32[]{:S(2)}, u32[]{:S(2)}) collective-permute-start(bf16[64,2,8,128]{3,2,1,0:T(8,128)(2,1)S(1)} %bitcast.12), channel_id=1, source_target_pairs={{0,1},{1,0},{2,3},{3,2},{4,5},{5,4},{6,7},{7,6},{8,9},{9,8},{10,11... | collective-permute-start | bytes 786440 | tf_op jit(solution)/shard_map/ppermute | solution.py:397
  101.2 0.7 copy-start.2
